TPU v7x, 32 devices: a whole 2x2x4 slice. The times are simulated.
32 devices in a mesh: dp: 8 (over z, y), tensor: 4 (over x, core).
Axes of the slice: x: 2, y: 2, z: 4, core: 2. Of those that a mesh axis runs over, the one named last changes fastest.
Arguments:
- tokens: bfloat16 [8192, 1024], P('dp', 'tensor'), may hold values from -6 to 6
- dealing: int32 [8192], P('dp'), may hold values from 0 to 8191, as said below
- seq_ids: int32 [8192], P('dp'), may hold values from 0 to 8191, as said below
- first_values: bfloat16 [8192, 1024], P('dp', 'tensor'), may hold values from -6 to 6
- out_grad: bfloat16 [8192, 1024], P('dp', 'tensor'), may hold values from -6 to 6
- norm1_gain: bfloat16 [1024], replicated, may hold values from 0.5 to 1.5
- norm2_gain: bfloat16 [1024], replicated, may hold values from 0.5 to 1.5
- w_query: bfloat16 [1024, 1024], P(None, 'tensor'), may hold values from -0.1875 to 0.1875
- w_key: bfloat16 [1024, 1024], P(None, 'tensor'), may hold values from -0.1875 to 0.1875
- w_value: bfloat16 [1024, 1024], P(None, 'tensor'), may hold values from -0.1875 to 0.1875
- w_out: bfloat16 [1024, 1024], P('tensor'), may hold values from -1 to 1
- w_gate: bfloat16 [1024, 2816], P(None, 'tensor'), may hold values from -0.1875 to 0.1875
- w_up: bfloat16 [1024, 2816], P(None, 'tensor'), may hold values from -0.1875 to 0.1875
- w_down: bfloat16 [2816, 1024], P('tensor'), may hold values from -0.109375 to 0.109375
Outputs:
- output: bfloat16 [8192, 1024], P('dp', 'tensor')
- input_grad: bfloat16 [8192, 1024], P('dp', 'tensor')
- first_values_grad: bfloat16 [8192, 1024], P('dp', 'tensor')
- norm1_gain_grad: float32 [4, 256], P('tensor', 'dp')
- norm2_gain_grad: float32 [4, 256], P('tensor', 'dp')
- w_query_grad: float32 [1024, 1024], P('dp', 'tensor')
- w_key_grad: float32 [1024, 1024], P('dp', 'tensor')
- w_value_grad: float32 [1024, 1024], P('dp', 'tensor')
- w_out_grad: float32 [1024, 1024], P('tensor', 'dp')
- w_gate_grad: float32 [1024, 2816], P('dp', 'tensor')
- w_up_grad: float32 [1024, 2816], P('dp', 'tensor')
- w_down_grad: float32 [2816, 1024], P('tensor', 'dp')
Inputs may be any that keep to these rules, and one draw needn't show every extreme that they name: `dealing`: a permutation; the tokens of each dp index go evenly, 1024 / 8 of them, to the rows of each dp index's block of 1024 dealt rows. `seq_ids`: never fall; no sequence crosses a multiple of 1024 rows; in every draw some block of 1024 rows is a single sequence; the rows of block b carry ids from b * 1024 to b * 1024 + 1023.
All inputs are finite; a program needn't handle non-finite values.
Results may differ from a plain program's by a relative error of at most 0.013.
Values may be sent and summed in bfloat16 or wider, within the bound.
No kernel may reach another device: no remote copies, remote signals or barrier semaphores. Data moves between devices by JAX's collectives and lax.ppermute only.
A program may use at most 128 MiB of HBM per device.

v0:
```python
import jax
import jax.numpy as jnp
from jax import lax
from jax.sharding import PartitionSpec as P

HEAD_DIM = 64


EPS = 1e-06
THETA = 10000.0
NEG = -1e30


def rope_tables(seq_row, head_dim):
    count = seq_row.shape[0]
    places = jnp.arange(count, dtype=jnp.int32)
    change = jnp.concatenate([jnp.ones((1,), bool), seq_row[1:] != seq_row[:-1]])
    starts = lax.cummax(jnp.where(change, places, jnp.zeros_like(places)), axis=0)
    offset = (places - starts).astype(jnp.float32)
    half = head_dim // 2
    freqs = THETA ** (-jnp.arange(half, dtype=jnp.float32) / half)
    angles = offset[:, None] * freqs[None, :]
    return (jnp.cos(angles), jnp.sin(angles))


def rotate(values, cos_rows, sin_rows):
    count = values.shape[0]
    half = cos_rows.shape[1]
    parts = values.reshape(count, -1, 2, half)
    first = parts[:, :, 0]
    second = parts[:, :, 1]
    cos_b = cos_rows[:, None, :]
    sin_b = sin_rows[:, None, :]
    return jnp.stack(
        [first * cos_b - second * sin_b, second * cos_b + first * sin_b], axis=2
    ).reshape(count, -1)


def rotate_back(grads, cos_rows, sin_rows):
    count = grads.shape[0]
    half = cos_rows.shape[1]
    parts = grads.reshape(count, -1, 2, half)
    first = parts[:, :, 0]
    second = parts[:, :, 1]
    cos_b = cos_rows[:, None, :]
    sin_b = sin_rows[:, None, :]
    return jnp.stack(
        [first * cos_b + second * sin_b, second * cos_b - first * sin_b], axis=2
    ).reshape(count, -1)


def row_total(values):
    return lax.psum(values, "tensor")


def gather_normed(normed):
    return lax.all_gather(normed, "tensor", axis=1, tiled=True)


def branch_sum(term):
    return lax.psum_scatter(term, "tensor", scatter_dimension=1, tiled=True)


def gather_grad(grads):
    return lax.all_gather(grads, "tensor", axis=1, tiled=True)


def input_sum(term):
    return lax.psum_scatter(term, "tensor", scatter_dimension=1, tiled=True)


def norm_forward(resid, gain):
    width = resid.shape[1] * lax.axis_size("tensor")
    total = row_total(jnp.sum(resid * resid, axis=1))
    scale = lax.rsqrt(total / width + EPS)[:, None]
    normed = (resid * scale * gain).astype(jnp.bfloat16)
    return (gather_normed(normed), scale)


def norm_backward(dnormed, resid, scale, gain):
    width = resid.shape[1] * lax.axis_size("tensor")
    weighted = dnormed * gain
    dot_row = row_total(jnp.sum(weighted * resid, axis=1))[:, None]
    dresid = scale * weighted - resid * (scale * scale * scale) * dot_row / width
    dgain = jnp.sum(dnormed * resid * scale, axis=0)
    return (dresid, dgain)


def block_mask(seq_block, seq_row, start):
    block = seq_block.shape[0]
    count = seq_row.shape[0]
    rows = start + jnp.arange(block, dtype=jnp.int32)
    cols = jnp.arange(count, dtype=jnp.int32)
    return (seq_block[:, None] == seq_row[None, :]) & (cols[None, :] <= rows[:, None])


def attend(queries, keys, values, seq_row, block):
    count, heads, depth = queries.shape
    blocks = count // block
    factor = depth ** (-0.5)
    query_blocks = queries.reshape(blocks, block, heads, depth)
    seq_blocks = seq_row.reshape(blocks, block)
    starts = jnp.arange(blocks, dtype=jnp.int32) * block

    def one_block(items):
        query_block, seq_block, start = items
        scores = (
            jnp.einsum("qhd,khd->hqk", query_block, keys, preferred_element_type=jnp.float32)
            * factor
        )
        mask = block_mask(seq_block, seq_row, start)
        scores = jnp.where(mask[None], scores, NEG)
        top = jnp.max(scores, axis=-1, keepdims=True)
        expo = jnp.exp(scores - top)
        total = jnp.sum(expo, axis=-1, keepdims=True)
        probs = expo / total
        result = jnp.einsum(
            "hqk,khd->qhd", probs.astype(jnp.bfloat16), values, preferred_element_type=jnp.float32
        )
        return (result.astype(jnp.bfloat16), (top + jnp.log(total))[:, :, 0])

    results, log_totals = lax.map(one_block, (query_blocks, seq_blocks, starts))
    return (results.reshape(count, heads * depth), log_totals)


def attend_back(queries, keys, values, seq_row, log_totals, dattn, block):
    count, heads, depth = queries.shape
    blocks = count // block
    factor = depth ** (-0.5)
    query_blocks = queries.reshape(blocks, block, heads, depth)
    seq_blocks = seq_row.reshape(blocks, block)
    grad_blocks = dattn.reshape(blocks, block, heads, depth)
    starts = jnp.arange(blocks, dtype=jnp.int32) * block

    def one_back(carry, items):
        dkey_acc, dval_acc = carry
        query_block, seq_block, start, log_block, grad_block = items
        scores = (
            jnp.einsum("qhd,khd->hqk", query_block, keys, preferred_element_type=jnp.float32)
            * factor
        )
        mask = block_mask(seq_block, seq_row, start)
        probs = jnp.where(mask[None], jnp.exp(scores - log_block[:, :, None]), 0.0)
        dval_acc = dval_acc + jnp.einsum(
            "hqk,qhd->khd",
            probs.astype(jnp.bfloat16),
            grad_block,
            preferred_element_type=jnp.float32,
        )
        dprob = jnp.einsum("qhd,khd->hqk", grad_block, values, preferred_element_type=jnp.float32)
        delta = jnp.sum(probs * dprob, axis=-1, keepdims=True)
        dscore = (probs * (dprob - delta)).astype(jnp.bfloat16)
        dquery = (
            jnp.einsum("hqk,khd->qhd", dscore, keys, preferred_element_type=jnp.float32) * factor
        )
        dkey_acc = (
            dkey_acc
            + jnp.einsum("hqk,qhd->khd", dscore, query_block, preferred_element_type=jnp.float32)
            * factor
        )
        return ((dkey_acc, dval_acc), dquery)

    zeros = jnp.zeros((count, heads, depth), jnp.float32)
    (dkeys, dvals), dqueries = lax.scan(
        one_back, (zeros, zeros), (query_blocks, seq_blocks, starts, log_totals, grad_blocks)
    )
    return (
        dqueries.reshape(count, heads * depth),
        dkeys.reshape(count, heads * depth),
        dvals.reshape(count, heads * depth),
    )


def per_device(
    tokens,
    dealing,
    seq_ids,
    first_values,
    out_grad,
    norm1_gain,
    norm2_gain,
    w_query,
    w_key,
    w_value,
    w_out,
    w_gate,
    w_up,
    w_down,
):
    order = jnp.argsort(dealing)
    arrived = (
        lax.all_to_all(tokens[order], "dp", split_axis=0, concat_axis=0, tiled=True),
        lax.all_to_all(first_values[order], "dp", split_axis=0, concat_axis=0, tiled=True),
        lax.all_to_all(out_grad[order], "dp", split_axis=0, concat_axis=0, tiled=True),
        lax.all_to_all(dealing[order], "dp", split_axis=0, concat_axis=0, tiled=True),
    )
    in_rows, in_first, in_grad, in_slots = arrived
    count = in_rows.shape[0]
    local_slot = in_slots % count
    arrange = jnp.argsort(local_slot)
    resid = in_rows[arrange].astype(jnp.float32)
    first_rows = in_first[arrange].astype(jnp.float32)
    grad_bf = in_grad[arrange]
    shard = resid.shape[1]
    rank = lax.axis_index("tensor")
    gain1 = lax.dynamic_slice_in_dim(norm1_gain, rank * shard, shard).astype(jnp.float32)
    gain2 = lax.dynamic_slice_in_dim(norm2_gain, rank * shard, shard).astype(jnp.float32)
    cos_rows, sin_rows = rope_tables(seq_ids, HEAD_DIM)
    heads = w_query.shape[1] // HEAD_DIM
    block = min(512, count)
    normed1, scale1 = norm_forward(resid, gain1)
    query_pre = jnp.dot(normed1, w_query, preferred_element_type=jnp.float32)
    key_pre = jnp.dot(normed1, w_key, preferred_element_type=jnp.float32)
    value_pre = jnp.dot(normed1, w_value, preferred_element_type=jnp.float32)
    queries = (
        rotate(query_pre, cos_rows, sin_rows).astype(jnp.bfloat16).reshape(count, heads, HEAD_DIM)
    )
    keys = rotate(key_pre, cos_rows, sin_rows).astype(jnp.bfloat16).reshape(count, heads, HEAD_DIM)
    values = (
        (0.5 * value_pre + 0.5 * first_rows).astype(jnp.bfloat16).reshape(count, heads, HEAD_DIM)
    )
    attended, log_totals = attend(queries, keys, values, seq_ids, block)
    middle = resid + branch_sum(jnp.dot(attended, w_out, preferred_element_type=jnp.float32))
    normed2, scale2 = norm_forward(middle, gain2)
    gate = jnp.dot(normed2, w_gate, preferred_element_type=jnp.float32)
    upval = jnp.dot(normed2, w_up, preferred_element_type=jnp.float32)
    sigmoid = jax.nn.sigmoid(gate)
    hidden = (gate * sigmoid * upval).astype(jnp.bfloat16)
    result = (
        middle + branch_sum(jnp.dot(hidden, w_down, preferred_element_type=jnp.float32))
    ).astype(jnp.bfloat16)
    full_grad = gather_grad(grad_bf)
    grad_down = jnp.einsum("tf,td->fd", hidden, full_grad, preferred_element_type=jnp.float32)
    grad_hidden = jnp.einsum("td,fd->tf", full_grad, w_down, preferred_element_type=jnp.float32)
    grad_up = (grad_hidden * gate * sigmoid).astype(jnp.bfloat16)
    grad_gate = (grad_hidden * upval * sigmoid * (1.0 + gate * (1.0 - sigmoid))).astype(
        jnp.bfloat16
    )
    grad_wgate = jnp.einsum("td,tf->df", normed2, grad_gate, preferred_element_type=jnp.float32)
    grad_wup = jnp.einsum("td,tf->df", normed2, grad_up, preferred_element_type=jnp.float32)
    dnormed2 = input_sum(
        jnp.einsum("tf,df->td", grad_gate, w_gate, preferred_element_type=jnp.float32)
        + jnp.einsum("tf,df->td", grad_up, w_up, preferred_element_type=jnp.float32)
    )
    dmiddle_norm, dgain2 = norm_backward(dnormed2, middle, scale2, gain2)
    dmiddle = grad_bf.astype(jnp.float32) + dmiddle_norm
    full_attn_grad = gather_grad(dmiddle.astype(jnp.bfloat16))
    grad_wout = jnp.einsum(
        "tc,td->cd", attended, full_attn_grad, preferred_element_type=jnp.float32
    )
    dattn = jnp.einsum(
        "td,cd->tc", full_attn_grad, w_out, preferred_element_type=jnp.float32
    ).astype(jnp.bfloat16)
    dqueries, dkeys, dvals = attend_back(queries, keys, values, seq_ids, log_totals, dattn, block)
    dquery_pre = rotate_back(dqueries, cos_rows, sin_rows).astype(jnp.bfloat16)
    dkey_pre = rotate_back(dkeys, cos_rows, sin_rows).astype(jnp.bfloat16)
    half_dval = (0.5 * dvals.astype(jnp.bfloat16).astype(jnp.float32)).astype(jnp.bfloat16)
    grad_wquery = jnp.einsum("td,tc->dc", normed1, dquery_pre, preferred_element_type=jnp.float32)
    grad_wkey = jnp.einsum("td,tc->dc", normed1, dkey_pre, preferred_element_type=jnp.float32)
    grad_wvalue = jnp.einsum("td,tc->dc", normed1, half_dval, preferred_element_type=jnp.float32)
    dnormed1 = input_sum(
        jnp.einsum("tc,dc->td", dquery_pre, w_query, preferred_element_type=jnp.float32)
        + jnp.einsum("tc,dc->td", dkey_pre, w_key, preferred_element_type=jnp.float32)
        + jnp.einsum("tc,dc->td", half_dval, w_value, preferred_element_type=jnp.float32)
    )
    dresid_norm, dgain1 = norm_backward(dnormed1, resid, scale1, gain1)
    dresid = (dmiddle + dresid_norm).astype(jnp.bfloat16)
    summed = (
        lax.psum_scatter(grad_wquery, "dp", scatter_dimension=0, tiled=True),
        lax.psum_scatter(grad_wkey, "dp", scatter_dimension=0, tiled=True),
        lax.psum_scatter(grad_wvalue, "dp", scatter_dimension=0, tiled=True),
        lax.psum_scatter(grad_wout, "dp", scatter_dimension=1, tiled=True),
        lax.psum_scatter(grad_wgate, "dp", scatter_dimension=0, tiled=True),
        lax.psum_scatter(grad_wup, "dp", scatter_dimension=0, tiled=True),
        lax.psum_scatter(grad_down, "dp", scatter_dimension=1, tiled=True),
        lax.psum_scatter(dgain1[None, :], "dp", scatter_dimension=1, tiled=True),
        lax.psum_scatter(dgain2[None, :], "dp", scatter_dimension=1, tiled=True),
    )
    returned = (
        lax.all_to_all(result[local_slot], "dp", split_axis=0, concat_axis=0, tiled=True),
        lax.all_to_all(dresid[local_slot], "dp", split_axis=0, concat_axis=0, tiled=True),
        lax.all_to_all(half_dval[local_slot], "dp", split_axis=0, concat_axis=0, tiled=True),
    )
    restore = jnp.argsort(order)
    output = returned[0][restore]
    input_grad = returned[1][restore]
    first_grad = returned[2][restore]
    return (
        output,
        input_grad,
        first_grad,
        summed[7],
        summed[8],
        summed[0],
        summed[1],
        summed[2],
        summed[3],
        summed[4],
        summed[5],
        summed[6],
    )


def solution(mesh):
    in_specs = (
        P("dp", "tensor"),
        P("dp"),
        P("dp"),
        P("dp", "tensor"),
        P("dp", "tensor"),
        P(),
        P(),
        P(None, "tensor"),
        P(None, "tensor"),
        P(None, "tensor"),
        P("tensor", None),
        P(None, "tensor"),
        P(None, "tensor"),
        P("tensor", None),
    )
    out_specs = (
        P("dp", "tensor"),
        P("dp", "tensor"),
        P("dp", "tensor"),
        P("tensor", "dp"),
        P("tensor", "dp"),
        P("dp", "tensor"),
        P("dp", "tensor"),
        P("dp", "tensor"),
        P("tensor", "dp"),
        P("dp", "tensor"),
        P("dp", "tensor"),
        P("tensor", "dp"),
    )
    return jax.shard_map(
        per_device, mesh=mesh, in_specs=in_specs, out_specs=out_specs, check_vma=False
    )
```

profile of v0, /device:TPU:0, one launch (start us, length us, event | category | flops | bytes accessed | tf_op | source)
XLA Modules:
  0.0 1111.1 jit_solution(10349196735572572018)
XLA Ops:
  7.2 5.2 sort.45
  12.4 8.8 gather_fusion.1
  21.3 7.3 all-to-all-start.1
  28.6 5.0 gather_fusion
  34.9 4.6 all-to-all-start
  40.4 4.4 sort.46
  44.8 8.8 all-to-all-done
  53.5 3.9 gather_fusion.2
  57.7 5.7 psum.28
  65.0 5.0 gather_fusion.3
  70.0 4.2 all-to-all-start.2
  77.1 11.2 %all-to-all-done.2 = bf16[8,128,256]{2,1,0:T(8,128)(2,1)S(1)} async-done(((bf16[8,128,256]{2,1,0:T(8,128)(2,1)}), bf16[8,128,256]{2,1,0:T(8,128)(2,1)S(1)}, u32[]{:S(2)}, u32[]{:S(2)}) %all-to-all-start.2) | async-done | bytes 524320 | tf_op jit(solution)/shard_map/all_to_all | solution.py:193
  88.3 3.9 gather_fusion.4
  100.1 20.7 %while.27 = (s32[]{:T(128)}, bf16[2,512,4,64]{1,3,2,0:T(8,128)(2,1)}, f32[2,4,512]{2,1,0:T(4,128)}, s32[2,512]{1,0:T(2,128)S(1)}, s32[1024]{0:T(1024)S(1)}, /*in...) while((s32[]{:T(128)}, ...), condition=%wide.region_9.10_spmd, body=%wide.region_6.9_spmd.sunk | while | flops 563739136 | bytes 33241340 | solution.py:122
  123.4 3.8 fusion.65
  128.7 42.2 %reduce-scatter.18.cloned.1.call-done = f32[1024,256]{1,0:T(8,128)} async-done(((f32[1024,1024]{1,0:T(8,128)}), f32[1024,256]{1,0:T(8,128)}) %reduce-scatter.18.cloned.1.call-update) | async-done | bytes 1048592 | tf_op jit(solution)/shard_map/reduce_scatter | solution.py:61
  173.2 5.7 psum.29
  181.9 5.0 gather_fusion.7
  186.9 19.9 %all_to_all.87 = bf16[8,128,256]{2,1,0:T(8,128)(2,1)S(1)} all-to-all(bf16[8,128,256]{2,1,0:T(8,128)(2,1)} %bitcast.210), channel_id=1, replica_groups=mesh['dp'=8,'tensor'=4] {'dp'}, dimensions={0} | all-to-all | bytes 1048576 | tf_op jit(solution)/shard_map/all_to_all | solution.py:194
  206.8 5.3 gather_fusion.8
  212.7 5.4 fusion.67
  218.1 3.4 fusion.66
  221.5 11.8 %all-gather.12.cloned.1.call-done = bf16[1024,1024]{1,0:T(8,128)(2,1)} async-done(((bf16[1024,256]{1,0:T(8,128)(2,1)}), bf16[1024,1024]{1,0:T(8,128)(2,1)}) %all-gather.12.cloned.1.call-update) | async-done | bytes 2097168 | tf_op jit(solution)/shard_map/all_gather | solution.py:65
  233.2 6.3 multiply_convert_fusion.1
  242.0 3.9 convolution_add_fusion
  246.0 5.2 fusion.68
  251.3 39.3 %reduce-scatter.22.cloned.1.call-done = f32[1024,256]{1,0:T(8,128)} async-done(((f32[1024,1024]{1,0:T(8,128)}), f32[1024,256]{1,0:T(8,128)}) %reduce-scatter.22.cloned.1.call-update) | async-done | bytes 1048592 | tf_op jit(solution)/shard_map/reduce_scatter | solution.py:69
  292.2 5.8 psum.30
  298.0 39.6 %reduce-scatter.20.cloned.1.call-done = f32[1024,256]{1,0:T(8,128)} async-done(((f32[1024,1024]{1,0:T(8,128)}), f32[1024,256]{1,0:T(8,128)}) %reduce-scatter.20.cloned.1.call-update) | async-done | bytes 1048592 | tf_op jit(solution)/shard_map/reduce_scatter | solution.py:61
  337.5 3.4 fusion.62
  341.2 22.7 %all-gather.10.cloned.1.call-done = bf16[1024,1024]{1,0:T(8,128)(2,1)} async-done(((bf16[1024,256]{1,0:T(8,128)(2,1)}), bf16[1024,1024]{1,0:T(8,128)(2,1)}) %all-gather.10.cloned.1.call-update) | async-done | bytes 2097168 | tf_op jit(solution)/shard_map/all_gather | solution.py:65
  364.0 3.1 convolution_convert_fusion
  372.2 55.3 %while.28 = (s32[]{:T(128)}, f32[1024,4,64]{0,2,1:T(8,128)S(1)}, f32[1024,4,64]{0,2,1:T(8,128)}, f32[2,512,4,64]{1,0,3,2:T(2,128)}, bf16[2,512,4,64]{1,3,2,0:T(8...) while((s32[]{:T(128)}, f32[1024,4,64]{0,2,1:T(8,128)S(1)}, ...), condition=%wide.region_20.21_spmd.clone, body=%wide.region_18.20_spmd.clone.sunk | while | flops 1376647680 | bytes 74520776 | solution.py:164
  375.4 4.0 fusion.166
  379.4 4.4 multiply_reduce_fusion.5
  389.2 10.4 dynamic_update_slice.20
  402.7 4.4 fusion.166
  407.1 4.4 multiply_reduce_fusion.5
  416.9 10.4 dynamic_update_slice.20
  437.3 43.7 %reduce-scatter.24.cloned.1.call-done = f32[1024,256]{1,0:T(8,128)} async-done(((f32[1024,1024]{1,0:T(8,128)}), f32[1024,256]{1,0:T(8,128)}) %reduce-scatter.24.cloned.1.call-update) | async-done | bytes 1048592 | tf_op jit(solution)/shard_map/reduce_scatter | solution.py:69
  483.7 4.6 fusion.76
  489.9 4.7 fusion.78
  494.6 4.6 fusion.77
  500.3 3.3 fusion.75
  508.5 5.0 gather_fusion.5
  513.5 5.5 all-to-all-start.3
  522.2 5.2 gather_fusion.11
  527.4 6.1 all-to-all-done.3
  533.5 3.6 all-to-all-start.6
  537.1 6.1 psum.31
  545.0 5.0 gather_fusion.9
  552.1 3.7 all-to-all-start.5
  555.8 4.4 sort.47
  561.5 5.0 gather_fusion.6
  566.5 5.0 gather_fusion.12
  571.5 39.7 %reduce-scatter.40.cloned.1.call-done = f32[32,1]{1,0:T(8,128)} async-done(((f32[256,1]{1,0:T(8,128)}), f32[32,1]{1,0:T(8,128)}) %reduce-scatter.40.cloned.1.call-update) | async-done | bytes 144
  612.5 5.0 gather_fusion.10
  617.5 69.2 %reduce-scatter.38.cloned.1.call-done = f32[704,128]{1,0:T(8,128)} async-done(((f32[704,1024]{1,0:T(8,128)}), f32[704,128]{1,0:T(8,128)}) %reduce-scatter.38.cloned.1.call-update) | async-done | bytes 360464 | tf_op jit(solution)/shard_map/reduce_scatter | solution.py:275
  686.7 75.3 %reduce-scatter.36.cloned.1.call-done = f32[128,704]{0,1:T(8,128)} async-done(((f32[1024,704]{0,1:T(8,128)}), f32[128,704]{0,1:T(8,128)}) %reduce-scatter.36.cloned.1.call-update) | async-done | bytes 360464 | tf_op jit(solution)/shard_map/reduce_scatter | solution.py:274
  761.9 75.5 %reduce-scatter.34.cloned.1.call-done = f32[128,704]{0,1:T(8,128)} async-done(((f32[1024,704]{0,1:T(8,128)}), f32[128,704]{0,1:T(8,128)}) %reduce-scatter.34.cloned.1.call-update) | async-done | bytes 360464 | tf_op jit(solution)/shard_map/reduce_scatter | solution.py:273
  837.4 67.0 %reduce-scatter.32.cloned.1.call-done = f32[256,128]{1,0:T(8,128)} async-done(((f32[256,1024]{1,0:T(8,128)}), f32[256,128]{1,0:T(8,128)}) %reduce-scatter.32.cloned.1.call-update) | async-done | bytes 131088 | tf_op jit(solution)/shard_map/reduce_scatter | solution.py:272
  904.4 66.7 %reduce-scatter.30.cloned.1.call-done = f32[128,256]{1,0:T(8,128)} async-done(((f32[1024,256]{1,0:T(8,128)}), f32[128,256]{1,0:T(8,128)}) %reduce-scatter.30.cloned.1.call-update) | async-done | bytes 131088 | tf_op jit(solution)/shard_map/reduce_scatter | solution.py:271
  971.2 66.4 %reduce-scatter.28.cloned.1.call-done = f32[128,256]{1,0:T(8,128)} async-done(((f32[1024,256]{1,0:T(8,128)}), f32[128,256]{1,0:T(8,128)}) %reduce-scatter.28.cloned.1.call-update) | async-done | bytes 131088 | tf_op jit(solution)/shard_map/reduce_scatter | solution.py:270
  1037.5 66.8 %reduce-scatter.26.cloned.1.call-done = f32[128,256]{1,0:T(8,128)} async-done(((f32[1024,256]{1,0:T(8,128)}), f32[128,256]{1,0:T(8,128)}) %reduce-scatter.26.cloned.1.call-update) | async-done | bytes 131088 | tf_op jit(solution)/shard_map/reduce_scatter | solution.py:269
  (271 shorter events, 100.8 us)
Async XLA Ops:
  7.2 226.1 %copy-start = (bf16[704,1024]{1,0:T(8,128)(2,1)S(1)}, bf16[704,1024]{1,0:T(8,128)(2,1)}, u32[]{:S(2)}) copy-start(bf16[704,1024]{1,0:T(8,128)(2,1)} %param.31) | copy-start | bytes 4325380
  7.2 5.2 copy-start.2
  7.2 21.3 %copy-start.6 = (bf16[1024,256]{1,0:T(8,128)(2,1)S(1)}, bf16[1024,256]{1,0:T(8,128)(2,1)}, u32[]{:S(2)}) copy-start(bf16[1024,256]{1,0:T(8,128)(2,1)} %param.18) | copy-start | bytes 1572868
  12.4 21.1 %copy-start.47 = (s32[1024]{0:T(1024)}, s32[1024]{0:T(1024)S(1)}, u32[]{:S(2)}) copy-start(s32[1024]{0:T(1024)S(1)} %get-tuple-element.127) | copy-start | bytes 12292
  21.3 13.7 %all-to-all-start.1 = ((s32[8,128,1]{1,2,0:T(1,128)}), s32[8,128,1]{1,2,0:T(1,128)S(1)}, u32[]{:S(2)}, u32[]{:S(2)}) async-start(s32[8,128,1]{1,2,0:T(1,128)} %bitcast.9), calls=%async_computation.1 | async-start | bytes 8192 | tf_op jit(solution)/shard_map/all_to_all | solution.py:195
  34.9 18.6 %copy-start.42 = (s32[8,128,1]{1,2,0:T(1,128)}, s32[8,128,1]{1,2,0:T(1,128)S(1)}, u32[]{:S(2)}) copy-start(s32[8,128,1]{1,2,0:T(1,128)S(1)} %all-to-all-done.1) | copy-start | bytes 12292
  34.9 18.6 %all-to-all-start = ((bf16[8,128,256]{2,1,0:T(8,128)(2,1)}), bf16[8,128,256]{2,1,0:T(8,128)(2,1)S(1)}, u32[]{:S(2)}, u32[]{:S(2)}) async-start(bf16[8,128,256]{2,1,0:T(8,128)(2,1)} %bitcast.6), calls=%async_computation | async-start | bytes 1048576 | tf_op jit(solution)/shard_map/all_to_all | solution.py:192
  39.5 53.7 %all-gather.6.cloned.1.call-start = ((), (), s32[]{:S(2)}) async-start(), calls=%async_computation.20 | async-start | bytes 2621440 | tf_op jit(solution)/shard_map/all_gather | solution.py:57
  40.4 24.6 %copy-start.44 = (f32[256]{0:T(256)}, f32[256]{0:T(256)S(1)}, u32[]{:S(2)}) copy-start(f32[256]{0:T(256)S(1)} %dynamic-slice_convert_fusion.1) | copy-start | bytes 3076
  44.8 43.5 %copy-start.41 = (s32[1024]{0:T(1024)}, s32[1024]{0:T(1024)S(1)}, u32[]{:S(2)}) copy-start(s32[1024]{0:T(1024)S(1)} %fusion.58) | copy-start | bytes 12292
  53.5 11.5 %copy-start.7 = (bf16[1024,256]{1,0:T(8,128)(2,1)S(1)}, bf16[1024,256]{1,0:T(8,128)(2,1)}, u32[]{:S(2)}) copy-start(bf16[1024,256]{1,0:T(8,128)(2,1)} %param.21) | copy-start | bytes 1572868
  57.5 113.4 %copy-start.9 = (bf16[1024,256]{1,0:T(8,128)(2,1)}, bf16[1024,256]{1,0:T(8,128)(2,1)S(1)}, u32[]{:S(2)}) copy-start(bf16[1024,256]{1,0:T(8,128)(2,1)S(1)} %gather_fusion.2) | copy-start | bytes 1572868
  64.0 6.0 copy-start.39
  65.0 9.6 copy-start.31
  70.0 18.3 %all-to-all-start.2 = ((bf16[8,128,256]{2,1,0:T(8,128)(2,1)}), bf16[8,128,256]{2,1,0:T(8,128)(2,1)S(1)}, u32[]{:S(2)}, u32[]{:S(2)}) async-start(bf16[8,128,256]{2,1,0:T(8,128)(2,1)} %bitcast.16), calls=%async_computation.2 | async-start | bytes 1048576 | tf_op jit(solution)/shard_map/all_to_all | solution.py:193
  74.3 96.6 %reduce-scatter.18.cloned.1.call-start = ((), (), s32[]{:S(2)}) async-start(), calls=%async_computation.21 | async-start | bytes 5242880 | tf_op jit(solution)/shard_map/reduce_scatter | solution.py:61
  88.3 5.0 copy-start.23
  92.2 3.5 copy-start.25
  93.2 3.3 copy-start.27
  93.2 3.3 copy-start.29
  120.8 6.4 copy-start.13
  127.2 54.6 %copy-start.8 = (bf16[1024,256]{1,0:T(8,128)(2,1)S(1)}, bf16[1024,256]{1,0:T(8,128)(2,1)}, u32[]{:S(2)}) copy-start(bf16[1024,256]{1,0:T(8,128)(2,1)} %param.22) | copy-start | bytes 1572868
  127.3 85.4 %all-gather.8.cloned.1.call-start = ((), (), s32[]{:S(2)}) async-start(), calls=%async_computation.22 | async-start | bytes 2621440 | tf_op jit(solution)/shard_map/all_gather | solution.py:57
  181.8 51.4 %all-gather.12.cloned.1.call-start = ((), (), s32[]{:S(2)}) async-start(), calls=%async_computation.34 | async-start | bytes 2621440 | tf_op jit(solution)/shard_map/all_gather | solution.py:65
  212.1 78.5 %reduce-scatter.22.cloned.1.call-start = ((), (), s32[]{:S(2)}) async-start(), calls=%async_computation.24 | async-start | bytes 5242880 | tf_op jit(solution)/shard_map/reduce_scatter | solution.py:69
  212.7 5.4 copy-start.51
  212.7 5.4 copy-start.54
  233.2 6.3 copy-start.55
  245.9 91.6 %reduce-scatter.20.cloned.1.call-start = ((), (), s32[]{:S(2)}) async-start(), calls=%async_computation.23 | async-start | bytes 5242880 | tf_op jit(solution)/shard_map/reduce_scatter | solution.py:61
  251.2 39.4 %copy-start.12 = (f32[1024,256]{1,0:T(8,128)S(1)}, f32[1024,256]{1,0:T(8,128)}, u32[]{:S(2)}) copy-start(f32[1024,256]{1,0:T(8,128)} %get-tuple-element.277) | copy-start | bytes 3145732
  251.2 39.4 %copy-start.50 = (f32[256]{0:T(256)S(1)}, f32[256]{0:T(256)}, u32[]{:S(2)}) copy-start(f32[256]{0:T(256)} %dynamic-slice_convert_fusion) | copy-start | bytes 3076
  251.2 86.4 %copy-start.21 = (bf16[1024,256]{1,0:T(8,128)(2,1)S(1)}, bf16[1024,256]{1,0:T(8,128)(2,1)}, u32[]{:S(2)}) copy-start(bf16[1024,256]{1,0:T(8,128)(2,1)} %gather_fusion.8) | copy-start | bytes 1572868
  251.2 86.4 %copy-start.49 = (f32[1024]{0:T(1024)S(1)}, f32[1024]{0:T(1024)}, u32[]{:S(2)}) copy-start(f32[1024]{0:T(1024)} %get-tuple-element.302) | copy-start | bytes 12292
  251.2 112.7 %all-gather.10.cloned.1.call-start = ((), (), s32[]{:S(2)}) async-start(), calls=%async_computation.25 | async-start | bytes 2621440 | tf_op jit(solution)/shard_map/all_gather | solution.py:65
  337.5 26.4 %copy-start.32 = (bf16[256,1024]{1,0:T(8,128)(2,1)S(1)}, bf16[256,1024]{1,0:T(8,128)(2,1)}, u32[]{:S(2)}) copy-start(bf16[256,1024]{1,0:T(8,128)(2,1)} %param.28) | copy-start | bytes 1572868
  341.0 140.1 %reduce-scatter.24.cloned.1.call-start = ((), (), s32[]{:S(2)}) async-start(), calls=%async_computation.26 | async-start | bytes 5242880 | tf_op jit(solution)/shard_map/reduce_scatter | solution.py:69
  367.1 5.1 copy-start.14
  367.1 5.1 copy-start.38
  367.1 5.1 copy-start.58
  427.5 3.6 copy-start.28
  427.5 3.6 copy-start.30
  436.4 44.7 %copy-start.10 = (bf16[1024,256]{1,0:T(8,128)(2,1)S(1)}, bf16[1024,256]{1,0:T(8,128)(2,1)}, u32[]{:S(2)}) copy-start(bf16[1024,256]{1,0:T(8,128)(2,1)} %copy-done.9) | copy-start | bytes 1572868
  436.4 44.7 %copy-start.40 = (f32[1024]{0:T(1024)S(1)}, f32[1024]{0:T(1024)}, u32[]{:S(2)}) copy-start(f32[1024]{0:T(1024)} %copy-done.39) | copy-start | bytes 12292
  436.4 44.7 %copy-start.45 = (f32[256]{0:T(256)S(1)}, f32[256]{0:T(256)}, u32[]{:S(2)}) copy-start(f32[256]{0:T(256)} %copy-done.44) | copy-start | bytes 3076
  436.4 47.3 %copy-start.53 = (bf16[1024,1024]{1,0:T(8,128)(2,1)S(1)}, bf16[1024,1024]{1,0:T(8,128)(2,1)}, u32[]{:S(2)}) copy-start(bf16[1024,1024]{1,0:T(8,128)(2,1)} %all-gather.12.cloned.1.call-done) | copy-start | bytes 6291460
  436.4 123.8 %reduce-scatter.42.cloned.1.call-start = ((), (), s32[]{:S(2)}) async-start(), calls=%async_computation.36 | async-start | bytes 147456
  437.3 173.9 %reduce-scatter.40.cloned.1.call-start = ((), (), s32[]{:S(2)}) async-start(), calls=%async_computation.35 | async-start | bytes 147456
  483.6 203.0 %reduce-scatter.38.cloned.1.call-start = ((), (), s32[]{:S(2)}) async-start(), calls=%async_computation.33 | async-start | bytes 3244032 | tf_op jit(solution)/shard_map/reduce_scatter | solution.py:275
  488.3 273.6 %reduce-scatter.36.cloned.1.call-start = ((), (), s32[]{:S(2)}) async-start(), calls=%async_computation.32 | async-start | bytes 3244032 | tf_op jit(solution)/shard_map/reduce_scatter | solution.py:274
  494.6 342.9 %reduce-scatter.34.cloned.1.call-start = ((), (), s32[]{:S(2)}) async-start(), calls=%async_computation.31 | async-start | bytes 3244032 | tf_op jit(solution)/shard_map/reduce_scatter | solution.py:273
  499.3 4.4 copy-start.4
  499.3 4.4 copy-start.16
  499.3 405.1 %reduce-scatter.32.cloned.1.call-start = ((), (), s32[]{:S(2)}) async-start(), calls=%async_computation.30 | async-start | bytes 1179648 | tf_op jit(solution)/shard_map/reduce_scatter | solution.py:272
  503.6 467.5 %reduce-scatter.30.cloned.1.call-start = ((), (), s32[]{:S(2)}) async-start(), calls=%async_computation.29 | async-start | bytes 1179648 | tf_op jit(solution)/shard_map/reduce_scatter | solution.py:271
  505.5 532.0 %reduce-scatter.28.cloned.1.call-start = ((), (), s32[]{:S(2)}) async-start(), calls=%async_computation.28 | async-start | bytes 1179648 | tf_op jit(solution)/shard_map/reduce_scatter | solution.py:270
  513.5 20.0 %all-to-all-start.3 = ((bf16[8,128,256]{2,1,0:T(8,128)(2,1)}), bf16[8,128,256]{2,1,0:T(8,128)(2,1)S(1)}, u32[]{:S(2)}, u32[]{:S(2)}) async-start(bf16[8,128,256]{2,1,0:T(8,128)(2,1)} %bitcast.209), calls=%async_computation.5 | async-start | bytes 1048576 | tf_op jit(solution)/shard_map/all_to_all | solution.py:280
  519.0 585.2 %reduce-scatter.26.cloned.1.call-start = ((), (), s32[]{:S(2)}) async-start(), calls=%async_computation.27 | async-start | bytes 1179648 | tf_op jit(solution)/shard_map/reduce_scatter | solution.py:269
  522.1 21.1 %copy-start.11 = (bf16[1024,256]{1,0:T(8,128)(2,1)S(1)}, bf16[1024,256]{1,0:T(8,128)(2,1)}, u32[]{:S(2)}) copy-start(bf16[1024,256]{1,0:T(8,128)(2,1)} %copy-done.9) | copy-start | bytes 1572868
  522.1 21.1 %copy-start.22 = (f32[1024,256]{1,0:T(8,128)S(1)}, f32[1024,256]{1,0:T(8,128)}, u32[]{:S(2)}) copy-start(f32[1024,256]{1,0:T(8,128)} %reduce-scatter.24.cloned.1.call-done) | copy-start | bytes 3145732
  522.1 21.1 %copy-start.46 = (f32[1024]{0:T(1024)S(1)}, f32[1024]{0:T(1024)}, u32[]{:S(2)}) copy-start(f32[1024]{0:T(1024)} %get-tuple-element.300) | copy-start | bytes 12292
  533.5 18.6 %all-to-all-start.6 = ((bf16[8,128,256]{2,1,0:T(8,128)(2,1)}), bf16[8,128,256]{2,1,0:T(8,128)(2,1)S(1)}, u32[]{:S(2)}, u32[]{:S(2)}) async-start(bf16[8,128,256]{2,1,0:T(8,128)(2,1)} %bitcast.31), calls=%async_computation.10 | async-start | bytes 1048576 | tf_op jit(solution)/shard_map/all_to_all | solution.py:282
  545.0 10.9 copy-start.48
  552.1 60.4 %all-to-all-start.5 = ((bf16[8,128,256]{2,1,0:T(8,128)(2,1)}), bf16[8,128,256]{2,1,0:T(8,128)(2,1)S(1)}, u32[]{:S(2)}, u32[]{:S(2)}) async-start(bf16[8,128,256]{2,1,0:T(8,128)(2,1)} %bitcast.29), calls=%async_computation.9 | async-start | bytes 1048576 | tf_op jit(solution)/shard_map/all_to_all | solution.py:281
  566.5 537.8 %copy-start.1 = (bf16[704,1024]{1,0:T(8,128)(2,1)S(1)}, bf16[704,1024]{1,0:T(8,128)(2,1)}, u32[]{:S(2)}) copy-start(bf16[704,1024]{1,0:T(8,128)(2,1)} %param.31) | copy-start | bytes 4325380
  (24 other events, 43.5 us)
Sparse Core Ops, SparseCore 0:
  65.1 22.1 all-gather.5
  127.4 43.4 reduce-scatter.17
  181.9 23.9 all-gather.7
  212.2 20.9 all-gather.11
  246.0 44.5 reduce-scatter.21
  293.0 44.5 reduce-scatter.19
  341.1 22.8 all-gather.9
  436.5 44.4 reduce-scatter.23
  484.4 62.3 reduce-scatter.41
  550.0 61.2 reduce-scatter.39
  615.4 71.2 reduce-scatter.37
  690.6 71.2 reduce-scatter.35
  766.0 71.3 reduce-scatter.33
  841.3 63.0 reduce-scatter.31
  908.6 62.4 reduce-scatter.29
  975.0 62.4 reduce-scatter.27
  1041.7 62.4 reduce-scatter.25
where the time goes:
time: 1120 us; the launch traced here: 1110 us
  waiting for transfers between devices  756 us (68%)
  local copies, waits for them, and re-layouts  114 us (10%)
  matrix products  102 us (9%)
  other arithmetic  50.5 us (5%)
  blocking collectives  43.2 us (4%)
  starting transfers between devices  30.7 us (3%)
  between operations  15 us (1%)
    reduce_scatter x2, waiting for transfers between devices, input_sum(): return lax.psum_scatter(term, 'tensor', scatter_dimension=1, tiled=True)  83 us
    reduce_scatter x2, waiting for transfers between devices, branch_sum(): return lax.psum_scatter(term, 'tensor', scatter_dimension=1, tiled=True)  81.8 us
    reduce_scatter x1, waiting for transfers between devices, per_device(): lax.psum_scatter(grad_wgate, 'dp', scatter_dimension=0, tiled=True)  75.5 us
    reduce_scatter x1, waiting for transfers between devices, per_device(): lax.psum_scatter(grad_wup, 'dp', scatter_dimension=0, tiled=True)  75.3 us
    reduce_scatter x1, waiting for transfers between devices, per_device(): lax.psum_scatter(grad_down, 'dp', scatter_dimension=1, tiled=True)  69.2 us
    reduce_scatter x1, waiting for transfers between devices, per_device(): lax.psum_scatter(grad_wout, 'dp', scatter_dimension=1, tiled=True)  67 us
    reduce_scatter x1, waiting for transfers between devices, per_device(): lax.psum_scatter(grad_wquery, 'dp', scatter_dimension=0, tiled=True)  66.8 us
    reduce_scatter x1, waiting for transfers between devices, per_device(): lax.psum_scatter(grad_wvalue, 'dp', scatter_dimension=0, tiled=True)  66.7 us
  transfers between devices with their start and end apart: 23, of which 19 were waited for; matrix products, arithmetic and copies ran while one was open for 11% of the time, Pallas kernels for 0%

commit v1 on v0

v1 whole, which is shorter than its diff:
```python
import functools

import jax
import jax.numpy as jnp
from jax import lax
from jax.experimental import pallas as pl
from jax.experimental.pallas import tpu as pltpu
from jax.sharding import PartitionSpec as P

HEAD_DIM = 64
EPS = 1e-06
THETA = 10000.0
NEG = -1e30
BF = jnp.bfloat16
F32 = jnp.float32
BLK = 256
EXTRA = 8
MIB = 1 << 20


def nn(a, b):
    return lax.dot_general(a, b, (((1,), (0,)), ((), ())), preferred_element_type=F32)


def nt(a, b):
    return lax.dot_general(a, b, (((1,), (1,)), ((), ())), preferred_element_type=F32)


def tn(a, b):
    return lax.dot_general(a, b, (((0,), (0,)), ((), ())), preferred_element_type=F32)


def iota(shape, dim):
    return lax.broadcasted_iota(jnp.int32, shape, dim)


def whole(shape):
    return pl.BlockSpec(shape, lambda i, *_: (0,) * len(shape))


def rows(block, width):
    return pl.BlockSpec((block, width), lambda i, *_: (i, 0))


def params(mib):
    return pltpu.CompilerParams(
        dimension_semantics=("arbitrary",), vmem_limit_bytes=mib * MIB
    )


def sds(shape, dtype):
    return jax.ShapeDtypeStruct(shape, dtype)


def call(kernel, grid, ids, ins, outs, scratch=(), mib=40, name=None):
    return pl.pallas_call(
        kernel,
        out_shape=tuple(sds(s, d) for s, d, _ in outs),
        grid_spec=pltpu.PrefetchScalarGridSpec(
            num_scalar_prefetch=1,
            grid=(grid,),
            in_specs=[s for _, s in ins],
            out_specs=tuple(s for _, _, s in outs),
            scratch_shapes=list(scratch),
        ),
        compiler_params=params(mib),
        name=name,
    )(ids, *[a for a, _ in ins])


def pack_tokens(ids, deal_row, tok, n_dp):
    count, width = tok.shape
    per = count // n_dp

    def kernel(ids_ref, deal_ref, tok_ref, out_ref, pos_ref):
        deal = deal_ref[...]
        dest = deal // count
        slot = deal % count
        oh = iota((n_dp, count), 0) == dest
        before = iota((count, count), 0) < iota((count, count), 1)
        seen = nn(oh.astype(BF), before.astype(BF))
        base = (iota((n_dp, 1), 0) * per).astype(F32)
        pos = jnp.sum(jnp.where(oh, seen + base, 0.0), axis=0, keepdims=True)
        pos = pos.astype(jnp.int32)
        pos_ref[...] = jnp.broadcast_to(pos, (8, count))
        high = jnp.broadcast_to(slot // 32, (8, count))
        lowp = jnp.broadcast_to(slot % 32, (8, count))
        hl = jnp.where(iota((8, count), 0) == 0, high, lowp).astype(F32).astype(BF)
        tok = tok_ref[...]
        out_ref[:, per : per + EXTRA, :] = jnp.zeros((n_dp, EXTRA, width), BF)
        for d in range(n_dp):
            pick = (iota((per, count), 0) + d * per == pos).astype(F32).astype(BF)
            out_ref[d, 0:per, :] = nn(pick, tok).astype(BF)
            out_ref[d, per : per + 8, 0:per] = nt(hl, pick).astype(BF)

    return call(
        kernel,
        1,
        ids,
        [(deal_row, whole((1, count))), (tok, whole(tok.shape))],
        [
            ((n_dp, per + EXTRA, width), BF, whole((n_dp, per + EXTRA, width))),
            ((8, count), jnp.int32, whole((8, count))),
        ],
        name="pack_tokens",
    )


def pack_rest(ids, pos8, arrays, n_dp):
    count = arrays[0].shape[0]
    per = count // n_dp

    def kernel(ids_ref, pos_ref, *refs):
        pos = pos_ref[0:1, :]
        srcs, dsts = refs[: len(arrays)], refs[len(arrays) :]
        vals = [s[...] for s in srcs]
        for d in range(n_dp):
            pick = (iota((per, count), 0) + d * per == pos).astype(F32).astype(BF)
            for v, dst in zip(vals, dsts):
                dst[d] = nn(pick, v).astype(BF)

    return call(
        kernel,
        1,
        ids,
        [(pos8, whole((8, count)))] + [(a, whole(a.shape)) for a in arrays],
        [
            ((n_dp, per, a.shape[1]), BF, whole((n_dp, per, a.shape[1])))
            for a in arrays
        ],
        name="pack_rest",
    )


def one_hot(ids, row, col):
    count = row.shape[1]

    def kernel(ids_ref, row_ref, col_ref, a_ref, b_ref):
        i = pl.program_id(0)
        a_ref[...] = (iota((BLK, count), 0) + i * BLK == row_ref[...]).astype(F32).astype(BF)
        b_ref[...] = (iota((BLK, count), 1) == col_ref[...]).astype(F32).astype(BF)

    return call(
        kernel,
        count // BLK,
        ids,
        [(row, whole((1, count))), (col, rows(BLK, 1))],
        [((count, count), BF, rows(BLK, count))] * 2,
        name="one_hot",
    )


def permute_sum(ids, perm, parts, name):
    count, width = parts[0].shape

    def kernel(ids_ref, perm_ref, *refs):
        total = refs[0][...].astype(F32)
        for r in refs[1:-1]:
            total = total + r[...].astype(F32)
        refs[-1][...] = nn(perm_ref[...], total.astype(BF)).astype(BF)

    return call(
        kernel,
        1,
        ids,
        [(perm, whole(perm.shape))] + [(p, whole(p.shape)) for p in parts],
        [((count, width), BF, whole((count, width)))],
        name=name,
    )[0]


def place_grad(ids, perm, near, far):
    n_dp, per, two = near.shape
    count = n_dp * per
    width = two // 2

    def kernel(ids_ref, perm_ref, a_ref, b_ref, out_ref):
        t = ids_ref[0]
        perm = perm_ref[...]
        a = nn(perm, a_ref[...].reshape(count, two)).astype(BF)
        b = nn(perm, b_ref[...].reshape(count, two)).astype(BF)
        for flip, val in ((0, a[:, :width]), (2, a[:, width:]), (1, b[:, :width]), (3, b[:, width:])):
            at = pl.multiple_of((t ^ flip) * width, width)
            out_ref[:, pl.ds(at, width)] = val

    return call(
        kernel,
        count // BLK,
        ids,
        [(perm, rows(BLK, count)), (near, whole(near.shape)), (far, whole(far.shape))],
        [((count, 4 * width), BF, rows(BLK, 4 * width))],
        name="place_grad",
    )[0]


def head_mask(shape, head, split):
    lane = iota(shape, 1)
    if split:
        return (lane % (shape[1] // 2)) // (HEAD_DIM // 2) == head
    return lane // HEAD_DIM == head


def split_perm(width):
    half = HEAD_DIM // 2
    src = iota((width, width), 0)
    dst = iota((width, width), 1)
    second = dst // (width // 2)
    rest = dst % (width // 2)
    want = (rest // half) * HEAD_DIM + second * half + rest % half
    return (src == want).astype(F32).astype(BF)


def qkv_attention(ids, perm, pieces, firsts, cos, sin, gain, wq, wk, wv, start_col):
    n_dp, padded, width = pieces[0].shape
    per = firsts.shape[1]
    count = n_dp * per
    dim = gain.shape[1]
    heads = width // HEAD_DIM
    blocks = count // BLK

    def kernel(
        ids_ref, perm_ref, x0, x1, x2, x3, fv_ref, cos_ref, sin_ref, gain_ref,
        wq_ref, wk_ref, wv_ref, start_ref,
        x_out, n_out, q_out, k_out, v_out, o_out, lse_out, wqp, wkp, xs, ks, vs,
    ):
        i = pl.program_id(0)
        t = ids_ref[0]

        @pl.when(i == 0)
        def _():
            sp = split_perm(width)
            wqp[...] = nn(wq_ref[...], sp).astype(BF)
            wkp[...] = nn(wk_ref[...], sp).astype(BF)

        perm = perm_ref[...]
        for flip, ref in enumerate((x0, x1, x2, x3)):
            at = pl.multiple_of((t ^ flip) * width, width)
            xs[:, pl.ds(at, width)] = nn(perm, ref[:, 0:per, :].reshape(count, width))
        x = xs[...]
        x_out[...] = x.astype(BF)
        scale = lax.rsqrt(jnp.sum(x * x, axis=1, keepdims=True) / dim + EPS)
        normed = (x * scale * gain_ref[...]).astype(BF)
        n_out[...] = normed
        qp = nn(normed, wqp[...])
        kp = nn(normed, wkp[...])
        half = width // 2
        c, s = cos_ref[...], sin_ref[...]

        def rope(v):
            a, b = v[:, :half], v[:, half:]
            return jnp.concatenate([a * c - b * s, b * c + a * s], axis=1).astype(BF)

        q = rope(qp)
        k = rope(kp)
        fv = nn(perm, fv_ref[...].reshape(count, width))
        v = (0.5 * nn(normed, wv_ref[...]) + 0.5 * fv).astype(BF)
        q = (q.astype(F32) * HEAD_DIM ** (-0.5)).astype(BF)
        q_out[...] = q
        k_out[...] = k
        v_out[...] = v
        at = pl.multiple_of(i * BLK, BLK)
        ks[pl.ds(at, BLK), :] = k
        vs[pl.ds(at, BLK), :] = v
        start = start_ref[...]
        for j in range(blocks):

            @pl.when(i == j)
            def _(j=j):
                n = (j + 1) * BLK
                keys = ks[0:n, :]
                vals = vs[0:n, :]
                col = iota((BLK, n), 1)
                valid = (col >= start) & (col <= iota((BLK, n), 0) + j * BLK)
                out = jnp.zeros((BLK, width), F32)
                lse = jnp.zeros((BLK, 128), F32)
                for h in range(heads):
                    qh = jnp.where(head_mask((BLK, width), h, True), q, jnp.zeros_like(q))
                    sc = jnp.where(valid, nt(qh, keys), NEG)
                    top = jnp.max(sc, axis=1, keepdims=True)
                    ex = jnp.exp(sc - top)
                    total = jnp.sum(ex, axis=1, keepdims=True)
                    oh = nn(ex.astype(BF), vals) * (1.0 / total)
                    out = jnp.where(head_mask((BLK, width), h, False), oh, out)
                    lse = jnp.where(iota((BLK, 128), 1) == h, top + jnp.log(total), lse)
                o_out[...] = out.astype(BF)
                lse_out[...] = jnp.transpose(lse)[0:8, :]

    wide = rows(BLK, dim)
    narrow = rows(BLK, width)
    return call(
        kernel,
        blocks,
        ids,
        [(perm, rows(BLK, count))]
        + [(p, whole(p.shape)) for p in pieces]
        + [
            (firsts, whole(firsts.shape)),
            (cos, rows(BLK, width // 2)),
            (sin, rows(BLK, width // 2)),
            (gain, whole(gain.shape)),
            (wq, whole(wq.shape)),
            (wk, whole(wk.shape)),
            (wv, whole(wv.shape)),
            (start_col, rows(BLK, 1)),
        ],
        [
            ((count, dim), BF, wide),
            ((count, dim), BF, wide),
            ((count, width), BF, narrow),
            ((count, width), BF, narrow),
            ((count, width), BF, narrow),
            ((count, width), BF, narrow),
            ((8, count), F32, pl.BlockSpec((8, BLK), lambda i, *_: (0, i))),
            ((dim, width), BF, whole((dim, width))),
            ((dim, width), BF, whole((dim, width))),
        ],
        scratch=[
            pltpu.VMEM((BLK, dim), F32),
            pltpu.VMEM((count, width), BF),
            pltpu.VMEM((count, width), BF),
        ],
        name="qkv_attention",
    )


def feed_forward(ids, x, o_pieces, w_pieces, gain, w_gate, w_up, w_down):
    count, dim = x.shape
    width = o_pieces[0].shape[1]
    units = w_gate.shape[1]

    def kernel(
        ids_ref, x_ref, o0, o1, o2, o3, w0, w1, w2, w3, gain_ref, wg_ref, wu_ref, wd_ref,
        x1_out, n_out, g_out, u_out, h_out, yk0, yk2, ysend, ys,
    ):
        t = ids_ref[0]
        x1 = x_ref[...].astype(F32)
        for o, w in ((o0, w0), (o1, w1), (o2, w2), (o3, w3)):
            x1 = x1 + nn(o[...], w[...])
        x1_out[...] = x1
        scale = lax.rsqrt(jnp.sum(x1 * x1, axis=1, keepdims=True) / dim + EPS)
        normed = (x1 * scale * gain_ref[...]).astype(BF)
        n_out[...] = normed
        g = nn(normed, wg_ref[...])
        u = nn(normed, wu_ref[...])
        g_out[...] = g
        u_out[...] = u
        hid = (g * jax.nn.sigmoid(g) * u).astype(BF)
        h_out[...] = hid
        ys[...] = nn(hid, wd_ref[...])

        def piece(flip):
            return pl.ds(pl.multiple_of((t ^ flip) * width, width), width)

        yk0[...] = ys[:, piece(0)] + x1_out[:, piece(0)]
        yk2[...] = ys[:, piece(2)]
        ysend[0] = ys[:, piece(1)].astype(BF)
        ysend[1] = ys[:, piece(3)].astype(BF)

    wide = rows(BLK, dim)
    narrow = rows(BLK, width)
    mid = rows(BLK, units)
    return call(
        kernel,
        count // BLK,
        ids,
        [(x, wide)]
        + [(o, narrow) for o in o_pieces]
        + [(w, whole(w.shape)) for w in w_pieces]
        + [
            (gain, whole(gain.shape)),
            (w_gate, whole(w_gate.shape)),
            (w_up, whole(w_up.shape)),
            (w_down, whole(w_down.shape)),
        ],
        [
            ((count, dim), F32, wide),
            ((count, dim), BF, wide),
            ((count, units), F32, mid),
            ((count, units), F32, mid),
            ((count, units), BF, mid),
            ((count, width), F32, narrow),
            ((count, width), F32, narrow),
            ((2, count, width), BF, pl.BlockSpec((2, BLK, width), lambda i, *_: (0, i, 0))),
        ],
        scratch=[pltpu.VMEM((BLK, dim), F32)],
        name="feed_forward",
    )


def feed_backward(ids, x1, dy, g, u, w_pieces, gain, w_gate, w_up, w_down):
    count, dim = x1.shape
    width = w_pieces[0].shape[0]
    units = w_gate.shape[1]

    def kernel(
        ids_ref, x1_ref, dy_ref, g_ref, u_ref, w0, w1, w2, w3, gain_ref, wg_ref, wu_ref, wd_ref,
        dg_out, du_out, ak0, ak2, asend, dk0, dk2, dsend, gg_out, ds,
    ):
        i = pl.program_id(0)
        t = ids_ref[0]
        dy = dy_ref[...]
        g, u = g_ref[...], u_ref[...]
        sg = jax.nn.sigmoid(g)
        dh = nt(dy, wd_ref[...])
        du = (dh * (g * sg)).astype(BF)
        dg = (dh * u * sg * (1.0 + g * (1.0 - sg))).astype(BF)
        dg_out[...] = dg
        du_out[...] = du
        dn = nt(dg, wg_ref[...]) + nt(du, wu_ref[...])
        x1 = x1_ref[...]
        scale = lax.rsqrt(jnp.sum(x1 * x1, axis=1, keepdims=True) / dim + EPS)

        @pl.when(i == 0)
        def _():
            gg_out[...] = jnp.zeros_like(gg_out)

        gg_out[0:1, :] += jnp.sum(dn * (x1 * scale), axis=0, keepdims=True)
        z = dn * gain_ref[...]
        dot_row = jnp.sum(z * x1, axis=1, keepdims=True)
        part = scale * z - x1 * (scale * scale * scale * dot_row / dim) + 0.25 * dy.astype(F32)
        ds[...] = part

        def piece(flip):
            return pl.ds(pl.multiple_of((t ^ flip) * width, width), width)

        dk0[...] = ds[:, piece(0)]
        dk2[...] = ds[:, piece(2)]
        dsend[0] = ds[:, piece(1)].astype(BF)
        dsend[1] = ds[:, piece(3)].astype(BF)
        low = part.astype(BF)
        ak0[...] = nt(low, w0[...])
        asend[0] = nt(low, w1[...]).astype(BF)
        ak2[...] = nt(low, w2[...])
        asend[1] = nt(low, w3[...]).astype(BF)

    wide = rows(BLK, dim)
    narrow = rows(BLK, width)
    mid = rows(BLK, units)
    pair = ((2, count, width), BF, pl.BlockSpec((2, BLK, width), lambda i, *_: (0, i, 0)))
    keep = ((count, width), F32, narrow)
    return call(
        kernel,
        count // BLK,
        ids,
        [(x1, wide), (dy, wide), (g, mid), (u, mid)]
        + [(w, whole(w.shape)) for w in w_pieces]
        + [
            (gain, whole(gain.shape)),
            (w_gate, whole(w_gate.shape)),
            (w_up, whole(w_up.shape)),
            (w_down, whole(w_down.shape)),
        ],
        [
            ((count, units), BF, mid),
            ((count, units), BF, mid),
            keep,
            keep,
            pair,
            keep,
            keep,
            pair,
            ((8, dim), F32, whole((8, dim))),
        ],
        scratch=[pltpu.VMEM((BLK, dim), F32)],
        name="feed_backward",
    )


def attention_backward(ids, q, k, v, o, lse, a_parts, start_row, cos, sin, x, gain, wqp, wkp, wv):
    count, width = q.shape
    dim = x.shape[1]
    heads = width // HEAD_DIM
    blocks = count // BLK
    half = width // 2

    def kernel(
        ids_ref, q_ref, k_ref, v_ref, o_ref, lse_ref, a0, a1, a2, start_ref, cos_ref, sin_ref,
        x_ref, gain_ref, wq_ref, wk_ref, wv_ref,
        dv_out, dqkv_out, ek0, ek2, esend, gg_out, da, delta, dq, es,
    ):
        i = pl.program_id(0)
        t = ids_ref[0]

        @pl.when(i == 0)
        def _():
            gg_out[...] = jnp.zeros_like(gg_out)
            grad = (a0[...] + a1[...].astype(F32) + a2[...].astype(F32)).astype(BF)
            da[...] = grad
            prod = grad.astype(F32) * o_ref[...].astype(F32)
            pick = (iota((8, width), 1) // HEAD_DIM == iota((8, width), 0)).astype(F32)
            delta[...] = lax.dot_general(
                pick, prod, (((1,), (1,)), ((), ())),
                precision=lax.Precision.HIGHEST, preferred_element_type=F32,
            )
            dq[...] = jnp.zeros_like(dq)

        for j in range(blocks):

            @pl.when(i == j)
            def _(j=j):
                q0 = j * BLK
                n = count - q0
                qs = q_ref[q0:count, :]
                ds = da[q0:count, :]
                kj = k_ref[q0 : q0 + BLK, :]
                vj = v_ref[q0 : q0 + BLK, :]
                key = iota((BLK, n), 0)
                valid = (key + q0 >= start_ref[:, q0:count]) & (key <= iota((BLK, n), 1))
                dk = jnp.zeros((BLK, width), F32)
                dv = jnp.zeros((BLK, width), F32)
                grads, masked = [], []
                for h in range(heads):
                    mk = head_mask((BLK, width), h, True)
                    mv = head_mask((BLK, width), h, False)
                    kh = jnp.where(mk, kj, jnp.zeros_like(kj))
                    vh = jnp.where(mv, vj, jnp.zeros_like(vj))
                    sc = nt(kh, qs) - lse_ref[h : h + 1, q0:count]
                    pr = jnp.exp(jnp.where(valid, sc, NEG))
                    dp = nt(vh, ds)
                    dsc = (pr * (dp - delta[h : h + 1, q0:count])).astype(BF)
                    dv = jnp.where(mv, nn(pr.astype(BF), ds), dv)
                    dk = jnp.where(mk, nn(dsc, qs), dk)
                    grads.append(dsc)
                    masked.append(kh)
                dq[q0:count, :] += tn(jnp.concatenate(grads, 0), jnp.concatenate(masked, 0))
                es[0, :, 0:width] = dk
                es[1, :, 0:width] = dv

        at = pl.multiple_of(i * BLK, BLK)
        dqj = dq[pl.ds(at, BLK), :] * HEAD_DIM ** (-0.5)
        dkj = es[0, :, 0:width]
        dvj = es[1, :, 0:width]
        c, s = cos_ref[...], sin_ref[...]

        def rope_back(g):
            a, b = g[:, :half], g[:, half:]
            return jnp.concatenate([a * c + b * s, b * c - a * s], axis=1).astype(BF)

        dqp = rope_back(dqj)
        dkp = rope_back(dkj)
        dvp = (0.5 * dvj.astype(BF).astype(F32)).astype(BF)
        dv_out[...] = dvp
        sp = split_perm(width)
        dqkv_out[:, 0:width] = nt(dqp, sp).astype(BF)
        dqkv_out[:, width : 2 * width] = nt(dkp, sp).astype(BF)
        dqkv_out[:, 2 * width : 3 * width] = dvp
        dn = nt(dqp, wq_ref[...]) + nt(dkp, wk_ref[...]) + nt(dvp, wv_ref[...])
        x = x_ref[...].astype(F32)
        scale = lax.rsqrt(jnp.sum(x * x, axis=1, keepdims=True) / dim + EPS)
        gg_out[0:1, :] += jnp.sum(dn * (x * scale), axis=0, keepdims=True)
        z = dn * gain_ref[...]
        dot_row = jnp.sum(z * x, axis=1, keepdims=True)
        es[0] = scale * z - x * (scale * scale * scale * dot_row / dim)

        def piece(flip):
            return pl.ds(pl.multiple_of((t ^ flip) * width, width), width)

        ek0[...] = es[0, :, piece(0)]
        ek2[...] = es[0, :, piece(2)]
        esend[0] = es[0, :, piece(1)].astype(BF)
        esend[1] = es[0, :, piece(3)].astype(BF)

    narrow = rows(BLK, width)
    pair = ((2, count, width), BF, pl.BlockSpec((2, BLK, width), lambda i, *_: (0, i, 0)))
    keep = ((count, width), F32, narrow)
    full = whole((count, width))
    return call(
        kernel,
        blocks,
        ids,
        [(q, full), (k, full), (v, full), (o, full), (lse, whole(lse.shape))]
        + [(a, full) for a in a_parts]
        + [
            (start_row, whole((1, count))),
            (cos, rows(BLK, half)),
            (sin, rows(BLK, half)),
            (x, rows(BLK, dim)),
            (gain, whole(gain.shape)),
            (wqp, whole(wqp.shape)),
            (wkp, whole(wkp.shape)),
            (wv, whole(wv.shape)),
        ],
        [
            ((count, width), BF, narrow),
            ((count, 3 * width), BF, rows(BLK, 3 * width)),
            keep,
            keep,
            pair,
            ((8, dim), F32, whole((8, dim))),
        ],
        scratch=[
            pltpu.VMEM((count, width), BF),
            pltpu.VMEM((8, count), F32),
            pltpu.VMEM((count, width), F32),
            pltpu.VMEM((2, BLK, dim), F32),
        ],
        mib=48,
        name="attention_backward",
    )


ORDER = (0, 2, 1, 3)


def weight_grads(ids, pairs, name):
    count, dim = pairs[0][0].shape
    chunk = dim // 8

    def kernel(ids_ref, *refs):
        m = len(pairs)
        ins, outs, tmp = refs[: 2 * m], refs[2 * m : 4 * m], refs[4 * m :]
        y = ids_ref[1] & 1
        for p in range(m):
            tmp[p][...] = tn(ins[2 * p][...], ins[2 * p + 1][...])
            keep = pl.ds(pl.multiple_of(y * chunk, chunk), chunk)
            send = pl.ds(pl.multiple_of((1 - y) * chunk, chunk), chunk)
            outs[2 * p][0] = tmp[p][keep, :].astype(BF)
            outs[2 * p + 1][0] = tmp[p][send, :].astype(BF)

    def left_map(j, ids):
        flip = (j & 1) * 2 + (j >> 1)
        return (0, (ids[1] >> 1) ^ flip)

    ins, outs, scratch = [], [], []
    for left, right in pairs:
        ins.append((left, pl.BlockSpec((count, 2 * chunk), left_map)))
        ins.append((right, whole(right.shape)))
        spec = pl.BlockSpec((1, chunk, right.shape[1]), lambda j, *_: (j, 0, 0))
        outs += [((4, chunk, right.shape[1]), BF, spec)] * 2
        scratch.append(pltpu.VMEM((2 * chunk, right.shape[1]), F32))
    flat = call(kernel, 4, ids, ins, outs, scratch, mib=48, name=name)
    return [(flat[2 * p], flat[2 * p + 1]) for p in range(len(pairs))]


def flip_dp(value, bit):
    n = lax.axis_size("dp")
    return lax.ppermute(value, "dp", [(d, d ^ bit) for d in range(n)])


def flip_tensor(value, bit):
    return lax.ppermute(value, "tensor", [(d, d ^ bit) for d in range(4)])


def halve_sum(keep, send):
    total = keep.astype(F32) + flip_dp(send, 1).astype(F32)
    total = total[0:2] + flip_dp(total[2:4].astype(BF), 2).astype(F32)
    return total[0] + flip_dp(total[1].astype(BF), 4).astype(F32)


def gather_pieces(own):
    one = flip_tensor(own, 1)
    two = flip_tensor(own, 2)
    three = flip_tensor(two, 1)
    return (own, one, two, three)


def scatter_parts(keep0, keep2, send):
    got = flip_tensor(send, 1)
    far = flip_tensor((keep2 + got[1].astype(F32)).astype(BF), 2)
    return (keep0, got[0], far)


def per_device(
    tokens,
    dealing,
    seq_ids,
    first_values,
    out_grad,
    norm1_gain,
    norm2_gain,
    w_query,
    w_key,
    w_value,
    w_out,
    w_gate,
    w_up,
    w_down,
):
    n_dp = lax.axis_size("dp")
    count, width = tokens.shape
    dim = norm1_gain.shape[0]
    per = count // n_dp
    t = lax.axis_index("tensor")
    d = lax.axis_index("dp")
    ids = jnp.stack([t, d]).astype(jnp.int32)

    def exchange(packed):
        return lax.all_to_all(packed, "dp", split_axis=0, concat_axis=0, tiled=True)

    deal_row = dealing.reshape(1, count)
    sent, pos8 = pack_tokens(ids, deal_row, tokens, n_dp)
    arrived = exchange(sent)
    grad_far = flip_tensor(out_grad, 2)
    pieces = gather_pieces(arrived)
    slots = (
        arrived[:, per, :per].astype(F32) * 32.0 + arrived[:, per + 1, :per].astype(F32)
    ).astype(jnp.int32)
    place, place_t = one_hot(ids, slots.reshape(1, count), slots.reshape(count, 1))

    first_sent, near_sent = pack_rest(
        ids, pos8, [first_values, jnp.concatenate([out_grad, grad_far], axis=1)], n_dp
    )
    first_sent, pieces0 = lax.optimization_barrier((first_sent, arrived))
    firsts = exchange(first_sent)
    near_sent, firsts = lax.optimization_barrier((near_sent, firsts))
    near = exchange(near_sent)
    far = flip_tensor(near, 1)

    start = jnp.sum(seq_ids[None, :] < seq_ids[:, None], axis=1, dtype=jnp.int32)
    start_flat = start
    offset = (jnp.arange(count, dtype=jnp.int32) - start_flat).astype(F32)
    half = HEAD_DIM // 2
    freqs = THETA ** (-jnp.arange(half, dtype=F32) / half)
    angles = offset[:, None] * freqs[None, :]
    reps = (1, width // HEAD_DIM)
    cos = jnp.tile(jnp.cos(angles), reps)
    sin = jnp.tile(jnp.sin(angles), reps)
    gain1 = norm1_gain.astype(F32).reshape(1, dim)
    gain2 = norm2_gain.astype(F32).reshape(1, dim)

    x, normed1, q, k, v, attended, lse, wqp, wkp = qkv_attention(
        ids, place, pieces, firsts, cos, sin, gain1, w_query, w_key, w_value,
        start_flat.reshape(count, 1),
    )
    w_pieces = gather_pieces(w_out)
    o_pieces = gather_pieces(attended)
    dy = place_grad(ids, place, near, far)
    x1, normed2, gate, up, hidden, yk0, yk2, ysend = feed_forward(
        ids, x, o_pieces, w_pieces, gain2, w_gate, w_up, w_down
    )
    dgate, dup, ak0, ak2, asend, dk0, dk2, dsend, gg2 = feed_backward(
        ids, x1, dy, gate, up, w_pieces, gain2, w_gate, w_up, w_down
    )
    a_parts = scatter_parts(ak0, ak2, asend)
    y_parts = scatter_parts(yk0, yk2, ysend)
    d_parts = scatter_parts(dk0, dk2, dsend)
    dx1 = d_parts[0] + d_parts[1].astype(F32) + d_parts[2].astype(F32)
    da = gather_pieces(dx1.astype(BF))

    dvp, dqkv, ek0, ek2, esend, gg1 = attention_backward(
        ids, q, k, v, attended, lse, a_parts, start_flat.reshape(1, count), cos, sin, x, gain1,
        wqp, wkp, w_value,
    )
    e_parts = scatter_parts(ek0, ek2, esend)

    da_full = jnp.zeros((count, dim), BF)
    for flip in range(4):
        da_full = lax.dynamic_update_slice(da_full, da[flip], (0, (t ^ flip) * width))

    if n_dp == 8:
        mlp = weight_grads(
            ids, [(normed2, dgate), (normed2, dup), (dy, hidden)], "grads_mlp"
        )
        gw_gate, gw_up, gw_down = [halve_sum(*pair) for pair in mlp]
        gw_down = gw_down.T
        (att,) = weight_grads(ids, [(normed1, dqkv)], "grads_qkv")
        gw_qkv = halve_sum(*att)
        gw_q, gw_k, gw_v = jnp.split(gw_qkv, 3, axis=1)
        (wo,) = weight_grads(ids, [(da_full, attended)], "grads_out")
        gw_out = halve_sum(*wo).T
    else:

        def scattered(left, right, dim_):
            full = jnp.einsum("ta,tb->ab", left, right, preferred_element_type=F32)
            return lax.psum_scatter(full, "dp", scatter_dimension=dim_, tiled=True)

        gw_gate = scattered(normed2, dgate, 0)
        gw_up = scattered(normed2, dup, 0)
        gw_down = scattered(hidden, dy, 1)
        gw_q, gw_k, gw_v = [
            scattered(normed1, p, 0) for p in jnp.split(dqkv, 3, axis=1)
        ]
        gw_out = scattered(attended, da_full, 1)

    gains = lax.psum(jnp.concatenate([gg1[0:1], gg2[0:1]], axis=0), ("dp", "tensor"))
    part = width // n_dp
    mine = lax.dynamic_slice(gains, (0, t * width + d * part), (2, part))

    pos = pos8[0]
    restore = one_hot(ids, pos.reshape(1, count), pos.reshape(count, 1))[1]

    def send_back(parts, name):
        packed = permute_sum(ids, place_t, parts, name).reshape(n_dp, per, width)
        back = exchange(packed).reshape(count, width)
        return permute_sum(ids, restore, [back], name + "_restore")

    output = send_back(list(y_parts), "output")
    first_grad = send_back([dvp], "first_grad")
    input_grad = send_back(list(e_parts) + [dx1], "input_grad")
    return (
        output,
        input_grad,
        first_grad,
        mine[0:1],
        mine[1:2],
        gw_q,
        gw_k,
        gw_v,
        gw_out,
        gw_gate,
        gw_up,
        gw_down,
    )


def solution(mesh):
    in_specs = (
        P("dp", "tensor"),
        P("dp"),
        P("dp"),
        P("dp", "tensor"),
        P("dp", "tensor"),
        P(),
        P(),
        P(None, "tensor"),
        P(None, "tensor"),
        P(None, "tensor"),
        P("tensor", None),
        P(None, "tensor"),
        P(None, "tensor"),
        P("tensor", None),
    )
    out_specs = (
        P("dp", "tensor"),
        P("dp", "tensor"),
        P("dp", "tensor"),
        P("tensor", "dp"),
        P("tensor", "dp"),
        P("dp", "tensor"),
        P("dp", "tensor"),
        P("dp", "tensor"),
        P("tensor", "dp"),
        P("dp", "tensor"),
        P("dp", "tensor"),
        P("tensor", "dp"),
    )
    return jax.shard_map(
        per_device, mesh=mesh, in_specs=in_specs, out_specs=out_specs, check_vma=False
    )
```

time: 1120 us -> 447 us (0.40)
  waiting for transfers between devices: 756 us -> 91.3 us
  Pallas kernels: 0 us -> 113 us
  matrix products: 102 us -> 0 us
  starting transfers between devices: 30.7 us -> 70.2 us
  other arithmetic: 50.5 us -> 25.4 us
  local copies, waits for them, and re-layouts: 114 us -> 95.5 us
  between operations: 15 us -> 1.68 us
    reduce_scatter x11 -> x0, waiting for transfers between devices: 652 us -> none  [the longest x2 83 us: input_sum(): return lax.psum_scatter(term, 'tensor', scatter_dimension=1, tiled=True)]
    pallas_call x0 -> x18, Pallas kernels: none -> 113 us  [call(): pl.pallas_call(kernel, out_shape=tuple((sds(s, d) for s, d, _ in outs)),...]
    dot_general x35 -> x0, matrix products: 102 us -> none  [the longest x2 8.8 us: one_back(): jnp.einsum('qhd,khd->hqk', grad_block, values, preferred_element_type=jnp...]
    ppermute x0 -> x37, waiting for transfers between devices: none -> 91.2 us  [the longest x15 50.3 us: flip_dp(): return lax.ppermute(value, 'dp', [(d, d ^ bit) for d in range(n)])]
    gather x14 -> x0, local copies, waits for them, and re-layouts: 68.1 us -> none  [the longest x1 8.84 us: per_device(): dealing[order]]
    unnamed x120 -> x176, local copies, waits for them, and re-layouts: 11 us -> 62.8 us
    unnamed x19 -> x0, waiting for transfers between devices: 40 us -> none
    ppermute x0 -> x37, starting transfers between devices: none -> 37.3 us  [the longest x15 24 us: flip_dp(): return lax.ppermute(value, 'dp', [(d, d ^ bit) for d in range(n)])]
  transfers between devices with their start and end apart: 23 -> 43, of which waited for: 19 -> 11; matrix products, arithmetic and copies ran while one was open for 11% -> 16% of each run, Pallas kernels for 0% -> 24%
where the time goes in v1:
time: 447 us; the launch traced here: 441 us
  Pallas kernels  113 us (25%)
  local copies, waits for them, and re-layouts  95.5 us (21%)
  waiting for transfers between devices  91.3 us (20%)
  starting transfers between devices  70.2 us (16%)
  blocking collectives  43.9 us (10%)
  other arithmetic  25.4 us (6%)
    pallas_call x18, Pallas kernels, call(): pl.pallas_call(kernel, out_shape=tuple((sds(s, d) for s, d, _ in outs)),...  113 us
    unnamed x176, local copies, waits for them, and re-layouts  62.8 us
    ppermute x15, waiting for transfers between devices, flip_dp(): return lax.ppermute(value, 'dp', [(d, d ^ bit) for d in range(n)])  50.3 us
    psum x1, blocking collectives, per_device(): lax.psum(jnp.concatenate([gg1[0:1], gg2[0:1]], axis=0), ('dp', 'tensor'))  43.9 us
    ppermute x22, waiting for transfers between devices, flip_tensor(): return lax.ppermute(value, 'tensor', [(d, d ^ bit) for d in range(4)])  41 us
    all_to_all x6, starting transfers between devices, exchange(): return lax.all_to_all(packed, 'dp', split_axis=0, concat_axis=0, tiled=True)  32.9 us
    ppermute x15, starting transfers between devices, flip_dp(): return lax.ppermute(value, 'dp', [(d, d ^ bit) for d in range(n)])  24 us
    ppermute x22, starting transfers between devices, flip_tensor(): return lax.ppermute(value, 'tensor', [(d, d ^ bit) for d in range(4)])  13.2 us
  transfers between devices with their start and end apart: 43, of which 11 were waited for; matrix products, arithmetic and copies ran while one was open for 16% of the time, Pallas kernels for 24%

profile of v1, /device:TPU:0, one launch (start us, length us, event | category | flops | bytes accessed | tf_op | source)
XLA Modules:
  0.0 440.7 jit_solution(18135402659541158655)
XLA Ops:
  2.5 2.8 pack_tokens.1
  5.3 7.3 %all-to-all-start = ((bf16[8,136,256]{2,1,0:T(8,128)(2,1)}), bf16[8,136,256]{2,1,0:T(8,128)(2,1)}, u32[]{:S(2)}, u32[]{:S(2)}) async-start(bf16[8,136,256]{2,1,0:T(8,128)(2,1)} %get-tuple-element.66), calls=%async_computation | async-start | bytes 1114112 | tf_op jit(solution)/shard_map/all_to_all | solution.py:688
  14.1 12.1 %collective-permute-done.3 = bf16[1024,256]{1,0:T(8,128)(2,1)S(1)} collective-permute-done((bf16[1024,256]{1,0:T(8,128)(2,1)}, bf16[1024,256]{1,0:T(8,128)(2,1)S(1)}, u32[]{:S(2)}, u32[]{:S(2)}) %collective-permute-start.3) | collective-permute-done | bytes 524320 | tf_op jit(solution)/shard_map/ppermute | solution.py:641
  27.4 3.4 pack_rest.1
  30.7 5.7 %all-to-all-start.1 = ((bf16[8,128,256]{2,1,0:T(8,128)(2,1)}), bf16[8,128,256]{2,1,0:T(8,128)(2,1)S(1)}, u32[]{:S(2)}, u32[]{:S(2)}) async-start(bf16[8,128,256]{2,1,0:T(8,128)(2,1)} %get-tuple-element.71), calls=%async_computation.1 | async-start | bytes 1048576 | tf_op jit(solution)/shard_map/all_to_all | solution.py:688
  39.1 13.2 %collective-permute-done.1.x2 = bf16[8,136,256]{2,1,0:T(8,128)(2,1)} collective-permute-done((bf16[8,136,256]{2,1,0:T(8,128)(2,1)}, bf16[8,136,256]{2,1,0:T(8,128)(2,1)}, u32[]{:S(2)}, u32[]{:S(2)}) %collective-permute-start.1) | collective-permute-done | bytes 557088 | tf_op jit(solution)/shard_map/ppermute | solution.py:641
  52.3 6.2 %all-to-all-start.3 = ((bf16[8,128,512]{2,1,0:T(8,128)(2,1)}), bf16[8,128,512]{2,1,0:T(8,128)(2,1)}, u32[]{:S(2)}, u32[]{:S(2)}) async-start(bf16[8,128,512]{2,1,0:T(8,128)(2,1)} %get-tuple-element.83), calls=%async_computation.3 | async-start | bytes 2097152 | tf_op jit(solution)/shard_map/all_to_all | solution.py:688
  64.3 1.7 one_hot.3
  72.6 15.7 %qkv_attention.1 = (bf16[1024,1024]{1,0:T(8,128)(2,1)S(1)}, bf16[1024,1024]{1,0:T(8,128)(2,1)S(1)}, bf16[1024,256]{1,0:T(8,128)(2,1)S(1)}, bf16[1024,256]{1,0:T(...) custom-call(s32[2]{0:T(128)S(1)} %pad_add_fusion.ids_ref, ...), custom_call_target="tpu_custom_call" | custom-call | tf_op jit(solution)/shard_map/qkv_attention/pallas_call | solution.py:56
  97.7 12.3 %collective-permute-done.5.o2 = bf16[1024,256]{1,0:T(8,128)(2,1)} collective-permute-done((bf16[1024,256]{1,0:T(8,128)(2,1)}, bf16[1024,256]{1,0:T(8,128)(2,1)}, u32[]{:S(2)}, u32[]{:S(2)}) %collective-permute-start.5) | collective-permute-done | bytes 524320 | tf_op jit(solution)/shard_map/ppermute | solution.py:641
  110.0 2.6 copy.76.wg_ref
  112.6 2.7 copy.77.wu_ref
  118.2 12.5 %feed_forward.1 = (f32[1024,1024]{1,0:T(8,128)}, bf16[1024,1024]{1,0:T(8,128)(2,1)}, f32[1024,704]{1,0:T(8,128)}, f32[1024,704]{1,0:T(8,128)}, bf16[1024,704]{1,...) custom-call(s32[2]{0:T(128)S(1)} %pad_add_fusion.ids_ref, ...), custom_call_target="tpu_custom_call" | custom-call | tf_op jit(solution)/shard_map/feed_forward/pallas_call | solution.py:56
  134.4 3.3 collective-permute-done.10
  137.7 2.3 fusion.4
  141.5 5.0 %place_grad.1.dy_ref.refs_4_ = bf16[1024,1024]{1,0:T(8,128)(2,1)S(1)} custom-call(s32[2]{0:T(128)S(1)} %pad_add_fusion.ids_ref, bf16[1024,1024]{1,0:T(8,128)(2,1)S(1)} %copy-done.9, bf16[8,128,512]{2,1,0:T(8,128)(2,1)} %all-to-all-done.3.a_ref, bf16[8,128,512]{2,1,0:T(8,128)(2,1)S(1)} %collective-permute-done.12.b_ref), custom_call_target="tpu_custom_call" | custom-call | tf_op jit(solution)/shard_map/place_grad/pallas_call | solution.py:56
  147.8 18.9 %feed_backward.1 = (bf16[1024,704]{1,0:T(8,128)(2,1)S(1)}, bf16[1024,704]{1,0:T(8,128)(2,1)S(1)}, f32[1024,256]{1,0:T(8,128)S(1)}, f32[1024,256]{1,0:T(8,128)S(1...) custom-call(s32[2]{0:T(128)S(1)} %pad_add_fusion.ids_ref, ...), custom_call_target="tpu_custom_call" | custom-call | tf_op jit(solution)/shard_map/feed_backward/pallas_call | solution.py:56
  175.0 10.9 %grads_mlp.1 = (bf16[4,128,704]{2,1,0:T(8,128)(2,1)S(1)}, bf16[4,128,704]{2,1,0:T(8,128)(2,1)S(1)}, bf16[4,128,704]{2,1,0:T(8,128)(2,1)S(1)}, bf16[4,128,704]{2,...) custom-call(s32[2]{0:T(128)S(1)} %pad_add_fusion.ids_ref, ...), custom_call_target="tpu_custom_call" | custom-call | tf_op jit(solution)/shard_map/grads_mlp/pallas_call | solution.py:56
  191.3 2.4 copy.82
  193.7 1.7 collective-permute-start.28
  195.5 2.3 copy.84
  199.1 3.1 output.1
  202.2 5.7 %all-to-all-start.2 = ((bf16[8,128,256]{2,1,0:T(8,128)(2,1)}), bf16[8,128,256]{2,1,0:T(8,128)(2,1)S(1)}, u32[]{:S(2)}, u32[]{:S(2)}) async-start(bf16[8,128,256]{2,1,0:T(8,128)(2,1)} %bitcast.13), calls=%async_computation.2 | async-start | bytes 1048576 | tf_op jit(solution)/shard_map/all_to_all | solution.py:688
  208.0 2.3 copy.86
  210.3 2.0 collective-permute-start.34
  213.3 3.0 one_hot.2
  224.7 7.9 %collective-permute-done.31 = bf16[4,128,704]{1,2,0:T(8,128)(2,1)} collective-permute-done((bf16[4,128,704]{1,2,0:T(8,128)(2,1)}, bf16[4,128,704]{1,2,0:T(8,128)(2,1)}, u32[]{:S(2)}, u32[]{:S(2)}) %collective-permute-start.31) | collective-permute-done | bytes 720928 | tf_op jit(solution)/shard_map/ppermute | solution.py:637
  232.7 2.3 copy.85
  235.0 1.6 convert_add_fusion.1
  238.5 1.8 collective-permute-start.32
  240.3 8.3 %collective-permute-done.34 = bf16[4,128,704]{1,2,0:T(8,128)(2,1)} collective-permute-done((bf16[4,128,704]{1,2,0:T(8,128)(2,1)}, bf16[4,128,704]{1,2,0:T(8,128)(2,1)}, u32[]{:S(2)}, u32[]{:S(2)}) %collective-permute-start.34) | collective-permute-done | bytes 720928 | tf_op jit(solution)/shard_map/ppermute | solution.py:637
  248.7 2.3 copy.87
  253.7 1.8 collective-permute-start.35
  255.5 1.6 copy-done.2
  257.1 2.0 output_restore.1
  265.9 2.4 collective-permute-start.30
  271.2 2.4 collective-permute-start.36
  273.6 11.3 %collective-permute-done.30 = bf16[128,704]{1,0:T(8,128)(2,1)S(1)} collective-permute-done((bf16[128,704]{1,0:T(8,128)(2,1)S(1)}, bf16[128,704]{1,0:T(8,128)(2,1)S(1)}, u32[]{:S(2)}, u32[]{:S(2)}) %collective-permute-start.30) | collective-permute-done | bytes 180256 | tf_op jit(solution)/shard_map/ppermute | solution.py:637
  285.7 3.4 collective-permute-done.33
  290.0 1.6 broadcast_in_dim.2
  291.6 2.4 constant_dynamic-update-slice_fusion.3
  294.6 17.3 %attention_backward.1 = (bf16[1024,256]{1,0:T(8,128)(2,1)S(1)}, bf16[1024,768]{1,0:T(8,128)(2,1)}, f32[1024,256]{1,0:T(8,128)}, f32[1024,256]{1,0:T(8,128)}, bf1...) custom-call(s32[2]{0:T(128)S(1)} %pad_add_fusion.ids_ref, bf16[1024,256]{1,0:T(8,128)(2,1)S(1)} %copy-done.56, ...), custom_call_target="tpu_custom_call" | custom-call | tf_op jit(solution)/shard_map/attention_backward/pallas_call | solution.py:56
  313.6 4.5 %grads_qkv.1 = (bf16[4,128,768]{2,1,0:T(8,128)(2,1)S(1)}, bf16[4,128,768]{2,1,0:T(8,128)(2,1)}) custom-call(s32[2]{0:T(128)S(1)} %pad_add_fusion.ids_ref, bf16[1024,1024]{1,0:T(8,128)(2,1)S(1)} %copy-done.21, bf16[1024,768]{1,0:T(8,128)(2,1)S(1)} %copy-done.25), custom_call_target="tpu_custom_call" | custom-call | tf_op jit(solution)/shard_map/grads_qkv/pallas_call | solution.py:56
  319.0 1.7 collective-permute-start.19
  321.5 1.9 copy.89
  323.4 1.9 copy.90
  325.3 1.9 copy.91
  330.3 4.4 all-to-all-start.5
  334.7 43.9 %psum.7 = f32[2,1024]{1,0:T(2,128)S(1)} all-reduce(f32[2,1024]{1,0:T(2,128)S(1)} %pad_maximum_fusion.1), channel_id=1, replica_groups=mesh['dp'=8,'tensor'=4] {'dp','tensor'}, use_global_device_ids=true, to_apply=%region_1.0 | all-reduce | flops 2048 | bytes 16384 | tf_op jit(solution)/shard_map/psum | solution.py:775
  379.3 2.0 constant_dynamic-update-slice_fusion.2
  381.2 1.9 constant_dynamic-update-slice_fusion.1
  385.8 1.6 copy-done.3
  387.4 3.1 first_grad_restore.1
  391.6 2.3 collective-permute-start.16
  395.0 2.1 constant_dynamic-update-slice_fusion.refs_0_
  397.1 4.1 grads_out.1
  403.1 2.2 collective-permute-start.21
  405.3 4.4 collective-permute-done.25
  410.5 1.7 collective-permute-start.26
  412.2 3.0 collective-permute-done.21
  417.4 3.7 all-to-all-start.4
  422.1 3.0 collective-permute-start.27
  425.8 11.9 %collective-permute-done.27 = bf16[128,256]{1,0:T(8,128)(2,1)S(1)} collective-permute-done((bf16[128,256]{1,0:T(8,128)(2,1)S(1)}, bf16[128,256]{1,0:T(8,128)(2,1)S(1)}, u32[]{:S(2)}, u32[]{:S(2)}) %collective-permute-start.27) | collective-permute-done | bytes 65568 | tf_op jit(solution)/shard_map/ppermute | solution.py:637
  438.5 2.0 input_grad_restore.1
  (284 shorter events, 98.2 us)
Async XLA Ops:
  2.5 24.9 %copy-start.52 = (bf16[1024,256]{1,0:T(8,128)(2,1)S(1)}, bf16[1024,256]{1,0:T(8,128)(2,1)}, u32[]{:S(2)}) copy-start(bf16[1024,256]{1,0:T(8,128)(2,1)} %refs_0_.1) | copy-start | bytes 1572868
  5.3 25.5 %copy-start.65 = (s32[8,1024]{1,0:T(8,128)}, s32[8,1024]{1,0:T(8,128)S(1)}, u32[]{:S(2)}) copy-start(s32[8,1024]{1,0:T(8,128)S(1)} %get-tuple-element.64.pos_ref) | copy-start | bytes 98308
  5.3 25.5 %all-to-all-start = ((bf16[8,136,256]{2,1,0:T(8,128)(2,1)}), bf16[8,136,256]{2,1,0:T(8,128)(2,1)}, u32[]{:S(2)}, u32[]{:S(2)}) async-start(bf16[8,136,256]{2,1,0:T(8,128)(2,1)} %get-tuple-element.66), calls=%async_computation | async-start | bytes 1114112 | tf_op jit(solution)/shard_map/all_to_all | solution.py:688
  12.6 25.9 %copy-start.82 = (s32[1024]{0:T(1024)S(1)}, s32[1024]{0:T(1024)}, u32[]{:S(2)}) copy-start(s32[1024]{0:T(1024)} %param.16) | copy-start | bytes 12292
  12.6 13.7 %collective-permute-start.3 = (bf16[1024,256]{1,0:T(8,128)(2,1)}, bf16[1024,256]{1,0:T(8,128)(2,1)S(1)}, u32[]{:S(2)}, u32[]{:S(2)}) collective-permute-start(bf16[1024,256]{1,0:T(8,128)(2,1)} %param.18), channel_id=1, source_target_pairs={{0,2},{1,3},{2,0},{3,1},{4,6},{5,7},{6,4},{7,5},{8,10},{9,11},{10,... | collective-permute-start | bytes 1572872 | tf_op jit(solution)/shard_map/ppermute | solution.py:641
  30.7 21.5 %all-to-all-start.1 = ((bf16[8,128,256]{2,1,0:T(8,128)(2,1)}), bf16[8,128,256]{2,1,0:T(8,128)(2,1)S(1)}, u32[]{:S(2)}, u32[]{:S(2)}) async-start(bf16[8,128,256]{2,1,0:T(8,128)(2,1)} %get-tuple-element.71), calls=%async_computation.1 | async-start | bytes 1048576 | tf_op jit(solution)/shard_map/all_to_all | solution.py:688
  36.4 15.9 %collective-permute-start.1 = (bf16[8,136,256]{2,1,0:T(8,128)(2,1)}, bf16[8,136,256]{2,1,0:T(8,128)(2,1)}, u32[]{:S(2)}, u32[]{:S(2)}) collective-permute-start(bf16[8,136,256]{2,1,0:T(8,128)(2,1)} %all-to-all-done.x0), channel_id=1, source_target_pairs={{0,2},{1,3},{2,0},{3,1},{4,6},{5,7},{6,4},{7,5},{8,10},{9,11},{10,... | collective-permute-start | bytes 1671176 | tf_op jit(solution)/shard_map/ppermute | solution.py:641
  37.9 59.3 %collective-permute-start.8 = (bf16[256,1024]{1,0:T(8,128)(2,1)}, bf16[256,1024]{1,0:T(8,128)(2,1)}, u32[]{:S(2)}, u32[]{:S(2)}) collective-permute-start(bf16[256,1024]{1,0:T(8,128)(2,1)} %w0.3), channel_id=1, source_target_pairs={{0,2},{1,3},{2,0},{3,1},{4,6},{5,7},{6,4},{7,5},{8,10},{9,11},{10,... | collective-permute-start | bytes 1572872 | tf_op jit(solution)/shard_map/ppermute | solution.py:641
  39.0 28.4 %collective-permute-start = (bf16[8,136,256]{2,1,0:T(8,128)(2,1)}, bf16[8,136,256]{2,1,0:T(8,128)(2,1)}, u32[]{:S(2)}, u32[]{:S(2)}) collective-permute-start(bf16[8,136,256]{2,1,0:T(8,128)(2,1)} %all-to-all-done.x0), channel_id=1, source_target_pairs={{0,1},{1,0},{2,3},{3,2},{4,5},{5,4},{6,7},{7,6},{8,9},{9,8},{10,11... | collective-permute-start | bytes 1671176 | tf_op jit(solution)/shard_map/ppermute | solution.py:641
  52.3 15.1 %collective-permute-start.2 = (bf16[8,136,256]{2,1,0:T(8,128)(2,1)}, bf16[8,136,256]{2,1,0:T(8,128)(2,1)}, u32[]{:S(2)}, u32[]{:S(2)}) collective-permute-start(bf16[8,136,256]{2,1,0:T(8,128)(2,1)} %collective-permute-done.1.x2), channel_id=1, source_target_pairs={{0,1},{1,0},{2,3},{3,2},{4,5},{5,4},{6,7},{7,6},{8,9},{9,8},{10,11... | collective-permute-start | bytes 1671176 | tf_op jit(solution)/shard_map/ppermute | solution.py:641
  52.3 7.1 %copy-start.16 = (bf16[8,128,256]{2,1,0:T(8,128)(2,1)}, bf16[8,128,256]{2,1,0:T(8,128)(2,1)S(1)}, u32[]{:S(2)}) copy-start(bf16[8,128,256]{2,1,0:T(8,128)(2,1)S(1)} %all-to-all-done.1.fv_ref) | copy-start | bytes 1572868
  52.3 82.1 %all-to-all-start.3 = ((bf16[8,128,512]{2,1,0:T(8,128)(2,1)}), bf16[8,128,512]{2,1,0:T(8,128)(2,1)}, u32[]{:S(2)}, u32[]{:S(2)}) async-start(bf16[8,128,512]{2,1,0:T(8,128)(2,1)} %get-tuple-element.83), calls=%async_computation.3 | async-start | bytes 2097152 | tf_op jit(solution)/shard_map/all_to_all | solution.py:688
  59.3 29.0 %copy-start.12 = (f32[1024,128]{1,0:T(8,128)}, f32[1024,128]{1,0:T(8,128)S(1)}, u32[]{:S(2)}) copy-start(f32[1024,128]{1,0:T(8,128)S(1)} %copy.73.cos_ref) | copy-start | bytes 1572868
  59.6 28.7 %copy-start.14 = (f32[1024,128]{1,0:T(8,128)}, f32[1024,128]{1,0:T(8,128)S(1)}, u32[]{:S(2)}) copy-start(f32[1024,128]{1,0:T(8,128)S(1)} %copy.74.sin_ref) | copy-start | bytes 1572868
  72.6 37.4 %copy-start.84 = (bf16[1024]{0:T(1024)(128)(2,1)S(1)}, bf16[1024]{0:T(1024)(128)(2,1)}, u32[]{:S(2)}) copy-start(bf16[1024]{0:T(1024)(128)(2,1)} %param.20) | copy-start | bytes 6148
  95.6 14.4 %collective-permute-start.5 = (bf16[1024,256]{1,0:T(8,128)(2,1)}, bf16[1024,256]{1,0:T(8,128)(2,1)}, u32[]{:S(2)}, u32[]{:S(2)}) collective-permute-start(bf16[1024,256]{1,0:T(8,128)(2,1)} %get-tuple-element.74.o0.o_ref.refs_1_), channel_id=1, source_target_pairs={{0,2},{1,3},{2,0},{3,1},{4,6},{5,7},{6,4},{7,5},{8,10},{9,11},{10,... | collective-permute-start | bytes 1572872 | tf_op jit(solution)/shard_map/ppermute | solution.py:641
  97.1 18.2 %collective-permute-start.7 = (bf16[256,1024]{1,0:T(8,128)(2,1)}, bf16[256,1024]{1,0:T(8,128)(2,1)}, u32[]{:S(2)}, u32[]{:S(2)}) collective-permute-start(bf16[256,1024]{1,0:T(8,128)(2,1)} %w0.3), channel_id=1, source_target_pairs={{0,1},{1,0},{2,3},{3,2},{4,5},{5,4},{6,7},{7,6},{8,9},{9,8},{10,11... | collective-permute-start | bytes 1572872 | tf_op jit(solution)/shard_map/ppermute | solution.py:641
  97.1 18.2 %collective-permute-start.9 = (bf16[256,1024]{1,0:T(8,128)(2,1)}, bf16[256,1024]{1,0:T(8,128)(2,1)}, u32[]{:S(2)}, u32[]{:S(2)}) collective-permute-start(bf16[256,1024]{1,0:T(8,128)(2,1)} %collective-permute-done.8.w2), channel_id=1, source_target_pairs={{0,1},{1,0},{2,3},{3,2},{4,5},{5,4},{6,7},{7,6},{8,9},{9,8},{10,11... | collective-permute-start | bytes 1572872 | tf_op jit(solution)/shard_map/ppermute | solution.py:641
  97.7 17.7 %collective-permute-start.4 = (bf16[1024,256]{1,0:T(8,128)(2,1)}, bf16[1024,256]{1,0:T(8,128)(2,1)}, u32[]{:S(2)}, u32[]{:S(2)}) collective-permute-start(bf16[1024,256]{1,0:T(8,128)(2,1)} %get-tuple-element.74.o0.o_ref.refs_1_), channel_id=1, source_target_pairs={{0,1},{1,0},{2,3},{3,2},{4,5},{5,4},{6,7},{7,6},{8,9},{9,8},{10,11... | collective-permute-start | bytes 1572872 | tf_op jit(solution)/shard_map/ppermute | solution.py:641
  110.0 5.3 %collective-permute-start.6 = (bf16[1024,256]{1,0:T(8,128)(2,1)}, bf16[1024,256]{1,0:T(8,128)(2,1)}, u32[]{:S(2)}, u32[]{:S(2)}) collective-permute-start(bf16[1024,256]{1,0:T(8,128)(2,1)} %collective-permute-done.5.o2), channel_id=1, source_target_pairs={{0,1},{1,0},{2,3},{3,2},{4,5},{5,4},{6,7},{7,6},{8,9},{9,8},{10,11... | collective-permute-start | bytes 1572872 | tf_op jit(solution)/shard_map/ppermute | solution.py:641
  133.9 3.9 collective-permute-start.10
  134.4 7.1 %copy-start.9 = (bf16[1024,1024]{1,0:T(8,128)(2,1)S(1)}, bf16[1024,1024]{1,0:T(8,128)(2,1)}, u32[]{:S(2)}) copy-start(bf16[1024,1024]{1,0:T(8,128)(2,1)} %copy-done.8) | copy-start | bytes 6291460
  134.4 7.1 %collective-permute-start.12 = (bf16[8,128,512]{2,1,0:T(8,128)(2,1)}, bf16[8,128,512]{2,1,0:T(8,128)(2,1)S(1)}, u32[]{:S(2)}, u32[]{:S(2)}) collective-permute-start(bf16[8,128,512]{2,1,0:T(8,128)(2,1)} %all-to-all-done.3.a_ref), channel_id=1, source_target_pairs={{0,1},{1,0},{2,3},{3,2},{4,5},{5,4},{6,7},{7,6},{8,9},{9,8},{10,11... | collective-permute-start | bytes 3145736 | tf_op jit(solution)/shard_map/ppermute | solution.py:641
  140.0 7.8 %copy-start.6 = (bf16[1024,704]{1,0:T(8,128)(2,1)S(1)}, bf16[1024,704]{1,0:T(8,128)(2,1)}, u32[]{:S(2)}) copy-start(bf16[1024,704]{1,0:T(8,128)(2,1)} %copy.76.wg_ref) | copy-start | bytes 4325380
  140.0 59.1 %collective-permute-start.11 = (bf16[1024,256]{1,0:T(8,128)(2,1)}, bf16[1024,256]{1,0:T(8,128)(2,1)}, u32[]{:S(2)}, u32[]{:S(2)}) collective-permute-start(bf16[1024,256]{1,0:T(8,128)(2,1)} %fusion.4), channel_id=1, source_target_pairs={{0,2},{1,3},{2,0},{3,1},{4,6},{5,7},{6,4},{7,5},{8,10},{9,11},{10,... | collective-permute-start | bytes 1572872 | tf_op jit(solution)/shard_map/ppermute | solution.py:641
  175.0 10.9 %copy-start.69 = (f32[8,1024]{1,0:T(8,128)}, f32[8,1024]{1,0:T(8,128)S(1)}, u32[]{:S(2)}) copy-start(f32[8,1024]{1,0:T(8,128)S(1)} %get-tuple-element.99) | copy-start | bytes 98308
  191.3 7.8 %copy-start.32 = (f32[1024,256]{1,0:T(8,128)S(1)}, f32[1024,256]{1,0:T(8,128)}, u32[]{:S(2)}) copy-start(f32[1024,256]{1,0:T(8,128)} %copy-done.31) | copy-start | bytes 3145732
  193.7 24.9 %collective-permute-start.28 = (bf16[4,128,704]{1,2,0:T(8,128)(2,1)}, bf16[4,128,704]{1,2,0:T(8,128)(2,1)}, u32[]{:S(2)}, u32[]{:S(2)}) collective-permute-start(bf16[4,128,704]{1,2,0:T(8,128)(2,1)} %copy.82), channel_id=1, source_target_pairs={{0,4},{4,0},{8,12},{12,8},{16,20},{20,16},{24,28},{28,24},{1,5},{5... | collective-permute-start | bytes 2162696 | tf_op jit(solution)/shard_map/ppermute | solution.py:637
  197.7 34.9 %collective-permute-start.31 = (bf16[4,128,704]{1,2,0:T(8,128)(2,1)}, bf16[4,128,704]{1,2,0:T(8,128)(2,1)}, u32[]{:S(2)}, u32[]{:S(2)}) collective-permute-start(bf16[4,128,704]{1,2,0:T(8,128)(2,1)} %copy.84), channel_id=1, source_target_pairs={{0,4},{4,0},{8,12},{12,8},{16,20},{20,16},{24,28},{28,24},{1,5},{5... | collective-permute-start | bytes 2162696 | tf_op jit(solution)/shard_map/ppermute | solution.py:637
  202.2 53.2 %all-to-all-start.2 = ((bf16[8,128,256]{2,1,0:T(8,128)(2,1)}), bf16[8,128,256]{2,1,0:T(8,128)(2,1)S(1)}, u32[]{:S(2)}, u32[]{:S(2)}) async-start(bf16[8,128,256]{2,1,0:T(8,128)(2,1)} %bitcast.13), calls=%async_computation.2 | async-start | bytes 1048576 | tf_op jit(solution)/shard_map/all_to_all | solution.py:688
  208.0 51.1 %collective-permute-start.13 = (bf16[2,1024,256]{2,1,0:T(8,128)(2,1)}, bf16[2,1024,256]{2,1,0:T(8,128)(2,1)}, u32[]{:S(2)}, u32[]{:S(2)}) collective-permute-start(bf16[2,1024,256]{2,1,0:T(8,128)(2,1)} %copy-done.71), channel_id=1, source_target_pairs={{0,1},{1,0},{2,3},{3,2},{4,5},{5,4},{6,7},{7,6},{8,9},{9,8},{10,11... | collective-permute-start | bytes 3145736 | tf_op jit(solution)/shard_map/ppermute | solution.py:641
  210.3 38.4 %collective-permute-start.34 = (bf16[4,128,704]{1,2,0:T(8,128)(2,1)}, bf16[4,128,704]{1,2,0:T(8,128)(2,1)}, u32[]{:S(2)}, u32[]{:S(2)}) collective-permute-start(bf16[4,128,704]{1,2,0:T(8,128)(2,1)} %copy.86), channel_id=1, source_target_pairs={{0,4},{4,0},{8,12},{12,8},{16,20},{20,16},{24,28},{28,24},{1,5},{5... | collective-permute-start | bytes 2162696 | tf_op jit(solution)/shard_map/ppermute | solution.py:637
  217.6 43.3 %collective-permute-start.17 = (bf16[2,1024,256]{2,1,0:T(8,128)(2,1)}, bf16[2,1024,256]{2,1,0:T(8,128)(2,1)}, u32[]{:S(2)}, u32[]{:S(2)}) collective-permute-start(bf16[2,1024,256]{2,1,0:T(8,128)(2,1)} %copy-done.70), channel_id=1, source_target_pairs={{0,1},{1,0},{2,3},{3,2},{4,5},{5,4},{6,7},{7,6},{8,9},{9,8},{10,11... | collective-permute-start | bytes 3145736 | tf_op jit(solution)/shard_map/ppermute | solution.py:641
  223.3 41.4 %collective-permute-start.29 = (bf16[2,128,704]{2,1,0:T(8,128)(2,1)}, bf16[2,128,704]{2,1,0:T(8,128)(2,1)}, u32[]{:S(2)}, u32[]{:S(2)}) collective-permute-start(bf16[2,128,704]{2,1,0:T(8,128)(2,1)} %slice.255), channel_id=1, source_target_pairs={{0,8},{4,12},{8,0},{12,4},{16,24},{20,28},{24,16},{28,20},{1,9},{5... | collective-permute-start | bytes 1081352 | tf_op jit(solution)/shard_map/ppermute | solution.py:637
  235.0 16.0 %copy-start.44 = (bf16[4,128,704]{2,1,0:T(8,128)(2,1)S(1)}, bf16[4,128,704]{2,1,0:T(8,128)(2,1)}, u32[]{:S(2)}) copy-start(bf16[4,128,704]{2,1,0:T(8,128)(2,1)} %copy-done.43) | copy-start | bytes 2162692
  238.5 29.8 %collective-permute-start.32 = (bf16[2,128,704]{2,1,0:T(8,128)(2,1)}, bf16[2,128,704]{2,1,0:T(8,128)(2,1)}, u32[]{:S(2)}, u32[]{:S(2)}) collective-permute-start(bf16[2,128,704]{2,1,0:T(8,128)(2,1)} %slice.254), channel_id=1, source_target_pairs={{0,8},{4,12},{8,0},{12,4},{16,24},{20,28},{24,16},{28,20},{1,9},{5... | collective-permute-start | bytes 1081352 | tf_op jit(solution)/shard_map/ppermute | solution.py:637
  253.7 16.4 %collective-permute-start.35 = (bf16[2,128,704]{2,1,0:T(8,128)(2,1)}, bf16[2,128,704]{2,1,0:T(8,128)(2,1)}, u32[]{:S(2)}, u32[]{:S(2)}) collective-permute-start(bf16[2,128,704]{2,1,0:T(8,128)(2,1)} %slice.253), channel_id=1, source_target_pairs={{0,8},{4,12},{8,0},{12,4},{16,24},{20,28},{24,16},{28,20},{1,9},{5... | collective-permute-start | bytes 1081352 | tf_op jit(solution)/shard_map/ppermute | solution.py:637
  260.3 34.3 %collective-permute-start.14 = (bf16[1024,256]{1,0:T(8,128)(2,1)S(1)}, bf16[1024,256]{1,0:T(8,128)(2,1)S(1)}, u32[]{:S(2)}, u32[]{:S(2)}) collective-permute-start(bf16[1024,256]{1,0:T(8,128)(2,1)S(1)} %fusion.3), channel_id=1, source_target_pairs={{0,2},{1,3},{2,0},{3,1},{4,6},{5,7},{6,4},{7,5},{8,10},{9,11},{10,... | collective-permute-start | bytes 1572872 | tf_op jit(solution)/shard_map/ppermute | solution.py:641
  262.1 6.3 %copy-start.75 = (f32[4,128,704]{2,1,0:T(8,128)S(1)}, f32[4,128,704]{2,1,0:T(8,128)}, u32[]{:S(2)}) copy-start(f32[4,128,704]{2,1,0:T(8,128)} %copy-done.74) | copy-start | bytes 4325380
  262.1 27.9 %collective-permute-start.18 = (bf16[1024,256]{1,0:T(8,128)(2,1)S(1)}, bf16[1024,256]{1,0:T(8,128)(2,1)S(1)}, u32[]{:S(2)}, u32[]{:S(2)}) collective-permute-start(bf16[1024,256]{1,0:T(8,128)(2,1)S(1)} %fusion), channel_id=1, source_target_pairs={{0,2},{1,3},{2,0},{3,1},{4,6},{5,7},{6,4},{7,5},{8,10},{9,11},{10,... | collective-permute-start | bytes 1572872 | tf_op jit(solution)/shard_map/ppermute | solution.py:641
  264.7 5.4 %copy-start.77 = (f32[4,128,704]{2,1,0:T(8,128)S(1)}, f32[4,128,704]{2,1,0:T(8,128)}, u32[]{:S(2)}) copy-start(f32[4,128,704]{2,1,0:T(8,128)} %copy-done.76) | copy-start | bytes 4325380
  265.9 19.0 %collective-permute-start.30 = (bf16[128,704]{1,0:T(8,128)(2,1)S(1)}, bf16[128,704]{1,0:T(8,128)(2,1)S(1)}, u32[]{:S(2)}, u32[]{:S(2)}) collective-permute-start(bf16[128,704]{1,0:T(8,128)(2,1)S(1)} %fusion.11), channel_id=1, source_target_pairs={{0,16},{4,20},{8,24},{12,28},{16,0},{20,4},{24,8},{28,12},{1,17},{... | collective-permute-start | bytes 540680 | tf_op jit(solution)/shard_map/ppermute | solution.py:637
  269.4 19.7 %collective-permute-start.33 = (bf16[128,704]{1,0:T(8,128)(2,1)S(1)}, bf16[128,704]{1,0:T(8,128)(2,1)S(1)}, u32[]{:S(2)}, u32[]{:S(2)}) collective-permute-start(bf16[128,704]{1,0:T(8,128)(2,1)S(1)} %fusion.12), channel_id=1, source_target_pairs={{0,16},{4,20},{8,24},{12,28},{16,0},{20,4},{24,8},{28,12},{1,17},{... | collective-permute-start | bytes 540680 | tf_op jit(solution)/shard_map/ppermute | solution.py:637
  271.2 20.4 %copy-start.30 = (f32[1024,256]{1,0:T(8,128)S(1)}, f32[1024,256]{1,0:T(8,128)}, u32[]{:S(2)}) copy-start(f32[1024,256]{1,0:T(8,128)} %copy-done.29) | copy-start | bytes 3145732
  271.2 49.5 %collective-permute-start.36 = (bf16[128,704]{1,0:T(8,128)(2,1)S(1)}, bf16[128,704]{1,0:T(8,128)(2,1)S(1)}, u32[]{:S(2)}, u32[]{:S(2)}) collective-permute-start(bf16[128,704]{1,0:T(8,128)(2,1)S(1)} %fusion.13), channel_id=1, source_target_pairs={{0,16},{4,20},{8,24},{12,28},{16,0},{20,4},{24,8},{28,12},{1,17},{... | collective-permute-start | bytes 540680 | tf_op jit(solution)/shard_map/ppermute | solution.py:637
  294.0 85.2 %collective-permute-start.22 = (bf16[1024,256]{1,0:T(8,128)(2,1)}, bf16[1024,256]{1,0:T(8,128)(2,1)}, u32[]{:S(2)}, u32[]{:S(2)}) collective-permute-start(bf16[1024,256]{1,0:T(8,128)(2,1)} %get-tuple-element.165), channel_id=1, source_target_pairs={{0,1},{1,0},{2,3},{3,2},{4,5},{5,4},{6,7},{7,6},{8,9},{9,8},{10,11... | collective-permute-start | bytes 1572872 | tf_op jit(solution)/shard_map/ppermute | solution.py:641
  294.1 85.2 %collective-permute-start.23 = (bf16[1024,256]{1,0:T(8,128)(2,1)}, bf16[1024,256]{1,0:T(8,128)(2,1)}, u32[]{:S(2)}, u32[]{:S(2)}) collective-permute-start(bf16[1024,256]{1,0:T(8,128)(2,1)} %get-tuple-element.165), channel_id=1, source_target_pairs={{0,2},{1,3},{2,0},{3,1},{4,6},{5,7},{6,4},{7,5},{8,10},{9,11},{10,... | collective-permute-start | bytes 1572872 | tf_op jit(solution)/shard_map/ppermute | solution.py:641
  294.6 17.5 %copy-start.21 = (bf16[1024,1024]{1,0:T(8,128)(2,1)S(1)}, bf16[1024,1024]{1,0:T(8,128)(2,1)}, u32[]{:S(2)}) copy-start(bf16[1024,1024]{1,0:T(8,128)(2,1)} %copy-done.20) | copy-start | bytes 6291460
  311.9 6.2 %copy-start.53 = (bf16[1024,256]{1,0:T(8,128)(2,1)}, bf16[1024,256]{1,0:T(8,128)(2,1)S(1)}, u32[]{:S(2)}) copy-start(bf16[1024,256]{1,0:T(8,128)(2,1)S(1)} %get-tuple-element.97.refs_0_) | copy-start | bytes 1572868
  311.9 78.5 %collective-permute-start.15 = (bf16[2,1024,256]{2,1,0:T(8,128)(2,1)}, bf16[2,1024,256]{2,1,0:T(8,128)(2,1)}, u32[]{:S(2)}, u32[]{:S(2)}) collective-permute-start(bf16[2,1024,256]{2,1,0:T(8,128)(2,1)} %get-tuple-element.92), channel_id=1, source_target_pairs={{0,1},{1,0},{2,3},{3,2},{4,5},{5,4},{6,7},{7,6},{8,9},{9,8},{10,11... | collective-permute-start | bytes 3145736 | tf_op jit(solution)/shard_map/ppermute | solution.py:641
  319.0 64.2 %collective-permute-start.19 = (bf16[4,128,768]{2,1,0:T(8,128)(2,1)}, bf16[4,128,768]{2,1,0:T(8,128)(2,1)}, u32[]{:S(2)}, u32[]{:S(2)}) collective-permute-start(bf16[4,128,768]{2,1,0:T(8,128)(2,1)} %get-tuple-element.103), channel_id=1, source_target_pairs={{0,4},{4,0},{8,12},{12,8},{16,20},{20,16},{24,28},{28,24},{1,5},{5... | collective-permute-start | bytes 2359304 | tf_op jit(solution)/shard_map/ppermute | solution.py:637
  330.3 55.4 %all-to-all-start.5 = ((bf16[8,128,256]{2,1,0:T(8,128)(2,1)}), bf16[8,128,256]{2,1,0:T(8,128)(2,1)}, u32[]{:S(2)}, u32[]{:S(2)}) async-start(bf16[8,128,256]{2,1,0:T(8,128)(2,1)} %bitcast.93), calls=%async_computation.5 | async-start | bytes 1048576 | tf_op jit(solution)/shard_map/all_to_all | solution.py:688
  379.3 15.8 %collective-permute-start.24 = (bf16[1024,256]{1,0:T(8,128)(2,1)}, bf16[1024,256]{1,0:T(8,128)(2,1)}, u32[]{:S(2)}, u32[]{:S(2)}) collective-permute-start(bf16[1024,256]{1,0:T(8,128)(2,1)} %collective-permute-done.23), channel_id=1, source_target_pairs={{0,1},{1,0},{2,3},{3,2},{4,5},{5,4},{6,7},{7,6},{8,9},{9,8},{10,11... | collective-permute-start | bytes 1572872 | tf_op jit(solution)/shard_map/ppermute | solution.py:641
  385.7 16.4 %collective-permute-start.20 = (bf16[2,128,768]{2,1,0:T(8,128)(2,1)S(1)}, bf16[2,128,768]{2,1,0:T(8,128)(2,1)}, u32[]{:S(2)}, u32[]{:S(2)}) collective-permute-start(bf16[2,128,768]{2,1,0:T(8,128)(2,1)S(1)} %slice.256), channel_id=1, source_target_pairs={{0,8},{4,12},{8,0},{12,4},{16,24},{20,28},{24,16},{28,20},{1,9},{5... | collective-permute-start | bytes 1179656 | tf_op jit(solution)/shard_map/ppermute | solution.py:637
  391.6 23.6 %collective-permute-start.16 = (bf16[1024,256]{1,0:T(8,128)(2,1)S(1)}, bf16[1024,256]{1,0:T(8,128)(2,1)S(1)}, u32[]{:S(2)}, u32[]{:S(2)}) collective-permute-start(bf16[1024,256]{1,0:T(8,128)(2,1)S(1)} %fusion.2), channel_id=1, source_target_pairs={{0,2},{1,3},{2,0},{3,1},{4,6},{5,7},{6,4},{7,5},{8,10},{9,11},{10,... | collective-permute-start | bytes 1572872 | tf_op jit(solution)/shard_map/ppermute | solution.py:641
  395.0 7.0 %copy-start.79 = (f32[4,128,768]{2,1,0:T(8,128)S(1)}, f32[4,128,768]{2,1,0:T(8,128)}, u32[]{:S(2)}) copy-start(f32[4,128,768]{2,1,0:T(8,128)} %copy-done.78) | copy-start | bytes 4718596
  401.2 14.0 %copy-start.38 = (f32[1024,256]{1,0:T(8,128)S(1)}, f32[1024,256]{1,0:T(8,128)}, u32[]{:S(2)}) copy-start(f32[1024,256]{1,0:T(8,128)} %get-tuple-element.91.refs_0_) | copy-start | bytes 3145732
  401.2 8.5 %collective-permute-start.25 = (bf16[4,128,256]{2,1,0:T(8,128)(2,1)S(1)}, bf16[4,128,256]{2,1,0:T(8,128)(2,1)S(1)}, u32[]{:S(2)}, u32[]{:S(2)}) collective-permute-start(bf16[4,128,256]{2,1,0:T(8,128)(2,1)S(1)} %get-tuple-element.105), channel_id=1, source_target_pairs={{0,4},{4,0},{8,12},{12,8},{16,20},{20,16},{24,28},{28,24},{1,5},{5... | collective-permute-start | bytes 786440 | tf_op jit(solution)/shard_map/ppermute | solution.py:637
  403.1 12.0 %collective-permute-start.21 = (bf16[128,768]{1,0:T(8,128)(2,1)S(1)}, bf16[128,768]{1,0:T(8,128)(2,1)S(1)}, u32[]{:S(2)}, u32[]{:S(2)}) collective-permute-start(bf16[128,768]{1,0:T(8,128)(2,1)S(1)} %fusion.10), channel_id=1, source_target_pairs={{0,16},{4,20},{8,24},{12,28},{16,0},{20,4},{24,8},{28,12},{1,17},{... | collective-permute-start | bytes 589832 | tf_op jit(solution)/shard_map/ppermute | solution.py:637
  409.7 6.8 %copy-start.80 = (f32[4,128,256]{2,1,0:T(8,128)}, f32[4,128,256]{2,1,0:T(8,128)S(1)}, u32[]{:S(2)}) copy-start(f32[4,128,256]{2,1,0:T(8,128)S(1)} %convert_add_fusion.9) | copy-start | bytes 1572868
  410.5 10.6 %collective-permute-start.26 = (bf16[2,128,256]{2,1,0:T(8,128)(2,1)}, bf16[2,128,256]{2,1,0:T(8,128)(2,1)}, u32[]{:S(2)}, u32[]{:S(2)}) collective-permute-start(bf16[2,128,256]{2,1,0:T(8,128)(2,1)} %slice.257), channel_id=1, source_target_pairs={{0,8},{4,12},{8,0},{12,4},{16,24},{20,28},{24,16},{28,20},{1,9},{5... | collective-permute-start | bytes 393224 | tf_op jit(solution)/shard_map/ppermute | solution.py:637
  417.4 21.1 %copy-start.4 = (bf16[1024,1024]{1,0:T(8,128)(2,1)S(1)}, bf16[1024,1024]{1,0:T(8,128)(2,1)}, u32[]{:S(2)}) copy-start(bf16[1024,1024]{1,0:T(8,128)(2,1)} %copy-done.1) | copy-start | bytes 6291460
  417.4 21.1 %all-to-all-start.4 = ((bf16[8,128,256]{2,1,0:T(8,128)(2,1)}), bf16[8,128,256]{2,1,0:T(8,128)(2,1)S(1)}, u32[]{:S(2)}, u32[]{:S(2)}) async-start(bf16[8,128,256]{2,1,0:T(8,128)(2,1)} %bitcast.91), calls=%async_computation.4 | async-start | bytes 1048576 | tf_op jit(solution)/shard_map/all_to_all | solution.py:688
  422.1 15.6 %collective-permute-start.27 = (bf16[128,256]{1,0:T(8,128)(2,1)S(1)}, bf16[128,256]{1,0:T(8,128)(2,1)S(1)}, u32[]{:S(2)}, u32[]{:S(2)}) collective-permute-start(bf16[128,256]{1,0:T(8,128)(2,1)S(1)} %fusion.16), channel_id=1, source_target_pairs={{0,16},{4,20},{8,24},{12,28},{16,0},{20,4},{24,8},{28,12},{1,17},{... | collective-permute-start | bytes 196616 | tf_op jit(solution)/shard_map/ppermute | solution.py:637
  (64 other events, 97.6 us)

commit v2 on v0

v2 whole, which is shorter than its diff:
```python
import functools

import jax
import jax.numpy as jnp
from jax import lax
from jax.experimental import pallas as pl
from jax.experimental.pallas import tpu as pltpu
from jax.sharding import PartitionSpec as P

HEAD_DIM = 64
EPS = 1e-06
THETA = 10000.0
NEG = -1e30
BF = jnp.bfloat16
F32 = jnp.float32
BLK = 256
EXTRA = 8
MIB = 1 << 20


def nn(a, b):
    return lax.dot_general(a, b, (((1,), (0,)), ((), ())), preferred_element_type=F32)


def nt(a, b):
    return lax.dot_general(a, b, (((1,), (1,)), ((), ())), preferred_element_type=F32)


def tn(a, b):
    return lax.dot_general(a, b, (((0,), (0,)), ((), ())), preferred_element_type=F32)


def iota(shape, dim):
    return lax.broadcasted_iota(jnp.int32, shape, dim)


TIMES = {
    "pack_tokens": 3,
    "pack_rows": 3,
    "qkv_attention": 14,
    "feed_forward": 12,
    "sort_rows": 3,
    "grads_down": 5,
    "feed_backward": 15,
    "grads_mlp": 8,
    "return_rows": 3,
    "attention_backward": 17,
    "grads_out": 4,
    "grads_qkv": 5,
    "pack_grads": 4,
    "unpack_grads": 4,
    "restore_rows": 3,
}


class Fetched:
    def __init__(self, src, buf, sems, base, parts):
        size = src.shape[0] // parts
        self.buf = buf
        self.copies = [
            pltpu.make_async_copy(
                src.at[pl.ds(p * size, size)], buf.at[pl.ds(p * size, size)], sems.at[base + p]
            )
            for p in range(parts)
        ]
        self.waited = [False] * parts

    def start(self):
        for c in self.copies:
            c.start()

    def __call__(self, part=None):
        for p in range(len(self.copies)) if part is None else (part,):
            if not self.waited[p]:
                self.copies[p].wait()
                self.waited[p] = True
        return self.buf


class Stored:
    def __init__(self, dst, buf, sems, base):
        self.dst, self.buf, self.sems, self.at = dst, buf, sems, base
        self.copies = []

    def flush(self, *index):
        src = self.buf.at[index] if index else self.buf
        dst = self.dst.at[index] if index else self.dst
        c = pltpu.make_async_copy(src, dst, self.sems.at[self.at + len(self.copies)])
        c.start()
        self.copies.append(c)


def call(body, ids, ins, outs, scratch=(), mib=48, name=None):
    took = TIMES[name]
    n_in, n_out = len(ins), len(outs)
    in_at = [sum(p for _, p in ins[:k]) for k in range(n_in + 1)]
    out_at = [sum(p for _, _, p in outs[:k]) for k in range(n_out + 1)]

    def kernel(ids_ref, *refs):
        srcs, refs = refs[:n_in], refs[n_in:]
        dsts, refs = refs[:n_out], refs[n_out:]
        bufs, refs = refs[:n_in], refs[n_in:]
        obufs, refs = refs[:n_out], refs[n_out:]
        in_sems, out_sems, refs = refs[0], refs[1], refs[2:]
        inputs = [
            Fetched(src, buf, in_sems, in_at[k], ins[k][1])
            for k, (src, buf) in enumerate(zip(srcs, bufs))
        ]
        outputs = [
            Stored(dst, buf, out_sems, out_at[k]) for k, (dst, buf) in enumerate(zip(dsts, obufs))
        ]
        for i in inputs:
            i.start()
        body(ids_ref, inputs, outputs, refs)
        for i in inputs:
            i()
        for k, o in enumerate(outputs):
            assert len(o.copies) == outs[k][2]
            for c in o.copies:
                c.wait()

    return pl.pallas_call(
        kernel,
        out_shape=tuple(pltpu.HBM(s, d) for s, d, _ in outs),
        in_specs=[pl.BlockSpec(memory_space=pltpu.SMEM)]
        + [pl.BlockSpec(memory_space=pl.ANY)] * n_in,
        out_specs=tuple(pl.BlockSpec(memory_space=pl.ANY) for _ in outs),
        scratch_shapes=[pltpu.VMEM(a.shape, a.dtype) for a, _ in ins]
        + [pltpu.VMEM(s, d) for s, d, _ in outs]
        + [pltpu.SemaphoreType.DMA((in_at[-1],)), pltpu.SemaphoreType.DMA((out_at[-1],))]
        + list(scratch),
        compiler_params=pltpu.CompilerParams(vmem_limit_bytes=mib * MIB),
        cost_estimate=pl.CostEstimate(
            flops=took * 1_150_000_000, transcendentals=0, bytes_accessed=took * 3_690_000
        ),
        name=name,
    )(ids, *[pltpu.with_memory_space_constraint(a, pltpu.HBM) for a, _ in ins])


def piece(ids_ref, flip, width):
    return pl.ds(pl.multiple_of((ids_ref[0] ^ flip) * width, width), width)


def picks(index, first, size):
    shape = (size, index.shape[1])
    return jnp.where(iota(shape, 0) + first == index, 1.0, 0.0).astype(BF)


def pack_tokens(ids, deal_row, tok, n_dp):
    count, width = tok.shape
    per = count // n_dp
    lanes = 128

    def body(ids_ref, ins, outs, scratch):
        deal_in, tok_in = ins
        out, pos_out = outs
        deal = deal_in()[...]
        dest = deal // count
        slot = deal % count
        oh = jnp.where(iota((n_dp, count), 0) == dest, 1.0, 0.0)
        upto = jnp.where(iota((lanes, lanes), 0) <= iota((lanes, lanes), 1), 1.0, 0.0)
        parts = [oh[:, b * lanes : (b + 1) * lanes] for b in range(count // lanes)]
        inner = nn(jnp.concatenate(parts, axis=0).astype(BF), upto.astype(BF))
        base = (iota((n_dp, 1), 0) * per - 1).astype(F32)
        rows_ = []
        for b, part in enumerate(parts):
            seen = inner[b * n_dp : (b + 1) * n_dp]
            rows_.append(jnp.sum(part * (seen + base), axis=0, keepdims=True))
            base = base + seen[:, lanes - 1 :]
        pos = jnp.concatenate(rows_, axis=1).astype(jnp.int32)
        pos_out.buf[...] = jnp.broadcast_to(pos, (8, count))
        pos_out.flush()
        high = jnp.broadcast_to(slot // 32, (8, count))
        low = jnp.broadcast_to(slot % 32, (8, count))
        hl = jnp.where(iota((8, count), 0) == 0, high, low).astype(F32).astype(BF)
        out.buf[:, per : per + EXTRA, :] = jnp.zeros((n_dp, EXTRA, width), BF)
        size = min(count, 512)
        group = size // per
        for g in range(count // size):
            pick = picks(pos, g * size, size)
            moved = nn(pick, tok_in()[...]).astype(BF)
            marks = nt(hl, pick).astype(BF)
            for e in range(group):
                d = g * group + e
                out.buf[d, 0:per, :] = moved[e * per : (e + 1) * per]
                out.buf[d, per : per + 8, 0:per] = marks[:, e * per : (e + 1) * per]
            out.flush(pl.ds(g * group, group))

    return call(
        body,
        ids,
        [(deal_row, 1), (tok, 1)],
        [
            ((n_dp, per + EXTRA, width), BF, count // min(count, 512)),
            ((8, count), jnp.int32, 1),
        ],
        name="pack_tokens",
    )


def permuted(ids, index, parts, transpose, name):
    count, width = parts[0].shape
    blocks = 2
    size = count // blocks

    def body(ids_ref, ins, outs, scratch):
        idx = ins[0]()[0:1, :]
        total = ins[1]()[...]
        for r in ins[2:]:
            total = total.astype(F32) + r()[...].astype(F32)
        total = total.astype(BF)
        (out,) = outs
        if transpose:
            acc = tn(picks(idx, 0, count), total)
            out.buf[...] = acc.astype(BF)
            out.flush()
        else:
            for b in range(blocks):
                at = slice(b * size, (b + 1) * size)
                out.buf[at, :] = nn(picks(idx, b * size, size), total).astype(BF)
                out.flush(pl.ds(b * size, size))

    return call(
        body,
        ids,
        [(index, 1)] + [(p, 1) for p in parts],
        [((count, width), BF, 1 if transpose else blocks)],
        name=name,
    )[0]


def head_mask(shape, head, split):
    lane = iota(shape, 1)
    if split:
        return (lane % (shape[1] // 2)) // (HEAD_DIM // 2) == head
    return lane // HEAD_DIM == head


def split_perm(width):
    half = HEAD_DIM // 2
    src = iota((width, width), 0)
    dst = iota((width, width), 1)
    second = dst // (width // 2)
    rest = dst % (width // 2)
    want = (rest // half) * HEAD_DIM + second * half + rest % half
    return (src == want).astype(F32).astype(BF)


def qkv_attention(ids, slot_row, pieces, firsts, cos, sin, gain, wq, wk, wv, start_row):
    n_dp, padded, width = pieces[0].shape
    per = firsts.shape[1]
    count = n_dp * per
    dim = gain.shape[1]
    heads = width // HEAD_DIM
    blocks = count // BLK
    half = width // 2

    def body(ids_ref, ins, outs, scratch):
        slot_in, x0, x1, x2, x3, fv_in, wq_in, wk_in, wv_in, cos_in, sin_in, gain_in, start_in = ins
        x_out, n_out, qkv_out, o_out, lse_out, w_out = outs
        cat, vt = scratch
        slots = slot_in()[...]
        for flip, ref in enumerate((x0, x1, x2, x3)):
            cat[:, piece(ids_ref, flip, width)] = ref()[:, 0:per, :].reshape(count, width)
        cat[:, dim:] = fv_in()[...].reshape(count, width)
        sp = split_perm(width)
        w_out.buf[:, 0:width] = nn(wq_in()[...], sp).astype(BF)
        w_out.buf[:, width : 2 * width] = nn(wk_in()[...], sp).astype(BF)
        w_out.buf[:, 2 * width :] = wv_in()[...]
        w_out.flush()
        lse_out.buf[...] = jnp.zeros_like(lse_out.buf)

        def rope(v, c, s):
            a, b = v[:, :half], v[:, half:]
            return jnp.concatenate([a * c - b * s, b * c + a * s], axis=1).astype(BF)

        for j in range(blocks):
            at = slice(j * BLK, (j + 1) * BLK)
            ds = pl.ds(j * BLK, BLK)
            moved = nn(picks(slots, j * BLK, BLK), cat[...])
            x = moved[:, :dim]
            x_out.buf[at, :] = x.astype(BF)
            x_out.flush(ds)
            scale = lax.rsqrt(jnp.sum(x * x, axis=1, keepdims=True) / dim + EPS)
            normed = (x * scale * gain_in()[...]).astype(BF)
            n_out.buf[at, :] = normed
            n_out.flush(ds)
            qkv = nn(normed, w_out.buf[...])
            c, s = cos_in()[at, :], sin_in()[at, :]
            q = rope(qkv[:, 0:width], c, s)
            v = 0.5 * qkv[:, 2 * width :] + 0.5 * moved[:, dim:]
            q = (q.astype(F32) * HEAD_DIM ** (-0.5)).astype(BF)
            qkv_out.buf[at, 0:width] = q
            qkv_out.buf[at, width : 2 * width] = rope(qkv[:, width : 2 * width], c, s)
            qkv_out.buf[at, 2 * width :] = v.astype(BF)
            qkv_out.flush(ds)
            vt[:, at] = jnp.transpose(v).astype(BF)
            start = start_in()[:, at]
            n = (j + 1) * BLK
            keys = qkv_out.buf[0:n, width : 2 * width]
            key = iota((n, BLK), 0)
            valid = (key >= start) & (key <= iota((n, BLK), 1) + j * BLK)
            out = []
            for h in range(heads):
                qh = jnp.where(head_mask((BLK, width), h, True), q, jnp.zeros_like(q))
                sc = jnp.where(valid, nt(keys, qh), NEG)
                top = jnp.max(sc, axis=0, keepdims=True)
                ex = jnp.exp(sc - top)
                total = jnp.sum(ex, axis=0, keepdims=True)
                vals = vt[h * HEAD_DIM : (h + 1) * HEAD_DIM, 0:n]
                out.append(nn(vals, ex.astype(BF)) * (1.0 / total))
                lse_out.buf[h : h + 1, at] = top + jnp.log(total)
            o_out.buf[at, :] = jnp.transpose(jnp.concatenate(out, axis=0)).astype(BF)
            o_out.flush(ds)
        lse_out.flush()

    return call(
        body,
        ids,
        [(slot_row, 1)]
        + [(p, 1) for p in pieces]
        + [(a, 1) for a in (firsts, wq, wk, wv, cos, sin, gain, start_row)],
        [
            ((count, dim), BF, blocks),
            ((count, dim), BF, blocks),
            ((count, 3 * width), BF, blocks),
            ((count, width), BF, blocks),
            ((8, count), F32, 1),
            ((dim, 3 * width), BF, 1),
        ],
        scratch=[pltpu.VMEM((count, dim + width), BF), pltpu.VMEM((width, count), BF)],
        name="qkv_attention",
    )


FEED = 512


def feed_forward(ids, x, o_pieces, w_pieces, gain, w_gate, w_up, w_down):
    count, dim = x.shape
    width = o_pieces[0].shape[1]
    units = w_gate.shape[0]
    size = min(FEED, count)
    blocks = count // size

    def body(ids_ref, ins, outs, scratch):
        w_ins, o_ins = ins[0:4], ins[4:8]
        x_in, gain_in, wg_in, wu_in, wd_in = ins[8:]
        x1_out, n_out, fg_out, fu_out, h_out, yk0, yk2, ysend = outs
        ys, xs, wo = scratch
        for k, w in enumerate(w_ins):
            wo[k * width : (k + 1) * width, :] = w()[...]
        for j in range(blocks):
            at = slice(j * size, (j + 1) * size)
            ds = pl.ds(j * size, size)
            heads = jnp.concatenate([o()[at, :] for o in o_ins], axis=1)
            x1 = x_in(j)[at, :].astype(F32) + nn(heads, wo[...])
            xs[...] = x1
            x1_out.buf[at, :] = x1.astype(BF)
            x1_out.flush(ds)
            scale = lax.rsqrt(jnp.sum(x1 * x1, axis=1, keepdims=True) / dim + EPS)
            normed = (x1 * scale * gain_in()[...]).astype(BF)
            n_out.buf[at, :] = normed
            n_out.flush(ds)
            g = nt(normed, wg_in()[...])
            u = nt(normed, wu_in()[...])
            sg = jax.nn.sigmoid(g)
            silu = g * sg
            hid = (silu * u).astype(BF)
            h_out.buf[at, :] = hid
            h_out.flush(ds)
            fu_out.buf[at, :] = silu.astype(BF)
            fu_out.flush(ds)
            fg_out.buf[at, :] = (u * sg * (1.0 + g * (1.0 - sg))).astype(BF)
            fg_out.flush(ds)
            ys[...] = nn(hid, wd_in()[...])
            ysend.buf[0, at, :] = ys[:, piece(ids_ref, 1, width)].astype(BF)
            ysend.buf[1, at, :] = ys[:, piece(ids_ref, 3, width)].astype(BF)
            ysend.flush(slice(None), ds)
            own = piece(ids_ref, 0, width)
            yk0.buf[at, :] = ys[:, own] + xs[:, own]
            yk0.flush(ds)
            yk2.buf[at, :] = ys[:, piece(ids_ref, 2, width)].astype(BF)
            yk2.flush(ds)

    return call(
        body,
        ids,
        [(w, 1) for w in w_pieces]
        + [(o, 1) for o in o_pieces]
        + [(x, blocks), (gain, 1), (w_gate, 1), (w_up, 1), (w_down, 1)],
        [
            ((count, dim), BF, blocks),
            ((count, dim), BF, blocks),
            ((count, units), BF, blocks),
            ((count, units), BF, blocks),
            ((count, units), BF, blocks),
            ((count, width), F32, blocks),
            ((count, width), BF, blocks),
            ((2, count, width), BF, blocks),
        ],
        scratch=[
            pltpu.VMEM((size, dim), F32),
            pltpu.VMEM((size, dim), F32),
            pltpu.VMEM((4 * width, dim), BF),
        ],
        mib=60,
        name="feed_forward",
    )


def feed_backward(ids, x1, near, far, fg, fu, w_pieces, gain, w_gate, w_up, w_down):
    count, dim = x1.shape
    width = w_pieces[0].shape[0]
    units = w_gate.shape[0]
    size = min(FEED, count)
    blocks = count // size

    def body(ids_ref, ins, outs, scratch):
        wd_in, near_in, far_in, fg_in, fu_in, wg_in, wu_in, x1_in, gain_in = ins[:9]
        w_ins = ins[9:]
        dg_out, du_out, ak0, ak2, asend, dk0, dk2, dsend, gg_out = outs
        ds_, ys, wo = scratch
        sums = jnp.zeros((1, dim), F32)
        for j in range(blocks):
            at = slice(j * size, (j + 1) * size)
            ds = pl.ds(j * size, size)
            near_, far_ = near_in(j)[at, :], far_in(j)[at, :]
            ys[:, piece(ids_ref, 0, width)] = near_[:, :width]
            ys[:, piece(ids_ref, 2, width)] = near_[:, width:]
            ys[:, piece(ids_ref, 1, width)] = far_[:, :width]
            ys[:, piece(ids_ref, 3, width)] = far_[:, width:]
            dy = ys[...]
            dh = nt(dy, wd_in()[...])
            dg = (dh * fg_in(j)[at, :].astype(F32)).astype(BF)
            du = (dh * fu_in(j)[at, :].astype(F32)).astype(BF)
            dg_out.buf[at, :] = dg
            du_out.buf[at, :] = du
            dg_out.flush(ds)
            du_out.flush(ds)
            dn = nn(dg, wg_in()[...]) + nn(du, wu_in()[...])
            x1 = x1_in(j)[at, :].astype(F32)
            scale = lax.rsqrt(jnp.sum(x1 * x1, axis=1, keepdims=True) / dim + EPS)
            sums = sums + jnp.sum(dn * (x1 * scale), axis=0, keepdims=True)
            z = dn * gain_in()[...]
            dot_row = jnp.sum(z * x1, axis=1, keepdims=True)
            part = scale * z - x1 * (scale * scale * scale * dot_row / dim)
            part = part + 0.25 * dy.astype(F32)
            ds_[...] = part
            if j == 0:
                for k, w in enumerate(w_ins):
                    wo[k * width : (k + 1) * width, :] = w()[...]
            da = nt(part.astype(BF), wo[...])
            asend.buf[0, at, :] = da[:, width : 2 * width].astype(BF)
            asend.buf[1, at, :] = da[:, 3 * width :].astype(BF)
            asend.flush(slice(None), ds)
            ak0.buf[at, :] = da[:, 0:width]
            ak0.flush(ds)
            ak2.buf[at, :] = da[:, 2 * width : 3 * width].astype(BF)
            ak2.flush(ds)
            dsend.buf[0, at, :] = ds_[:, piece(ids_ref, 1, width)].astype(BF)
            dsend.buf[1, at, :] = ds_[:, piece(ids_ref, 3, width)].astype(BF)
            dsend.flush(slice(None), ds)
            dk0.buf[at, :] = ds_[:, piece(ids_ref, 0, width)]
            dk0.flush(ds)
            dk2.buf[at, :] = ds_[:, piece(ids_ref, 2, width)].astype(BF)
            dk2.flush(ds)
        gg_out.buf[...] = jnp.broadcast_to(sums, (8, dim))
        gg_out.flush()

    return call(
        body,
        ids,
        [(w_down, 1), (near, blocks), (far, blocks), (fg, blocks), (fu, blocks)]
        + [(w_gate, 1), (w_up, 1), (x1, blocks), (gain, 1)]
        + [(w, 1) for w in w_pieces],
        [
            ((count, units), BF, blocks),
            ((count, units), BF, blocks),
            ((count, width), F32, blocks),
            ((count, width), BF, blocks),
            ((2, count, width), BF, blocks),
            ((count, width), F32, blocks),
            ((count, width), BF, blocks),
            ((2, count, width), BF, blocks),
            ((8, dim), F32, 1),
        ],
        scratch=[
            pltpu.VMEM((size, dim), F32),
            pltpu.VMEM((size, dim), BF),
            pltpu.VMEM((4 * width, dim), BF),
        ],
        mib=60,
        name="feed_backward",
    )


def attention_backward(ids, qkv, o, lse, a_parts, start_row, cos, sin, x, gain, w_qkv, gg2):
    count, width = o.shape
    dim = x.shape[1]
    heads = width // HEAD_DIM
    blocks = count // BLK
    half = width // 2
    part = HEAD_DIM // 2

    def body(ids_ref, ins, outs, scratch):
        qkv_in, a0, a1, a2, o_in, lse_in, start_in, cos_in, sin_in, w_in, x_in, gain_in, g2_in = ins
        dv_out, dqkv_out, ek0, ek2, esend, gg_out = outs
        kt, dk, dv, es = scratch
        qkv_ref = qkv_in()
        for b in range(blocks):
            at = slice(b * BLK, (b + 1) * BLK)
            kt[:, at] = jnp.transpose(qkv_ref[at, width : 2 * width].astype(F32)).astype(BF)
        sums = jnp.zeros((1, dim), F32)
        pick = (iota((8, width), 1) // HEAD_DIM == iota((8, width), 0)).astype(F32)
        sp = split_perm(width)

        def rope_back(g, c, s):
            a, b = g[:, :half], g[:, half:]
            return jnp.concatenate([a * c + b * s, b * c - a * s], axis=1).astype(BF)

        for j in reversed(range(blocks)):
            at = slice(j * BLK, (j + 1) * BLK)
            ds = pl.ds(j * BLK, BLK)
            q = qkv_ref[at, 0:width]
            do = (a0()[at, :] + a1()[at, :].astype(F32) + a2()[at, :].astype(F32)).astype(BF)
            prod = do.astype(F32) * o_in()[at, :].astype(F32)
            delta = lax.dot_general(
                pick, prod, (((1,), (1,)), ((), ())),
                precision=lax.Precision.HIGHEST, preferred_element_type=F32,
            )
            start = start_in()[:, at]
            lse = lse_in()[:, at]
            n = (j + 1) * BLK
            keys = qkv_ref[0:n, width : 2 * width]
            vals = qkv_ref[0:n, 2 * width :]
            key = iota((n, BLK), 0)
            valid = (key >= start) & (key <= iota((n, BLK), 1) + j * BLK)
            probs, grads, q_heads, do_heads = [], [], [], []
            first, second = [], []
            for h in range(heads):
                qh = jnp.where(head_mask((BLK, width), h, True), q, jnp.zeros_like(q))
                dh = jnp.where(head_mask((BLK, width), h, False), do, jnp.zeros_like(do))
                sc = jnp.where(valid, nt(keys, qh) - lse[h : h + 1, :], NEG)
                pr = jnp.exp(sc)
                dsc = (pr * (nt(vals, dh) - delta[h : h + 1, :])).astype(BF)
                probs.append(pr.astype(BF))
                grads.append(dsc)
                q_heads.append(qh)
                do_heads.append(dh)
                kh = jnp.concatenate(
                    [
                        kt[h * part : (h + 1) * part, 0:n],
                        kt[half + h * part : half + (h + 1) * part, 0:n],
                    ],
                    axis=0,
                )
                dqh = nn(kh, dsc)
                first.append(dqh[:part])
                second.append(dqh[part:])
            dvn = nn(jnp.concatenate(probs, 1), jnp.concatenate(do_heads, 0))
            dkn = nn(jnp.concatenate(grads, 1), jnp.concatenate(q_heads, 0))
            if j == blocks - 1:
                dv[...] = dvn
                dk[...] = dkn
            else:
                dv[0:n, :] += dvn
                dk[0:n, :] += dkn
            dqj = jnp.transpose(jnp.concatenate(first + second, axis=0)) * HEAD_DIM ** (-0.5)
            c, s = cos_in()[at, :], sin_in()[at, :]
            dqp = rope_back(dqj, c, s)
            dkp = rope_back(dk[at, :], c, s)
            dvp = (0.5 * dv[at, :].astype(BF).astype(F32)).astype(BF)
            dv_out.buf[at, :] = dvp
            dv_out.flush(ds)
            dqkv_out.buf[at, 0:width] = nt(dqp, sp).astype(BF)
            dqkv_out.buf[at, width : 2 * width] = nt(dkp, sp).astype(BF)
            dqkv_out.buf[at, 2 * width :] = dvp
            dqkv_out.flush(ds)
            dn = nt(jnp.concatenate([dqp, dkp, dvp], axis=1), w_in()[...])
            x = x_in()[at, :].astype(F32)
            scale = lax.rsqrt(jnp.sum(x * x, axis=1, keepdims=True) / dim + EPS)
            sums = sums + jnp.sum(dn * (x * scale), axis=0, keepdims=True)
            z = dn * gain_in()[...]
            dot_row = jnp.sum(z * x, axis=1, keepdims=True)
            es[...] = scale * z - x * (scale * scale * scale * dot_row / dim)
            esend.buf[0, at, :] = es[:, piece(ids_ref, 1, width)].astype(BF)
            esend.buf[1, at, :] = es[:, piece(ids_ref, 3, width)].astype(BF)
            esend.flush(slice(None), ds)
            ek0.buf[at, :] = es[:, piece(ids_ref, 0, width)]
            ek0.flush(ds)
            ek2.buf[at, :] = es[:, piece(ids_ref, 2, width)].astype(BF)
            ek2.flush(ds)
        both = jnp.where(iota((8, dim), 0) == 0, sums, g2_in()[...])
        gg_out.buf[...] = both
        esend.buf[0, count:, :] = gg_out.buf[:, piece(ids_ref, 1, width)].astype(BF)
        esend.buf[1, count:, :] = gg_out.buf[:, piece(ids_ref, 3, width)].astype(BF)
        esend.flush(slice(None), pl.ds(count, EXTRA))
        gg_out.flush()

    return call(
        body,
        ids,
        [(qkv, 1)]
        + [(a, 1) for a in a_parts]
        + [(a, 1) for a in (o, lse, start_row, cos, sin, w_qkv, x, gain, gg2)],
        [
            ((count, width), BF, blocks),
            ((count, 3 * width), BF, blocks),
            ((count, width), F32, blocks),
            ((count, width), BF, blocks),
            ((2, count + EXTRA, width), BF, blocks + 1),
            ((8, dim), F32, 1),
        ],
        scratch=[
            pltpu.VMEM((width, count), BF),
            pltpu.VMEM((count, width), F32),
            pltpu.VMEM((count, width), F32),
            pltpu.VMEM((BLK, dim), F32),
        ],
        mib=56,
        name="attention_backward",
    )


def halves(ids_ref, size):
    y = ids_ref[1] & 1
    keep = pl.ds(pl.multiple_of(y * size, size), size)
    send = pl.ds(pl.multiple_of((1 - y) * size, size), size)
    return keep, send


def weight_grads(ids, pairs, by_rows, name):
    count, dim = pairs[0][0].shape
    chunk = dim // 8
    lefts = []
    for left, _ in pairs:
        if not any(left is x for x in lefts):
            lefts.append(left)
    m = len(lefts)

    def body(ids_ref, ins, outs, scratch):
        (tmp,) = scratch
        z = ids_ref[1] >> 1
        keep, send = halves(ids_ref, chunk)
        for p, (left, right_) in enumerate(pairs):
            k = [left is x for x in lefts].index(True)
            right = ins[m + p]()[...]
            for half in range(2):
                part = ins[k]()[:, half * 4 * chunk : (half + 1) * 4 * chunk]
                full = tn(part, right) if by_rows else tn(right, part)
                for b in range(2):
                    rel = z ^ (2 * half + b)
                    low, high = rel & 1, rel >> 1
                    at = slice(b * 2 * chunk, (b + 1) * 2 * chunk)
                    if by_rows:
                        tmp[...] = full[at, :]
                        outs[2 * p + 1].buf[low, high] = tmp[send, :].astype(BF)
                        outs[2 * p].buf[low, high] = tmp[keep, :].astype(BF)
                    else:
                        tmp[...] = full[:, at]
                        outs[2 * p + 1].buf[low, high] = tmp[:, send].astype(BF)
                        outs[2 * p].buf[low, high] = tmp[:, keep].astype(BF)
            outs[2 * p + 1].flush()
            outs[2 * p].flush()

    outs = []
    for left, right in pairs:
        n = right.shape[1]
        outs += [((2, 2) + ((chunk, n) if by_rows else (n, chunk)), BF, 1)] * 2
    flat = call(
        body,
        ids,
        [(a, 1) for a in lefts] + [(r, 1) for _, r in pairs],
        outs,
        scratch=[pltpu.VMEM((2 * chunk, n) if by_rows else (n, 2 * chunk), F32)],
        name=name,
    )
    return [(flat[2 * p], flat[2 * p + 1]) for p in range(len(pairs))]


def down_grads(ids, hidden, near, far):
    count, units = hidden.shape
    two = near.shape[1]
    width = two // 2
    chunk = width // 2

    def body(ids_ref, ins, outs, scratch):
        h_in, a_in, b_in = ins
        keep_out, send_out = outs
        (tmp,) = scratch
        keep, send = halves(ids_ref, chunk)
        for low, ref in ((0, a_in), (1, b_in)):
            full = tn(h_in()[...], ref()[...])
            for high in range(2):
                tmp[...] = full[:, high * width : (high + 1) * width]
                rel = ids_ref[0] ^ (ids_ref[1] >> 1) ^ (low + 2 * high)
                send_out.buf[rel & 1, rel >> 1] = tmp[:, send].astype(BF)
                keep_out.buf[rel & 1, rel >> 1] = tmp[:, keep].astype(BF)
        send_out.flush()
        keep_out.flush()

    shape = (2, 2, units, chunk)
    return call(
        body,
        ids,
        [(hidden, 1), (near, 1), (far, 1)],
        [(shape, BF, 1)] * 2,
        scratch=[pltpu.VMEM((units, width), F32)],
        name="grads_down",
    )


def out_grads(ids, o_pieces, parts):
    count, width = o_pieces[0].shape
    half = width // 2

    def body(ids_ref, ins, outs, scratch):
        keep_out, send_out = outs
        (tmp,) = scratch
        keep, send = halves(ids_ref, half)
        total = ins[0]()[...]
        for p in ins[1:3]:
            total = total + p()[...].astype(F32)
        grad = total.astype(BF)
        for flip, o in enumerate(ins[3:]):
            tmp[...] = tn(o()[...], grad)
            rel = (ids_ref[1] >> 1) ^ flip
            send_out.buf[rel & 1, rel >> 1] = tmp[:, send].astype(BF)
            keep_out.buf[rel & 1, rel >> 1] = tmp[:, keep].astype(BF)
        send_out.flush()
        keep_out.flush()

    shape = (2, 2, width, half)
    return call(
        body,
        ids,
        [(p, 1) for p in parts] + [(o, 1) for o in o_pieces],
        [(shape, BF, 1)] * 2,
        scratch=[pltpu.VMEM((width, width), F32)],
        name="grads_out",
    )


def flip_dp(value, bit):
    n = lax.axis_size("dp")
    return lax.ppermute(value, "dp", [(d, d ^ bit) for d in range(n)])


def flip_tensor(value, bit):
    return lax.ppermute(value, "tensor", [(d, d ^ bit) for d in range(4)])


def tie(values, *others):
    return lax.optimization_barrier((values, others))[0]


def halve_sum(keep, got, first, second, third):
    total = keep.astype(F32) + tie(got, first).astype(F32)
    total = total[0] + tie(flip_dp(total[1].astype(BF), 2), second).astype(F32)
    return total[0] + tie(flip_dp(total[1].astype(BF), 4), third).astype(F32)


def gather_pieces(own):
    two = flip_tensor(own, 2)
    one = flip_tensor(own, 1)
    three = flip_tensor(two, 1)
    return (own, one, two, three)


def middle(keep2, got):
    return (keep2.astype(F32) + got[1].astype(F32)).astype(BF)


def pack_grads(ids, slot_row, parts, other, gains, n_dp):
    count, width = other.shape
    per = count // n_dp
    k = len(parts)

    def body(ids_ref, ins, outs, scratch):
        (out,) = outs
        gain = ins[k + 2]()[...].astype(F32)
        for r in ins[k + 3 :]:
            gain = gain + r()[...].astype(F32)
        gain = jnp.concatenate([gain.astype(BF)] * 2, axis=1)
        total = ins[1]()[0:count, :].astype(F32)
        for r in ins[2 : k + 1]:
            total = total + r()[0:count, :].astype(F32)
        both = jnp.concatenate([total.astype(BF), ins[k + 1]()[...]], axis=1)
        moved = tn(picks(ins[0]()[...], 0, count), both).astype(BF)
        for d in range(n_dp):
            out.buf[d, 0:per, :] = moved[d * per : (d + 1) * per, :]
            out.buf[d, per:, :] = gain
        out.flush()

    return call(
        body,
        ids,
        [(slot_row, 1)] + [(p, 1) for p in (*parts, other, *gains)],
        [((n_dp, per + EXTRA, 2 * width), BF, 1)],
        name="pack_grads",
    )[0]


def unpack_grads(ids, pos8, back):
    n_dp, padded, two = back.shape
    width = two // 2
    per = padded - EXTRA
    count = n_dp * per

    def body(ids_ref, ins, outs, scratch):
        a_out, b_out, gain_out = outs
        pos_in, back_in = ins
        picked = picks(pos_in()[0:1, :], 0, count)
        ref = back_in()
        moved = tn(picked, ref[:, 0:per, :].reshape(count, two)).astype(BF)
        a_out.buf[...] = moved[:, :width]
        a_out.flush()
        b_out.buf[...] = moved[:, width:]
        b_out.flush()
        total = ref[0, per:, 0:width].astype(F32)
        for d in range(1, n_dp):
            total = total + ref[d, per:, 0:width].astype(F32)
        gain_out.buf[...] = total
        gain_out.flush()

    return call(
        body,
        ids,
        [(pos8, 1), (back, 1)],
        [((count, width), BF, 1), ((count, width), BF, 1), ((EXTRA, width), F32, 1)],
        name="unpack_grads",
    )


def per_device(
    tokens,
    dealing,
    seq_ids,
    first_values,
    out_grad,
    norm1_gain,
    norm2_gain,
    w_query,
    w_key,
    w_value,
    w_out,
    w_gate,
    w_up,
    w_down,
):
    n_dp = lax.axis_size("dp")
    count, width = tokens.shape
    dim = norm1_gain.shape[0]
    per = count // n_dp
    t = lax.axis_index("tensor")
    d = lax.axis_index("dp")
    ids = jnp.stack([t, d]).astype(jnp.int32)
    gate_t, up_t = w_gate.T, w_up.T

    def exchange(packed):
        return lax.all_to_all(packed, "dp", split_axis=0, concat_axis=0, tiled=True)

    deal_row = dealing.reshape(1, count)
    sent, pos8 = pack_tokens(ids, deal_row, tokens, n_dp)
    arrived = exchange(sent)
    grad_far = flip_tensor(tie(out_grad, sent), 2)
    pos8 = tie(pos8, sent)
    first_sent = permuted(ids, pos8, [first_values], False, "pack_rows")
    first_sent = first_sent.reshape(n_dp, per, width)

    start = jnp.sum(seq_ids[None, :] < seq_ids[:, None], axis=1, dtype=jnp.int32)
    offset = (jnp.arange(count, dtype=jnp.int32) - start).astype(F32)
    half = HEAD_DIM // 2
    freqs = THETA ** (-jnp.arange(half, dtype=F32) / half)
    angles = offset[:, None] * freqs[None, :]
    reps = (1, width // HEAD_DIM)
    cos = jnp.tile(jnp.cos(angles), reps)
    sin = jnp.tile(jnp.sin(angles), reps)
    start_row = start.reshape(1, count)
    gain1 = norm1_gain.astype(F32).reshape(1, dim)
    gain2 = norm2_gain.astype(F32).reshape(1, dim)

    arrived = tie(arrived, first_sent, cos, sin, start_row, grad_far)
    pieces = gather_pieces(arrived)
    first_sent = tie(first_sent, pieces[1])
    firsts = exchange(first_sent)
    slots = (
        arrived[:, per, :per].astype(F32) * 32.0 + arrived[:, per + 1, :per].astype(F32)
    ).astype(jnp.int32)
    slot_row = slots.reshape(1, count)
    grad_near = tie(out_grad, slot_row)
    grad_sent = permuted(
        ids, pos8, [jnp.concatenate([grad_near, grad_far], axis=1)], False, "pack_rows"
    ).reshape(n_dp, per, 2 * width)
    near = exchange(tie(grad_sent, firsts))
    w_pieces = gather_pieces(tie(w_out, pieces[3]))

    x, normed1, qkv, attended, lse, w_qkv = qkv_attention(
        ids, tie(slot_row, grad_sent), pieces, firsts, cos, sin, gain1, w_query, w_key, w_value,
        start_row,
    )
    o_pieces = gather_pieces(attended)
    near = tie(near, attended).reshape(count, 2 * width)
    near = permuted(ids, slot_row, [near], False, "sort_rows")
    far = flip_tensor(near, 1)
    x1, normed2, fg, fu, hidden, yk0, yk2, ysend = feed_forward(
        ids, tie(x, near), o_pieces, w_pieces, gain2, gate_t, up_t, w_down
    )
    fast = n_dp == 8
    y_got = flip_tensor(ysend, 1)
    y_mid = middle(yk2, y_got)
    y_far = flip_tensor(y_mid, 2)
    x1 = tie(x1, y_mid)
    if fast:
        down_keep, down_send = down_grads(ids, hidden, near, far)
        down_got = flip_dp(down_send, 1)
        x1 = tie(x1, down_keep)
    dgate, dup, ak0, ak2, asend, dk0, dk2, dsend, gg2 = feed_backward(
        ids, x1, near, far, fg, fu, w_pieces, gain2, gate_t, up_t, w_down
    )
    asend = tie(asend, y_far)
    if fast:
        asend = tie(asend, down_got)
    a_got = flip_tensor(asend, 1)
    a_mid = middle(ak2, a_got)
    a_far = flip_tensor(a_mid, 2)
    d_got = flip_tensor(tie(dsend, a_mid), 1)

    def send_back(parts, name):
        packed = permuted(ids, slot_row, parts, True, name).reshape(n_dp, per, width)
        return exchange(packed).reshape(count, width)

    y_back = send_back([tie(yk0, a_mid), y_got[0], y_far], "return_rows")
    d_mid = middle(dk2, d_got)
    if fast:
        gup = tie((dgate, dup), a_mid)
        (gate_keep, gate_send), (up_keep, up_send) = weight_grads(
            ids, [(normed2, gup[0]), (normed2, gup[1])], False, "grads_mlp"
        )
        a_far = tie(a_far, gate_keep)
        gate_got = flip_dp(gate_send, 1)
    d_far = flip_tensor(tie(d_mid, a_far), 2)
    dvp, dqkv, ek0, ek2, esend, gg1 = attention_backward(
        ids, qkv, attended, lse, (ak0, a_got[0], tie(a_far, d_mid)), start_row, cos, sin, x,
        gain1, w_qkv, gg2,
    )
    if fast:
        esend = tie(esend, gate_got)
    e_got = flip_tensor(esend, 1)
    gains = [
        lax.dynamic_slice(gg1, (0, (t ^ flip) * width), (EXTRA, width)) for flip in (0, 2)
    ]
    e_mid = jnp.concatenate(
        [
            (ek2.astype(F32) + e_got[1, :count].astype(F32)).astype(BF),
            (gains[1] + e_got[1, count:].astype(F32)).astype(BF),
        ],
        axis=0,
    )
    e_far = flip_tensor(e_mid, 2)
    d_parts = (dk0, d_got[0], d_far)
    if fast:
        up_got = flip_dp(tie(up_send, gate_got), 1)
        ((att_keep, att_send),) = weight_grads(
            ids, [(normed1, tie(dqkv, e_mid))], True, "grads_qkv"
        )
        out_keep, out_send = out_grads(ids, o_pieces, (tie(dk0, e_mid), d_got[0], d_far))
        e_far = tie(e_far, att_keep, out_keep)
    i_sent = pack_grads(
        ids,
        slot_row,
        [ek0, e_got[0], e_far, *d_parts],
        dvp,
        [gains[0], e_got[0, count:], e_far[count:]],
        n_dp,
    )
    i_back = exchange(i_sent)

    if fast:
        att_got = flip_dp(tie(att_send, up_got), 1)
        out_got = flip_dp(out_send, 1)
        gw_down = halve_sum(down_keep, down_got, e_mid, e_mid, e_far)
        gw_gate = halve_sum(gate_keep, gate_got, att_keep, i_sent, i_sent).T
        gw_up = halve_sum(up_keep, up_got, i_sent, i_sent, i_sent).T
        gw_qkv = halve_sum(att_keep, att_got, i_sent, i_sent, i_sent)
        gw_q, gw_k, gw_v = jnp.split(gw_qkv, 3, axis=1)
        gw_out = halve_sum(out_keep, out_got, i_sent, i_sent, i_sent)
        gw_out = lax.ppermute(
            gw_out,
            ("dp", "tensor"),
            [
                ((2 * z + y) * 4 + r, (2 * r + y) * 4 + (r ^ z))
                for z in range(4)
                for y in range(2)
                for r in range(4)
            ],
        )
    else:

        def scattered(left, right, dim_):
            full = jnp.einsum("ta,tb->ab", left, right, preferred_element_type=F32)
            return lax.psum_scatter(full, "dp", scatter_dimension=dim_, tiled=True)

        def natural(parts):
            full = jnp.zeros((count, dim), BF)
            for flip, part in enumerate(parts):
                full = lax.dynamic_update_slice(full, part, (0, (t ^ flip) * width))
            return full

        dy = natural((near[:, :width], far[:, :width], near[:, width:], far[:, width:]))
        dx1 = (dk0 + d_got[0].astype(F32) + d_far.astype(F32)).astype(BF)
        dx1 = lax.all_gather(dx1, "tensor", axis=1, tiled=True)
        gw_gate = scattered(normed2, dgate, 0)
        gw_up = scattered(normed2, dup, 0)
        gw_down = scattered(hidden, dy, 1)
        gw_q, gw_k, gw_v = [scattered(normed1, p, 0) for p in jnp.split(dqkv, 3, axis=1)]
        gw_out = scattered(attended, dx1, 1)

    output = permuted(ids, pos8, [tie(y_back, i_sent)], True, "restore_rows")
    input_grad, first_grad, gain_rows = unpack_grads(ids, pos8, i_back)
    part = width // n_dp
    mine = lax.dynamic_slice(gain_rows, (0, d * part), (2, part))
    return (
        output,
        input_grad,
        first_grad,
        mine[0:1],
        mine[1:2],
        gw_q,
        gw_k,
        gw_v,
        gw_out,
        gw_gate,
        gw_up,
        gw_down,
    )


def solution(mesh):
    in_specs = (
        P("dp", "tensor"),
        P("dp"),
        P("dp"),
        P("dp", "tensor"),
        P("dp", "tensor"),
        P(),
        P(),
        P(None, "tensor"),
        P(None, "tensor"),
        P(None, "tensor"),
        P("tensor", None),
        P(None, "tensor"),
        P(None, "tensor"),
        P("tensor", None),
    )
    out_specs = (
        P("dp", "tensor"),
        P("dp", "tensor"),
        P("dp", "tensor"),
        P("tensor", "dp"),
        P("tensor", "dp"),
        P("dp", "tensor"),
        P("dp", "tensor"),
        P("dp", "tensor"),
        P("tensor", "dp"),
        P("dp", "tensor"),
        P("dp", "tensor"),
        P("tensor", "dp"),
    )
    return jax.shard_map(
        per_device, mesh=mesh, in_specs=in_specs, out_specs=out_specs, check_vma=False
    )
```

time: 1120 us -> 328 us (0.29)
  waiting for transfers between devices: 756 us -> 102 us
  Pallas kernels: 0 us -> 127 us
  matrix products: 102 us -> 0 us
  local copies, waits for them, and re-layouts: 114 us -> 16.5 us
  blocking collectives: 43.2 us -> 0 us
  other arithmetic: 50.5 us -> 14.3 us
  starting transfers between devices: 30.7 us -> 60.9 us
  between operations: 15 us -> 1.51 us
    reduce_scatter x11 -> x0, waiting for transfers between devices: 652 us -> none  [the longest x2 83 us: input_sum(): return lax.psum_scatter(term, 'tensor', scatter_dimension=1, tiled=True)]
    pallas_call x0 -> x16, Pallas kernels: none -> 127 us  [call(): pl.pallas_call(kernel, out_shape=tuple((pltpu.HBM(s, d) for s, d, _ in ou...]
    dot_general x35 -> x0, matrix products: 102 us -> none  [the longest x2 8.8 us: one_back(): jnp.einsum('qhd,khd->hqk', grad_block, values, preferred_element_type=jnp...]
    ppermute x0 -> x35, waiting for transfers between devices: none -> 101 us  [the longest x15 64 us: flip_dp(): return lax.ppermute(value, 'dp', [(d, d ^ bit) for d in range(n)])]
    gather x14 -> x0, local copies, waits for them, and re-layouts: 68.1 us -> none  [the longest x1 8.84 us: per_device(): dealing[order]]
    unnamed x19 -> x0, waiting for transfers between devices: 40 us -> none
    ppermute x0 -> x35, starting transfers between devices: none -> 35.8 us  [the longest x15 24.1 us: flip_dp(): return lax.ppermute(value, 'dp', [(d, d ^ bit) for d in range(n)])]
    all_gather x4 -> x0, waiting for transfers between devices: 34.5 us -> none  [the longest x2 34.5 us: gather_grad(): return lax.all_gather(grads, 'tensor', axis=1, tiled=True)]
  transfers between devices with their start and end apart: 23 -> 40, of which waited for: 19 -> 18; matrix products, arithmetic and copies ran while one was open for 11% -> 6% of each run, Pallas kernels for 0% -> 32%
where the time goes in v2:
time: 328 us; the launch traced here: 323 us
  Pallas kernels  127 us (39%)
  waiting for transfers between devices  102 us (31%)
  starting transfers between devices  60.9 us (19%)
  local copies, waits for them, and re-layouts  16.5 us (5%)
  other arithmetic  14.3 us (4%)
    pallas_call x16, Pallas kernels, call(): pl.pallas_call(kernel, out_shape=tuple((pltpu.HBM(s, d) for s, d, _ in ou...  127 us
    ppermute x15, waiting for transfers between devices, flip_dp(): return lax.ppermute(value, 'dp', [(d, d ^ bit) for d in range(n)])  64 us
    ppermute x19, waiting for transfers between devices, flip_tensor(): return lax.ppermute(value, 'tensor', [(d, d ^ bit) for d in range(4)])  36.6 us
    all_to_all x5, starting transfers between devices, exchange(): return lax.all_to_all(packed, 'dp', split_axis=0, concat_axis=0, tiled=True)  25.1 us
    ppermute x15, starting transfers between devices, flip_dp(): return lax.ppermute(value, 'dp', [(d, d ^ bit) for d in range(n)])  24.1 us
    ppermute x19, starting transfers between devices, flip_tensor(): return lax.ppermute(value, 'tensor', [(d, d ^ bit) for d in range(4)])  11.1 us
    unnamed x71, local copies, waits for them, and re-layouts  7.54 us
  transfers between devices with their start and end apart: 40, of which 18 were waited for; matrix products, arithmetic and copies ran while one was open for 6% of the time, Pallas kernels for 32%

profile of v2, /device:TPU:0, one launch (start us, length us, event | category | flops | bytes accessed | tf_op | source)
XLA Modules:
  0.0 322.6 jit_solution(16102976417629470306)
XLA Ops:
  0.7 3.7 %pack_tokens.1 = (bf16[8,136,256]{2,1,0:T(8,128)(2,1)}, s32[8,1024]{1,0:T(8,128)}) custom-call(s32[2]{0:T(128)S(1)} %pad_add_fusion.ids_ref, s32[1,1024]{1,0:T(1,128)} %bitcast.136, bf16[1024,256]{1,0:T(8,128)(2,1)} %refs_1_.2), custom_call_target="tpu_custom_call" | custom-call | flops 3449999872 | bytes 11070000 | tf_op jit(solution)/shard_map/pack_tokens/pallas_call | solution.py:122
  4.4 7.3 %all-to-all-start = ((bf16[8,136,256]{2,1,0:T(8,128)(2,1)}), bf16[8,136,256]{2,1,0:T(8,128)(2,1)S(1)}, u32[]{:S(2)}, u32[]{:S(2)}) async-start(bf16[8,136,256]{2,1,0:T(8,128)(2,1)} %get-tuple-element.100), calls=%async_computation | async-start | bytes 1114112 | tf_op jit(solution)/shard_map/all_to_all | solution.py:862
  11.7 1.6 collective-permute-start
  14.4 3.1 pack_rows.2
  17.6 7.6 %collective-permute-done = bf16[1024,256]{1,0:T(8,128)(2,1)S(1)} collective-permute-done((bf16[1024,256]{1,0:T(8,128)(2,1)S(1)}, bf16[1024,256]{1,0:T(8,128)(2,1)S(1)}, u32[]{:S(2)}, u32[]{:S(2)}) %collective-permute-start) | collective-permute-done | bytes 524320 | tf_op jit(solution)/shard_map/ppermute | solution.py:751
  25.2 1.7 all-to-all-done.refs_1_
  27.1 1.6 collective-permute-start.1
  29.2 3.9 %all-to-all-start.1 = ((bf16[8,128,256]{2,1,0:T(8,128)(2,1)}), bf16[8,128,256]{2,1,0:T(8,128)(2,1)S(1)}, u32[]{:S(2)}, u32[]{:S(2)}) async-start(bf16[8,128,256]{2,1,0:T(8,128)(2,1)} %bitcast.125), calls=%async_computation.1 | async-start | bytes 1048576 | tf_op jit(solution)/shard_map/all_to_all | solution.py:862
  33.1 1.0 copy.31.refs_10_.refs_8_
  34.1 1.0 copy.30.refs_9_.refs_7_
  35.7 6.6 %collective-permute-done.1.refs_3_ = bf16[8,136,256]{2,1,0:T(8,128)(2,1)} collective-permute-done((bf16[8,136,256]{2,1,0:T(8,128)(2,1)S(1)}, bf16[8,136,256]{2,1,0:T(8,128)(2,1)}, u32[]{:S(2)}, u32[]{:S(2)}) %collective-permute-start.1) | collective-permute-done | bytes 557088 | tf_op jit(solution)/shard_map/ppermute | solution.py:751
  42.9 1.0 pad_maximum_fusion.refs_1_
  43.9 3.9 %pack_rows.3 = bf16[1024,512]{1,0:T(8,128)(2,1)} custom-call(s32[2]{0:T(128)S(1)} %pad_add_fusion.ids_ref, s32[8,1024]{1,0:T(8,128)} %get-tuple-element.101.refs_0_, bf16[1024,512]{1,0:T(8,128)(2,1)} %pad_maximum_fusion.refs_1_), custom_call_target="tpu_custom_call" | custom-call | flops 3449999872 | bytes 11070000 | tf_op jit(solution)/shard_map/pack_rows/pallas_call | solution.py:122
  47.8 1.6 collective-permute-start.4
  49.4 4.2 %all-to-all-start.2 = ((bf16[8,128,512]{2,1,0:T(8,128)(2,1)}), bf16[8,128,512]{2,1,0:T(8,128)(2,1)S(1)}, u32[]{:S(2)}, u32[]{:S(2)}) async-start(bf16[8,128,512]{2,1,0:T(8,128)(2,1)} %bitcast.122), calls=%async_computation.2 | async-start | bytes 2097152 | tf_op jit(solution)/shard_map/all_to_all | solution.py:862
  53.6 16.1 %qkv_attention.1 = (bf16[1024,1024]{1,0:T(8,128)(2,1)}, bf16[1024,1024]{1,0:T(8,128)(2,1)}, bf16[1024,768]{1,0:T(8,128)(2,1)}, bf16[1024,256]{1,0:T(8,128)(2,1)}...) custom-call(s32[2]{0:T(128)S(1)} %pad_add_fusion.ids_ref, s32[1,1024]{1,0:T(1,128)} %convert_bitcast_fusion.refs_0_, ...), custom_call_target="tpu_custom_call" | custom-call | flops 16099999744 | bytes 51660000 | tf_op jit(solution)/shard_map/qkv_attention/pallas_call | solution.py:122
  71.1 12.7 %collective-permute-done.8.refs_6_.refs_5_ = bf16[1024,256]{1,0:T(8,128)(2,1)S(1)} collective-permute-done((bf16[1024,256]{1,0:T(8,128)(2,1)}, bf16[1024,256]{1,0:T(8,128)(2,1)S(1)}, u32[]{:S(2)}, u32[]{:S(2)}) %collective-permute-start.8) | collective-permute-done | bytes 524320 | tf_op jit(solution)/shard_map/ppermute | solution.py:751
  84.4 1.0 copy-done.5
  85.4 4.4 %sort_rows.1.refs_1_ = bf16[1024,512]{1,0:T(8,128)(2,1)} custom-call(s32[2]{0:T(128)S(1)} %pad_add_fusion.ids_ref, s32[1,1024]{1,0:T(1,128)} %convert_bitcast_fusion.refs_0_, bf16[1024,512]{1,0:T(8,128)(2,1)} %bitcast.123), custom_call_target="tpu_custom_call" | custom-call | flops 3449999872 | bytes 11070000 | tf_op jit(solution)/shard_map/sort_rows/pallas_call | solution.py:122
  90.8 14.4 %feed_forward.1 = (bf16[1024,1024]{1,0:T(8,128)(2,1)}, bf16[1024,1024]{1,0:T(8,128)(2,1)}, bf16[1024,704]{1,0:T(8,128)(2,1)}, bf16[1024,704]{1,0:T(8,128)(2,1)},...) custom-call(s32[2]{0:T(128)} %copy-done, ...), custom_call_target="tpu_custom_call" | custom-call | flops 13799999488 | bytes 44280000 | tf_op jit(solution)/shard_map/feed_forward/pallas_call | solution.py:122
  105.9 3.0 collective-permute-done.11
  108.9 1.2 fusion.3
  110.1 1.1 collective-permute-start.12
  111.2 1.0 copy-done.27
  112.2 5.8 %grads_down.1 = (bf16[2,2,704,128]{3,2,1,0:T(8,128)(2,1)}, bf16[2,2,704,128]{3,2,1,0:T(8,128)(2,1)}) custom-call(s32[2]{0:T(128)S(1)} %copy-done.1, bf16[1024,704]{1,0:T(8,128)(2,1)} %get-tuple-element.120.refs_0_, bf16[1024,512]{1,0:T(8,128)(2,1)} %sort_rows.1.refs_1_, bf16[1024,512]{1,0:T(8,128)(2,1)} %copy-done.27), custom_call_target="tpu_custom_call" | custom-call | flops 5750000128 | bytes 18450000 | tf_op jit(solution)/shard_map/grads_down/pallas_call | solution.py:122
  118.0 1.8 collective-permute-start.13
  119.8 19.0 %feed_backward.1 = (bf16[1024,704]{1,0:T(8,128)(2,1)}, bf16[1024,704]{1,0:T(8,128)(2,1)}, f32[1024,256]{1,0:T(8,128)}, bf16[1024,256]{1,0:T(8,128)(2,1)}, bf16[2...) custom-call(s32[2]{0:T(128)} %copy-done, ...), custom_call_target="tpu_custom_call" | custom-call | flops 17250000896 | bytes 55350000 | tf_op jit(solution)/shard_map/feed_backward/pallas_call | solution.py:122
  138.9 2.9 collective-permute-done.14
  141.8 1.2 fusion.2
  143.0 1.0 collective-permute-start.15
  144.0 8.5 %grads_mlp.1 = (bf16[2,2,704,128]{3,2,1,0:T(8,128)(2,1)}, bf16[2,2,704,128]{3,2,1,0:T(8,128)(2,1)}, bf16[2,2,704,128]{3,2,1,0:T(8,128)(2,1)}, bf16[2,2,704,128]{3,2,1,0:T(8,128)(2,1)}) custom-call(s32[2]{0:T(128)S(1)} %copy-done.2, bf16[1024,1024]{1,0:T(8,128)(2,1)} %get-tuple-element.131.refs_0_, bf16[1024,704]{1,0:T(8,128)(2,1)} %get-tuple-element.134.refs_1_, ...), custom_call_target="tpu_custom_call" | custom-call | flops 9200000000 | bytes 29520000 | tf_op jit(solution)/shard_map/grads_mlp/pallas_call | solution.py:122
  153.7 3.3 %collective-permute-done.15.refs_3_ = bf16[1024,256]{1,0:T(8,128)(2,1)S(1)} collective-permute-done((bf16[1024,256]{1,0:T(8,128)(2,1)S(1)}, bf16[1024,256]{1,0:T(8,128)(2,1)S(1)}, u32[]{:S(2)}, u32[]{:S(2)}) %collective-permute-start.15) | collective-permute-done | bytes 524320 | tf_op jit(solution)/shard_map/ppermute | solution.py:751
  157.0 1.0 fusion.1
  158.0 19.7 %attention_backward.1 = (bf16[1024,256]{1,0:T(8,128)(2,1)}, bf16[1024,768]{1,0:T(8,128)(2,1)}, f32[1024,256]{1,0:T(8,128)}, bf16[1024,256]{1,0:T(8,128)(2,1)}, b...) custom-call(s32[2]{0:T(128)} %copy-done, bf16[1024,768]{1,0:T(8,128)(2,1)} %get-tuple-element.129.refs_0_, ...), custom_call_target="tpu_custom_call" | custom-call | flops 19549999104 | bytes 62730000 | tf_op jit(solution)/shard_map/attention_backward/pallas_call | solution.py:122
  179.5 3.7 %return_rows.1 = bf16[1024,256]{1,0:T(8,128)(2,1)} custom-call(s32[2]{0:T(128)S(1)} %copy-done.3, s32[1,1024]{1,0:T(1,128)} %convert_bitcast_fusion.refs_0_, f32[1024,256]{1,0:T(8,128)} %get-tuple-element.128.refs_1_, bf16[1024,256]{1,0:T(8,128)(2,1)} %slice_bitcast_fusion.9.refs_2_, bf16[1024,256]{1,0:T(8,128)(2,1)} %collective-permute-done.12.refs_3_), custom_call_target="tpu_custom_call" | custom-call | flops 3449999872 | bytes 11070000 | tf_op jit(solution)/shard_map/return_rows/pallas_call | solution.py:122
  183.2 4.6 %all-to-all-start.3 = ((bf16[8,128,256]{2,1,0:T(8,128)(2,1)}), bf16[8,128,256]{2,1,0:T(8,128)(2,1)}, u32[]{:S(2)}, u32[]{:S(2)}) async-start(bf16[8,128,256]{2,1,0:T(8,128)(2,1)} %bitcast.124), calls=%async_computation.3 | async-start | bytes 1048576 | tf_op jit(solution)/shard_map/all_to_all | solution.py:862
  187.8 2.0 collective-permute-start.21
  189.8 1.0 collective-permute-start.20
  191.6 1.2 fusion
  193.5 1.1 collective-permute-start.19
  194.6 6.1 %grads_qkv.1 = (bf16[2,2,128,768]{3,2,1,0:T(8,128)(2,1)}, bf16[2,2,128,768]{3,2,1,0:T(8,128)(2,1)}) custom-call(s32[2]{0:T(128)S(1)} %copy-done.3, bf16[1024,1024]{1,0:T(8,128)(2,1)} %get-tuple-element.151.refs_0_, bf16[1024,768]{1,0:T(8,128)(2,1)} %get-tuple-element.153.refs_1_), custom_call_target="tpu_custom_call" | custom-call | flops 5750000128 | bytes 18450000 | tf_op jit(solution)/shard_map/grads_qkv/pallas_call | solution.py:122
  200.7 11.2 %collective-permute-done.21 = bf16[2,2,704,128]{3,2,1,0:T(8,128)(2,1)S(1)} collective-permute-done((bf16[2,2,704,128]{3,2,1,0:T(8,128)(2,1)}, bf16[2,2,704,128]{3,2,1,0:T(8,128)(2,1)S(1)}, u32[]{:S(2)}, u32[]{:S(2)}) %collective-permute-start.21) | collective-permute-done | bytes 720928 | tf_op jit(solution)/shard_map/ppermute | solution.py:747
  212.8 1.4 convert_add_fusion.1
  215.3 5.1 %grads_out.1 = (bf16[2,2,256,128]{3,2,1,0:T(8,128)(2,1)}, bf16[2,2,256,128]{3,2,1,0:T(8,128)(2,1)}) custom-call(s32[2]{0:T(128)S(1)} %copy-done.3, f32[1024,256]{1,0:T(8,128)} %get-tuple-element.156.refs_0_.refs_4_, bf16[1024,256]{1,0:T(8,128)(2,1)} %slice_bitcast_fusion.5.refs_1_.refs_5_, bf16[1024,256]{1,0:T(8,128)(2,1)} %copy-done.33, ...), custom_call_target="tpu_custom_call" | custom-call | flops 4600000000 | bytes 14760000 | tf_op jit(solution)/shard_map/grads_out/pallas_call | solution.py:122
  220.8 1.8 collective-permute-start.33
  222.9 1.7 collective-permute-start.22
  226.1 6.1 %collective-permute-done.33 = bf16[2,704,128]{2,1,0:T(8,128)(2,1)S(1)} collective-permute-done((bf16[2,704,128]{2,1,0:T(8,128)(2,1)S(1)}, bf16[2,704,128]{2,1,0:T(8,128)(2,1)S(1)}, u32[]{:S(2)}, u32[]{:S(2)}) %collective-permute-start.33) | collective-permute-done | bytes 360480 | tf_op jit(solution)/shard_map/ppermute | solution.py:747
  232.3 2.7 collective-permute-start.34
  235.8 6.0 %pack_grads.1 = bf16[8,136,512]{2,1,0:T(8,128)(2,1)} custom-call(s32[2]{0:T(128)S(1)} %copy-done.3, s32[1,1024]{1,0:T(1,128)} %convert_bitcast_fusion.refs_0_, f32[1024,256]{1,0:T(8,128)} %get-tuple-element.145.refs_1_, bf16[1032,256]{1,0:T(8,128)(2,1)} %slice_bitcast_fusion.4.refs_2_, bf16[1032,256]{1,0:T(8,128)(2,1)} %copy-done.24, ...), custom_call_target="tpu_custom_call" | custom-call | flops 4600000000 | bytes 14760000 | tf_op jit(solution)/shard_map/pack_grads/pallas_call | solution.py:122
  242.6 5.1 %all-to-all-start.4 = ((bf16[8,136,512]{2,1,0:T(8,128)(2,1)}), bf16[8,136,512]{2,1,0:T(8,128)(2,1)S(1)}, u32[]{:S(2)}, u32[]{:S(2)}) async-start(bf16[8,136,512]{2,1,0:T(8,128)(2,1)} %pack_grads.1), calls=%async_computation.4 | async-start | bytes 2228224 | tf_op jit(solution)/shard_map/all_to_all | solution.py:862
  247.8 3.2 restore_rows.1
  251.0 2.1 collective-permute-start.26
  253.1 2.4 collective-permute-start.30
  255.7 13.6 %collective-permute-done.26 = bf16[2,256,128]{2,1,0:T(8,128)(2,1)S(1)} collective-permute-done((bf16[2,256,128]{2,1,0:T(8,128)(2,1)S(1)}, bf16[2,256,128]{2,1,0:T(8,128)(2,1)S(1)}, u32[]{:S(2)}, u32[]{:S(2)}) %collective-permute-start.26) | collective-permute-done | bytes 131104 | tf_op jit(solution)/shard_map/ppermute | solution.py:747
  269.4 5.4 %collective-permute-start.27 = (bf16[256,128]{1,0:T(8,128)(2,1)S(1)}, bf16[256,128]{1,0:T(8,128)(2,1)S(1)}, u32[]{:S(2)}, u32[]{:S(2)}) collective-permute-start(bf16[256,128]{1,0:T(8,128)(2,1)S(1)} %fusion.25), channel_id=1, source_target_pairs={{0,16},{4,20},{8,24},{12,28},{16,0},{20,4},{24,8},{28,12},{1,17},{... | collective-permute-start | bytes 196616 | tf_op jit(solution)/shard_map/ppermute | solution.py:747
  274.9 8.8 %collective-permute-done.30 = bf16[704,128]{1,0:T(8,128)(2,1)S(1)} collective-permute-done((bf16[704,128]{1,0:T(8,128)(2,1)S(1)}, bf16[704,128]{1,0:T(8,128)(2,1)S(1)}, u32[]{:S(2)}, u32[]{:S(2)}) %collective-permute-start.30) | collective-permute-done | bytes 180256 | tf_op jit(solution)/shard_map/ppermute | solution.py:747
  285.2 1.3 convert_add_fusion
  287.0 1.7 collective-permute-done.31
  288.9 2.5 collective-permute-start.32
  292.1 6.7 %collective-permute-done.32 = bf16[704,128]{1,0:T(8,128)(2,1)S(1)} collective-permute-done((bf16[704,128]{1,0:T(8,128)(2,1)S(1)}, bf16[704,128]{1,0:T(8,128)(2,1)S(1)}, u32[]{:S(2)}, u32[]{:S(2)}) %collective-permute-start.32) | collective-permute-done | bytes 180256 | tf_op jit(solution)/shard_map/ppermute | solution.py:747
  298.9 6.1 %collective-permute-done.23 = bf16[2,128,768]{2,1,0:T(8,128)(2,1)S(1)} collective-permute-done((bf16[2,128,768]{2,1,0:T(8,128)(2,1)S(1)}, bf16[2,128,768]{2,1,0:T(8,128)(2,1)S(1)}, u32[]{:S(2)}, u32[]{:S(2)}) %collective-permute-start.23) | collective-permute-done | bytes 393248 | tf_op jit(solution)/shard_map/ppermute | solution.py:747
  306.1 8.3 %collective-permute-done.24 = bf16[128,768]{1,0:T(8,128)(2,1)S(1)} collective-permute-done((bf16[128,768]{1,0:T(8,128)(2,1)S(1)}, bf16[128,768]{1,0:T(8,128)(2,1)S(1)}, u32[]{:S(2)}, u32[]{:S(2)}) %collective-permute-start.24) | collective-permute-done | bytes 196640 | tf_op jit(solution)/shard_map/ppermute | solution.py:747
  315.2 1.0 copy-done.4
  316.1 4.3 %unpack_grads.1 = (bf16[1024,256]{1,0:T(8,128)(2,1)}, bf16[1024,256]{1,0:T(8,128)(2,1)}, f32[8,256]{1,0:T(8,128)}) custom-call(s32[2]{0:T(128)S(1)} %copy-done.3, s32[8,1024]{1,0:T(8,128)} %get-tuple-element.101.refs_0_, bf16[8,136,512]{2,1,0:T(8,128)(2,1)} %copy-done.4), custom_call_target="tpu_custom_call" | custom-call | flops 4600000000 | bytes 14760000 | tf_op jit(solution)/shard_map/unpack_grads/pallas_call | solution.py:122
  (155 shorter events, 23.9 us)
Async XLA Ops:
  0.7 83.7 %copy-start = (s32[2]{0:T(128)}, s32[2]{0:T(128)S(1)}, u32[]{:S(2)}) copy-start(s32[2]{0:T(128)S(1)} %pad_add_fusion.ids_ref) | copy-start | bytes 28
  0.7 11.0 %copy-start.17 = (bf16[1024,256]{1,0:T(8,128)(2,1)S(1)}, bf16[1024,256]{1,0:T(8,128)(2,1)}, u32[]{:S(2)}) copy-start(bf16[1024,256]{1,0:T(8,128)(2,1)} %param.18) | copy-start | bytes 1572868
  0.7 12.6 %copy-start.20 = (s32[1024]{0:T(1024)S(1)}, s32[1024]{0:T(1024)}, u32[]{:S(2)}) copy-start(s32[1024]{0:T(1024)} %param.16) | copy-start | bytes 12292
  4.4 22.5 %all-to-all-start = ((bf16[8,136,256]{2,1,0:T(8,128)(2,1)}), bf16[8,136,256]{2,1,0:T(8,128)(2,1)S(1)}, u32[]{:S(2)}, u32[]{:S(2)}) async-start(bf16[8,136,256]{2,1,0:T(8,128)(2,1)} %get-tuple-element.100), calls=%async_computation | async-start | bytes 1114112 | tf_op jit(solution)/shard_map/all_to_all | solution.py:862
  11.7 13.5 %collective-permute-start = (bf16[1024,256]{1,0:T(8,128)(2,1)S(1)}, bf16[1024,256]{1,0:T(8,128)(2,1)S(1)}, u32[]{:S(2)}, u32[]{:S(2)}) collective-permute-start(bf16[1024,256]{1,0:T(8,128)(2,1)S(1)} %copy-done.17), channel_id=1, source_target_pairs={{0,2},{1,3},{2,0},{3,1},{4,6},{5,7},{6,4},{7,5},{8,10},{9,11},{10,... | collective-permute-start | bytes 1572872 | tf_op jit(solution)/shard_map/ppermute | solution.py:751
  13.9 3.7 %copy-start.19 = (s32[1024]{0:T(1024)}, s32[1024]{0:T(1024)S(1)}, u32[]{:S(2)}) copy-start(s32[1024]{0:T(1024)S(1)} %convert_reduce_fusion) | copy-start | bytes 12292
  26.9 15.3 %copy-start.14 = (bf16[8,136,256]{2,1,0:T(8,128)(2,1)}, bf16[8,136,256]{2,1,0:T(8,128)(2,1)S(1)}, u32[]{:S(2)}) copy-start(bf16[8,136,256]{2,1,0:T(8,128)(2,1)S(1)} %all-to-all-done.refs_1_) | copy-start | bytes 1671172
  27.0 8.1 %copy-start.22 = (bf16[1024]{0:T(1024)(128)(2,1)S(1)}, bf16[1024]{0:T(1024)(128)(2,1)}, u32[]{:S(2)}) copy-start(bf16[1024]{0:T(1024)(128)(2,1)} %param.19) | copy-start | bytes 6148
  27.0 2.2 collective-permute-start.6
  27.1 15.1 %collective-permute-start.1 = (bf16[8,136,256]{2,1,0:T(8,128)(2,1)S(1)}, bf16[8,136,256]{2,1,0:T(8,128)(2,1)}, u32[]{:S(2)}, u32[]{:S(2)}) collective-permute-start(bf16[8,136,256]{2,1,0:T(8,128)(2,1)S(1)} %all-to-all-done.refs_1_), channel_id=1, source_target_pairs={{0,2},{1,3},{2,0},{3,1},{4,6},{5,7},{6,4},{7,5},{8,10},{9,11},{10,... | collective-permute-start | bytes 1671176 | tf_op jit(solution)/shard_map/ppermute | solution.py:751
  29.2 20.2 %all-to-all-start.1 = ((bf16[8,128,256]{2,1,0:T(8,128)(2,1)}), bf16[8,128,256]{2,1,0:T(8,128)(2,1)S(1)}, u32[]{:S(2)}, u32[]{:S(2)}) async-start(bf16[8,128,256]{2,1,0:T(8,128)(2,1)} %bitcast.125), calls=%async_computation.1 | async-start | bytes 1048576 | tf_op jit(solution)/shard_map/all_to_all | solution.py:862
  42.2 5.5 %collective-permute-start.2 = (bf16[8,136,256]{2,1,0:T(8,128)(2,1)}, bf16[8,136,256]{2,1,0:T(8,128)(2,1)S(1)}, u32[]{:S(2)}, u32[]{:S(2)}) collective-permute-start(bf16[8,136,256]{2,1,0:T(8,128)(2,1)} %collective-permute-done.1.refs_3_), channel_id=1, source_target_pairs={{0,1},{1,0},{2,3},{3,2},{4,5},{5,4},{6,7},{7,6},{8,9},{9,8},{10,11... | collective-permute-start | bytes 1671176 | tf_op jit(solution)/shard_map/ppermute | solution.py:751
  43.9 3.9 %copy-start.29 = (bf16[256,1024]{1,0:T(8,128)(2,1)S(1)}, bf16[256,1024]{1,0:T(8,128)(2,1)}, u32[]{:S(2)}) copy-start(bf16[256,1024]{1,0:T(8,128)(2,1)} %refs_9_) | copy-start | bytes 1572868
  47.8 1.6 copy-start.28
  47.8 23.2 %collective-permute-start.4 = (bf16[256,1024]{1,0:T(8,128)(2,1)S(1)}, bf16[256,1024]{1,0:T(8,128)(2,1)}, u32[]{:S(2)}, u32[]{:S(2)}) collective-permute-start(bf16[256,1024]{1,0:T(8,128)(2,1)S(1)} %copy-done.29), channel_id=1, source_target_pairs={{0,2},{1,3},{2,0},{3,1},{4,6},{5,7},{6,4},{7,5},{8,10},{9,11},{10,... | collective-permute-start | bytes 1572872 | tf_op jit(solution)/shard_map/ppermute | solution.py:751
  49.4 4.2 %copy-start.16 = (bf16[8,128,256]{2,1,0:T(8,128)(2,1)}, bf16[8,128,256]{2,1,0:T(8,128)(2,1)S(1)}, u32[]{:S(2)}) copy-start(bf16[8,128,256]{2,1,0:T(8,128)(2,1)S(1)} %all-to-all-done.1.refs_5_) | copy-start | bytes 1572868
  49.4 35.0 %all-to-all-start.2 = ((bf16[8,128,512]{2,1,0:T(8,128)(2,1)}), bf16[8,128,512]{2,1,0:T(8,128)(2,1)S(1)}, u32[]{:S(2)}, u32[]{:S(2)}) async-start(bf16[8,128,512]{2,1,0:T(8,128)(2,1)} %bitcast.122), calls=%async_computation.2 | async-start | bytes 2097152 | tf_op jit(solution)/shard_map/all_to_all | solution.py:862
  53.6 30.2 %copy-start.23 = (bf16[1024]{0:T(1024)(128)(2,1)S(1)}, bf16[1024]{0:T(1024)(128)(2,1)}, u32[]{:S(2)}) copy-start(bf16[1024]{0:T(1024)(128)(2,1)} %param.20) | copy-start | bytes 6148
  69.7 14.1 %collective-permute-start.8 = (bf16[1024,256]{1,0:T(8,128)(2,1)}, bf16[1024,256]{1,0:T(8,128)(2,1)S(1)}, u32[]{:S(2)}, u32[]{:S(2)}) collective-permute-start(bf16[1024,256]{1,0:T(8,128)(2,1)} %get-tuple-element.108.refs_4_.refs_3_), channel_id=1, source_target_pairs={{0,2},{1,3},{2,0},{3,1},{4,6},{5,7},{6,4},{7,5},{8,10},{9,11},{10,... | collective-permute-start | bytes 1572872 | tf_op jit(solution)/shard_map/ppermute | solution.py:751
  70.6 19.3 %collective-permute-start.3 = (bf16[256,1024]{1,0:T(8,128)(2,1)S(1)}, bf16[256,1024]{1,0:T(8,128)(2,1)}, u32[]{:S(2)}, u32[]{:S(2)}) collective-permute-start(bf16[256,1024]{1,0:T(8,128)(2,1)S(1)} %copy-done.29), channel_id=1, source_target_pairs={{0,1},{1,0},{2,3},{3,2},{4,5},{5,4},{6,7},{7,6},{8,9},{9,8},{10,11... | collective-permute-start | bytes 1572872 | tf_op jit(solution)/shard_map/ppermute | solution.py:751
  70.6 19.3 %collective-permute-start.7 = (bf16[1024,256]{1,0:T(8,128)(2,1)}, bf16[1024,256]{1,0:T(8,128)(2,1)S(1)}, u32[]{:S(2)}, u32[]{:S(2)}) collective-permute-start(bf16[1024,256]{1,0:T(8,128)(2,1)} %get-tuple-element.108.refs_4_.refs_3_), channel_id=1, source_target_pairs={{0,1},{1,0},{2,3},{3,2},{4,5},{5,4},{6,7},{7,6},{8,9},{9,8},{10,11... | collective-permute-start | bytes 1572872 | tf_op jit(solution)/shard_map/ppermute | solution.py:751
  71.1 18.8 %collective-permute-start.5 = (bf16[256,1024]{1,0:T(8,128)(2,1)}, bf16[256,1024]{1,0:T(8,128)(2,1)}, u32[]{:S(2)}, u32[]{:S(2)}) collective-permute-start(bf16[256,1024]{1,0:T(8,128)(2,1)} %collective-permute-done.4.refs_2_.refs_11_), channel_id=1, source_target_pairs={{0,1},{1,0},{2,3},{3,2},{4,5},{5,4},{6,7},{7,6},{8,9},{9,8},{10,11... | collective-permute-start | bytes 1572872 | tf_op jit(solution)/shard_map/ppermute | solution.py:751
  83.8 6.0 %copy-start.30 = (bf16[1024,256]{1,0:T(8,128)(2,1)}, bf16[1024,256]{1,0:T(8,128)(2,1)S(1)}, u32[]{:S(2)}) copy-start(bf16[1024,256]{1,0:T(8,128)(2,1)S(1)} %collective-permute-done.8.refs_6_.refs_5_) | copy-start | bytes 1572868
  83.8 6.1 %collective-permute-start.9 = (bf16[1024,256]{1,0:T(8,128)(2,1)S(1)}, bf16[1024,256]{1,0:T(8,128)(2,1)S(1)}, u32[]{:S(2)}, u32[]{:S(2)}) collective-permute-start(bf16[1024,256]{1,0:T(8,128)(2,1)S(1)} %collective-permute-done.8.refs_6_.refs_5_), channel_id=1, source_target_pairs={{0,1},{1,0},{2,3},{3,2},{4,5},{5,4},{6,7},{7,6},{8,9},{9,8},{10,11... | collective-permute-start | bytes 1572872 | tf_op jit(solution)/shard_map/ppermute | solution.py:751
  90.8 14.9 %copy-start.25 = (bf16[1024,512]{1,0:T(8,128)(2,1)S(1)}, bf16[1024,512]{1,0:T(8,128)(2,1)}, u32[]{:S(2)}) copy-start(bf16[1024,512]{1,0:T(8,128)(2,1)} %sort_rows.1.refs_1_) | copy-start | bytes 3145732
  105.2 7.0 %copy-start.1 = (s32[2]{0:T(128)S(1)}, s32[2]{0:T(128)}, u32[]{:S(2)}) copy-start(s32[2]{0:T(128)} %copy-done) | copy-start | bytes 28
  105.2 3.6 %collective-permute-start.11 = (bf16[2,1024,256]{2,1,0:T(8,128)(2,1)}, bf16[2,1024,256]{2,1,0:T(8,128)(2,1)S(1)}, u32[]{:S(2)}, u32[]{:S(2)}) collective-permute-start(bf16[2,1024,256]{2,1,0:T(8,128)(2,1)} %get-tuple-element.118), channel_id=1, source_target_pairs={{0,1},{1,0},{2,3},{3,2},{4,5},{5,4},{6,7},{7,6},{8,9},{9,8},{10,11... | collective-permute-start | bytes 3145736 | tf_op jit(solution)/shard_map/ppermute | solution.py:751
  105.8 5.4 %collective-permute-start.10 = (bf16[1024,512]{1,0:T(8,128)(2,1)S(1)}, bf16[1024,512]{1,0:T(8,128)(2,1)S(1)}, u32[]{:S(2)}, u32[]{:S(2)}) collective-permute-start(bf16[1024,512]{1,0:T(8,128)(2,1)S(1)} %copy-done.25), channel_id=1, source_target_pairs={{0,1},{1,0},{2,3},{3,2},{4,5},{5,4},{6,7},{7,6},{8,9},{9,8},{10,11... | collective-permute-start | bytes 3145736 | tf_op jit(solution)/shard_map/ppermute | solution.py:751
  110.1 28.8 %collective-permute-start.12 = (bf16[1024,256]{1,0:T(8,128)(2,1)S(1)}, bf16[1024,256]{1,0:T(8,128)(2,1)}, u32[]{:S(2)}, u32[]{:S(2)}) collective-permute-start(bf16[1024,256]{1,0:T(8,128)(2,1)S(1)} %fusion.3), channel_id=1, source_target_pairs={{0,2},{1,3},{2,0},{3,1},{4,6},{5,7},{6,4},{7,5},{8,10},{9,11},{10,... | collective-permute-start | bytes 1572872 | tf_op jit(solution)/shard_map/ppermute | solution.py:751
  118.0 20.9 %collective-permute-start.13 = (bf16[2,2,704,128]{3,2,1,0:T(8,128)(2,1)}, bf16[2,2,704,128]{3,2,1,0:T(8,128)(2,1)}, u32[]{:S(2)}, u32[]{:S(2)}) collective-permute-start(bf16[2,2,704,128]{3,2,1,0:T(8,128)(2,1)} %get-tuple-element.126), channel_id=1, source_target_pairs={{0,4},{4,0},{8,12},{12,8},{16,20},{20,16},{24,28},{28,24},{1,5},{5... | collective-permute-start | bytes 2162696 | tf_op jit(solution)/shard_map/ppermute | solution.py:747
  138.8 5.2 %copy-start.26 = (bf16[2,1024,256]{2,1,0:T(8,128)(2,1)S(1)}, bf16[2,1024,256]{2,1,0:T(8,128)(2,1)}, u32[]{:S(2)}) copy-start(bf16[2,1024,256]{2,1,0:T(8,128)(2,1)} %get-tuple-element.140) | copy-start | bytes 3145732
  138.8 5.2 %copy-start.2 = (s32[2]{0:T(128)S(1)}, s32[2]{0:T(128)}, u32[]{:S(2)}) copy-start(s32[2]{0:T(128)} %copy-done) | copy-start | bytes 28
  138.9 2.9 collective-permute-start.14
  143.0 14.0 %collective-permute-start.15 = (bf16[1024,256]{1,0:T(8,128)(2,1)S(1)}, bf16[1024,256]{1,0:T(8,128)(2,1)S(1)}, u32[]{:S(2)}, u32[]{:S(2)}) collective-permute-start(bf16[1024,256]{1,0:T(8,128)(2,1)S(1)} %fusion.2), channel_id=1, source_target_pairs={{0,2},{1,3},{2,0},{3,1},{4,6},{5,7},{6,4},{7,5},{8,10},{9,11},{10,... | collective-permute-start | bytes 1572872 | tf_op jit(solution)/shard_map/ppermute | solution.py:751
  144.0 13.0 %collective-permute-start.16 = (bf16[2,1024,256]{2,1,0:T(8,128)(2,1)S(1)}, bf16[2,1024,256]{2,1,0:T(8,128)(2,1)S(1)}, u32[]{:S(2)}, u32[]{:S(2)}) collective-permute-start(bf16[2,1024,256]{2,1,0:T(8,128)(2,1)S(1)} %copy-done.26), channel_id=1, source_target_pairs={{0,1},{1,0},{2,3},{3,2},{4,5},{5,4},{6,7},{7,6},{8,9},{9,8},{10,11... | collective-permute-start | bytes 3145736 | tf_op jit(solution)/shard_map/ppermute | solution.py:751
  144.0 13.0 %copy-start.15 = (bf16[1024,256]{1,0:T(8,128)(2,1)S(1)}, bf16[1024,256]{1,0:T(8,128)(2,1)}, u32[]{:S(2)}) copy-start(bf16[1024,256]{1,0:T(8,128)(2,1)} %get-tuple-element.138) | copy-start | bytes 1572868
  152.5 25.2 %collective-permute-start.17 = (bf16[2,2,704,128]{3,2,1,0:T(8,128)(2,1)}, bf16[2,2,704,128]{3,2,1,0:T(8,128)(2,1)S(1)}, u32[]{:S(2)}, u32[]{:S(2)}) collective-permute-start(bf16[2,2,704,128]{3,2,1,0:T(8,128)(2,1)} %get-tuple-element.147), channel_id=1, source_target_pairs={{0,4},{4,0},{8,12},{12,8},{16,20},{20,16},{24,28},{28,24},{1,5},{5... | collective-permute-start | bytes 2162696 | tf_op jit(solution)/shard_map/ppermute | solution.py:747
  158.0 21.4 %copy-start.3 = (s32[2]{0:T(128)S(1)}, s32[2]{0:T(128)}, u32[]{:S(2)}) copy-start(s32[2]{0:T(128)} %copy-done) | copy-start | bytes 28
  178.6 13.0 %collective-permute-start.18 = (bf16[2,1032,256]{2,1,0:T(8,128)(2,1)}, bf16[2,1032,256]{2,1,0:T(8,128)(2,1)S(1)}, u32[]{:S(2)}, u32[]{:S(2)}) collective-permute-start(bf16[2,1032,256]{2,1,0:T(8,128)(2,1)} %get-tuple-element.148), channel_id=1, source_target_pairs={{0,1},{1,0},{2,3},{3,2},{4,5},{5,4},{6,7},{7,6},{8,9},{9,8},{10,11... | collective-permute-start | bytes 3170312 | tf_op jit(solution)/shard_map/ppermute | solution.py:751
  183.2 59.4 %all-to-all-start.3 = ((bf16[8,128,256]{2,1,0:T(8,128)(2,1)}), bf16[8,128,256]{2,1,0:T(8,128)(2,1)}, u32[]{:S(2)}, u32[]{:S(2)}) async-start(bf16[8,128,256]{2,1,0:T(8,128)(2,1)} %bitcast.124), calls=%async_computation.3 | async-start | bytes 1048576 | tf_op jit(solution)/shard_map/all_to_all | solution.py:862
  187.8 5.0 %copy-start.21 = (f32[8,1024]{1,0:T(8,128)S(1)}, f32[8,1024]{1,0:T(8,128)}, u32[]{:S(2)}) copy-start(f32[8,1024]{1,0:T(8,128)} %get-tuple-element.150) | copy-start | bytes 98308
  187.8 24.1 %collective-permute-start.21 = (bf16[2,2,704,128]{3,2,1,0:T(8,128)(2,1)}, bf16[2,2,704,128]{3,2,1,0:T(8,128)(2,1)S(1)}, u32[]{:S(2)}, u32[]{:S(2)}) collective-permute-start(bf16[2,2,704,128]{3,2,1,0:T(8,128)(2,1)} %get-tuple-element.167), channel_id=1, source_target_pairs={{0,4},{4,0},{8,12},{12,8},{16,20},{20,16},{24,28},{28,24},{1,5},{5... | collective-permute-start | bytes 2162696 | tf_op jit(solution)/shard_map/ppermute | solution.py:747
  189.8 24.6 %collective-permute-start.20 = (bf16[1024,256]{1,0:T(8,128)(2,1)}, bf16[1024,256]{1,0:T(8,128)(2,1)S(1)}, u32[]{:S(2)}, u32[]{:S(2)}) collective-permute-start(bf16[1024,256]{1,0:T(8,128)(2,1)} %fusion.1), channel_id=1, source_target_pairs={{0,2},{1,3},{2,0},{3,1},{4,6},{5,7},{6,4},{7,5},{8,10},{9,11},{10,... | collective-permute-start | bytes 1572872 | tf_op jit(solution)/shard_map/ppermute | solution.py:751
  193.5 41.6 %collective-permute-start.19 = (bf16[1032,256]{1,0:T(8,128)(2,1)S(1)}, bf16[1032,256]{1,0:T(8,128)(2,1)S(1)}, u32[]{:S(2)}, u32[]{:S(2)}) collective-permute-start(bf16[1032,256]{1,0:T(8,128)(2,1)S(1)} %pad_maximum_fusion.1), channel_id=1, source_target_pairs={{0,2},{1,3},{2,0},{3,1},{4,6},{5,7},{6,4},{7,5},{8,10},{9,11},{10,... | collective-permute-start | bytes 1585160 | tf_op jit(solution)/shard_map/ppermute | solution.py:751
  194.6 18.2 %copy-start.8 = (bf16[2,2,704,128]{3,2,1,0:T(8,128)(2,1)S(1)}, bf16[2,2,704,128]{3,2,1,0:T(8,128)(2,1)}, u32[]{:S(2)}) copy-start(bf16[2,2,704,128]{3,2,1,0:T(8,128)(2,1)} %get-tuple-element.121) | copy-start | bytes 2162692
  212.8 1.5 copy-start.13
  220.3 22.1 %collective-permute-start.25 = (bf16[2,2,256,128]{3,2,1,0:T(8,128)(2,1)}, bf16[2,2,256,128]{3,2,1,0:T(8,128)(2,1)S(1)}, u32[]{:S(2)}, u32[]{:S(2)}) collective-permute-start(bf16[2,2,256,128]{3,2,1,0:T(8,128)(2,1)} %get-tuple-element.172), channel_id=1, source_target_pairs={{0,4},{4,0},{8,12},{12,8},{16,20},{20,16},{24,28},{28,24},{1,5},{5... | collective-permute-start | bytes 786440 | tf_op jit(solution)/shard_map/ppermute | solution.py:747
  220.8 11.4 %collective-permute-start.33 = (bf16[2,704,128]{2,1,0:T(8,128)(2,1)S(1)}, bf16[2,704,128]{2,1,0:T(8,128)(2,1)S(1)}, u32[]{:S(2)}, u32[]{:S(2)}) collective-permute-start(bf16[2,704,128]{2,1,0:T(8,128)(2,1)S(1)} %fusion.12), channel_id=1, source_target_pairs={{0,8},{4,12},{8,0},{12,4},{16,24},{20,28},{24,16},{28,20},{1,9},{5... | collective-permute-start | bytes 1081352 | tf_op jit(solution)/shard_map/ppermute | solution.py:747
  222.6 19.8 %collective-permute-start.29 = (bf16[2,704,128]{2,1,0:T(8,128)(2,1)S(1)}, bf16[2,704,128]{2,1,0:T(8,128)(2,1)S(1)}, u32[]{:S(2)}, u32[]{:S(2)}) collective-permute-start(bf16[2,704,128]{2,1,0:T(8,128)(2,1)S(1)} %fusion.10), channel_id=1, source_target_pairs={{0,8},{4,12},{8,0},{12,4},{16,24},{20,28},{24,16},{28,20},{1,9},{5... | collective-permute-start | bytes 1081352 | tf_op jit(solution)/shard_map/ppermute | solution.py:747
  222.9 62.3 %collective-permute-start.22 = (bf16[2,2,128,768]{3,2,1,0:T(8,128)(2,1)}, bf16[2,2,128,768]{3,2,1,0:T(8,128)(2,1)}, u32[]{:S(2)}, u32[]{:S(2)}) collective-permute-start(bf16[2,2,128,768]{3,2,1,0:T(8,128)(2,1)} %get-tuple-element.168), channel_id=1, source_target_pairs={{0,4},{4,0},{8,12},{12,8},{16,20},{20,16},{24,28},{28,24},{1,5},{5... | collective-permute-start | bytes 2359304 | tf_op jit(solution)/shard_map/ppermute | solution.py:747
  232.3 42.7 %collective-permute-start.34 = (bf16[704,128]{1,0:T(8,128)(2,1)S(1)}, bf16[704,128]{1,0:T(8,128)(2,1)S(1)}, u32[]{:S(2)}, u32[]{:S(2)}) collective-permute-start(bf16[704,128]{1,0:T(8,128)(2,1)S(1)} %fusion.22), channel_id=1, source_target_pairs={{0,16},{4,20},{8,24},{12,28},{16,0},{20,4},{24,8},{28,12},{1,17},{... | collective-permute-start | bytes 540680 | tf_op jit(solution)/shard_map/ppermute | solution.py:747
  235.8 6.7 %copy-start.18 = (bf16[2,2,256,128]{3,2,1,0:T(8,128)(2,1)S(1)}, bf16[2,2,256,128]{3,2,1,0:T(8,128)(2,1)}, u32[]{:S(2)}) copy-start(bf16[2,2,256,128]{3,2,1,0:T(8,128)(2,1)} %get-tuple-element.158) | copy-start | bytes 786436
  242.6 72.5 %all-to-all-start.4 = ((bf16[8,136,512]{2,1,0:T(8,128)(2,1)}), bf16[8,136,512]{2,1,0:T(8,128)(2,1)S(1)}, u32[]{:S(2)}, u32[]{:S(2)}) async-start(bf16[8,136,512]{2,1,0:T(8,128)(2,1)} %pack_grads.1), calls=%async_computation.4 | async-start | bytes 2228224 | tf_op jit(solution)/shard_map/all_to_all | solution.py:862
  247.8 7.8 %copy-start.7 = (bf16[2,2,704,128]{3,2,1,0:T(8,128)(2,1)S(1)}, bf16[2,2,704,128]{3,2,1,0:T(8,128)(2,1)}, u32[]{:S(2)}) copy-start(bf16[2,2,704,128]{3,2,1,0:T(8,128)(2,1)} %get-tuple-element.179) | copy-start | bytes 2162692
  247.8 7.8 %copy-start.10 = (bf16[2,2,704,128]{3,2,1,0:T(8,128)(2,1)S(1)}, bf16[2,2,704,128]{3,2,1,0:T(8,128)(2,1)}, u32[]{:S(2)}) copy-start(bf16[2,2,704,128]{3,2,1,0:T(8,128)(2,1)} %copy-done.9) | copy-start | bytes 2162692
  251.0 18.3 %collective-permute-start.26 = (bf16[2,256,128]{2,1,0:T(8,128)(2,1)S(1)}, bf16[2,256,128]{2,1,0:T(8,128)(2,1)S(1)}, u32[]{:S(2)}, u32[]{:S(2)}) collective-permute-start(bf16[2,256,128]{2,1,0:T(8,128)(2,1)S(1)} %fusion.23), channel_id=1, source_target_pairs={{0,8},{4,12},{8,0},{12,4},{16,24},{20,28},{24,16},{28,20},{1,9},{5... | collective-permute-start | bytes 393224 | tf_op jit(solution)/shard_map/ppermute | solution.py:747
  253.1 30.6 %collective-permute-start.30 = (bf16[704,128]{1,0:T(8,128)(2,1)S(1)}, bf16[704,128]{1,0:T(8,128)(2,1)S(1)}, u32[]{:S(2)}, u32[]{:S(2)}) collective-permute-start(bf16[704,128]{1,0:T(8,128)(2,1)S(1)} %fusion.20), channel_id=1, source_target_pairs={{0,16},{4,20},{8,24},{12,28},{16,0},{20,4},{24,8},{28,12},{1,17},{... | collective-permute-start | bytes 540680 | tf_op jit(solution)/shard_map/ppermute | solution.py:747
  255.7 29.5 %copy-start.6 = (bf16[2,2,128,768]{3,2,1,0:T(8,128)(2,1)S(1)}, bf16[2,2,128,768]{3,2,1,0:T(8,128)(2,1)}, u32[]{:S(2)}) copy-start(bf16[2,2,128,768]{3,2,1,0:T(8,128)(2,1)} %get-tuple-element.154) | copy-start | bytes 2359300
  269.4 15.1 %collective-permute-start.27 = (bf16[256,128]{1,0:T(8,128)(2,1)S(1)}, bf16[256,128]{1,0:T(8,128)(2,1)S(1)}, u32[]{:S(2)}, u32[]{:S(2)}) collective-permute-start(bf16[256,128]{1,0:T(8,128)(2,1)S(1)} %fusion.25), channel_id=1, source_target_pairs={{0,16},{4,20},{8,24},{12,28},{16,0},{20,4},{24,8},{28,12},{1,17},{... | collective-permute-start | bytes 196616 | tf_op jit(solution)/shard_map/ppermute | solution.py:747
  274.8 13.9 %collective-permute-start.31 = (bf16[2,704,128]{2,1,0:T(8,128)(2,1)S(1)}, bf16[2,704,128]{2,1,0:T(8,128)(2,1)S(1)}, u32[]{:S(2)}, u32[]{:S(2)}) collective-permute-start(bf16[2,704,128]{2,1,0:T(8,128)(2,1)S(1)} %fusion.11), channel_id=1, source_target_pairs={{0,8},{4,12},{8,0},{12,4},{16,24},{20,28},{24,16},{28,20},{1,9},{5... | collective-permute-start | bytes 1081352 | tf_op jit(solution)/shard_map/ppermute | solution.py:747
  284.5 7.6 %collective-permute-start.28 = (f32[256,128]{1,0:T(8,128)S(1)}, f32[256,128]{1,0:T(8,128)S(1)}, u32[]{:S(2)}, u32[]{:S(2)}) collective-permute-start(f32[256,128]{1,0:T(8,128)S(1)} %fusion.24), channel_id=1, source_target_pairs={{0,0},{1,9},{2,18},{3,27},{4,4},{5,13},{6,22},{7,31},{8,1},{9,8},{... | collective-permute-start | bytes 393224 | tf_op jit(solution)/shard_map/ppermute | solution.py:989
  286.5 18.4 %collective-permute-start.23 = (bf16[2,128,768]{2,1,0:T(8,128)(2,1)S(1)}, bf16[2,128,768]{2,1,0:T(8,128)(2,1)S(1)}, u32[]{:S(2)}, u32[]{:S(2)}) collective-permute-start(bf16[2,128,768]{2,1,0:T(8,128)(2,1)S(1)} %fusion.8), channel_id=1, source_target_pairs={{0,8},{4,12},{8,0},{12,4},{16,24},{20,28},{24,16},{28,20},{1,9},{5... | collective-permute-start | bytes 1179656 | tf_op jit(solution)/shard_map/ppermute | solution.py:747
  288.9 10.0 %collective-permute-start.32 = (bf16[704,128]{1,0:T(8,128)(2,1)S(1)}, bf16[704,128]{1,0:T(8,128)(2,1)S(1)}, u32[]{:S(2)}, u32[]{:S(2)}) collective-permute-start(bf16[704,128]{1,0:T(8,128)(2,1)S(1)} %fusion.21), channel_id=1, source_target_pairs={{0,16},{4,20},{8,24},{12,28},{16,0},{20,4},{24,8},{28,12},{1,17},{... | collective-permute-start | bytes 540680 | tf_op jit(solution)/shard_map/ppermute | solution.py:747
  305.0 9.3 %collective-permute-start.24 = (bf16[128,768]{1,0:T(8,128)(2,1)S(1)}, bf16[128,768]{1,0:T(8,128)(2,1)S(1)}, u32[]{:S(2)}, u32[]{:S(2)}) collective-permute-start(bf16[128,768]{1,0:T(8,128)(2,1)S(1)} %fusion.19), channel_id=1, source_target_pairs={{0,16},{4,20},{8,24},{12,28},{16,0},{20,4},{24,8},{28,12},{1,17},{... | collective-permute-start | bytes 589832 | tf_op jit(solution)/shard_map/ppermute | solution.py:747
  (11 other events, 10.4 us)
